TPU v7x, 32 devices: a whole 2x2x4 slice. The times are simulated.
32 devices in a mesh: seq: 8 (over z, x), head: 4 (over y, core).
Axes of the slice: x: 2, y: 2, z: 4, core: 2. Of those that a mesh axis runs over, the one named last changes fastest.
Arguments:
- tokens: bfloat16 [2048, 2048], P('seq'), may hold values from -6 to 6
- input_gain: float32 [2048], replicated, may hold values from 0.1 to 1.9
- w_query: bfloat16 [2048, 4096], P(None, 'head'), may hold values from -0.125 to 0.125
- w_key: bfloat16 [2048, 512], P(None, 'head'), may hold values from -0.125 to 0.125
- w_value: bfloat16 [2048, 512], P(None, 'head'), may hold values from -0.125 to 0.125
- query_gain: float32 [128], replicated, may hold values from 1 to 8
- key_gain: float32 [128], replicated, may hold values from 1 to 8
- w_out: bfloat16 [4096, 2048], P('head'), may hold values from -0.09375 to 0.09375
- post_gain: float32 [2048], replicated, may hold values from 0.1 to 1.9
- expert_ids: int32 [2048, 8], P(('seq', 'head')), may hold values from 0 to 31, all different within a row; in each aligned block of 64 rows (0 to 63, 64 to 127, ...) at most 24 rows name the same one
- route_weights: float32 [2048, 8], P(('seq', 'head')), may hold values from 0.05 to 1
- w_gate: bfloat16 [32, 2048, 768], P(('seq', 'head')), may hold values from -0.125 to 0.125
- w_up: bfloat16 [32, 2048, 768], P(('seq', 'head')), may hold values from -0.125 to 0.125
- w_down: bfloat16 [32, 768, 2048], P(('seq', 'head')), may hold values from -0.21875 to 0.21875
Outputs:
- layer_out: bfloat16 [2048, 2048], P(('seq', 'head'))
Inputs may be any that keep to these rules, and one draw needn't show every extreme that they name: `expert_ids`: the 8 experts of a token differ. In the rows of one device (64 tokens, aligned blocks), no expert is named more than 24 times.
All inputs are finite; a program needn't handle non-finite values.
Results may differ from a plain program's by a relative error of at most 0.012.
The roundings to bfloat16 on the way count: a program that leaves them out, or rounds other values in their place, can miss the bound.
Values may be sent and summed in bfloat16 or wider, within the bound.
No kernel may reach another device: no remote copies, remote signals or barrier semaphores. Data moves between devices by JAX's collectives and lax.ppermute only.
A program may use at most 128 MiB of HBM per device.

v0:
```python
import functools

import jax
import jax.numpy as jnp
from jax import lax
from jax.experimental import pallas as pl
from jax.experimental.pallas import tpu as pltpu
from jax.sharding import PartitionSpec as P


EPSILON = 1e-06
THETA = 1000000.0
NEGATIVE = -1e30
LOG2E = 1.4426950408889634
BOTH = ("seq", "head")
VMEM = pl.BlockSpec(memory_space=pltpu.VMEM)


def rms_scale(vectors, gain_vector):
    mean_sq = jnp.mean(vectors * vectors, axis=-1, keepdims=True)
    return vectors * lax.rsqrt(mean_sq + EPSILON) * gain_vector


def turn(vectors, cos_ref, sin_ref):
    half = vectors.shape[-1] // 2
    return vectors * cos_ref[...] + pltpu.roll(vectors, half, 1) * sin_ref[...]


def first_kernel(x_ref, gain_ref, wk_ref, wv_ref, kgain_ref, cos_ref, sin_ref, normed_ref, kv_ref):
    head_dim = wk_ref.shape[1]
    normed = rms_scale(x_ref[...].astype(jnp.float32), gain_ref[...]).astype(jnp.bfloat16)
    normed_ref[...] = normed
    keys = jnp.dot(normed, wk_ref[...], preferred_element_type=jnp.float32)
    keys = turn(rms_scale(keys, kgain_ref[...]), cos_ref, sin_ref)
    kv_ref[:, :head_dim] = keys.astype(jnp.bfloat16)
    values = jnp.dot(normed, wv_ref[...], preferred_element_type=jnp.float32)
    kv_ref[:, head_dim:] = values.astype(jnp.bfloat16)


def query_kernel(head_dim, normed_ref, wq_ref, qgain_ref, cos_ref, sin_ref, q_ref):
    wide = jnp.dot(normed_ref[...], wq_ref[...], preferred_element_type=jnp.float32)
    for i in range(wide.shape[1] // head_dim):
        part = slice(i * head_dim, (i + 1) * head_dim)
        q_ref[:, part] = turn(rms_scale(wide[:, part], qgain_ref[...]), cos_ref, sin_ref).astype(
            jnp.bfloat16
        )


def attend_kernel(head_dim, blocks, first, last, bias_ref, q_ref, *rest):
    kv_refs, rest = rest[:blocks], rest[blocks:]
    s_ref = rest[-1]
    rows = q_ref.shape[0]
    queries = q_ref[...]
    scale = head_dim ** (-0.5) * LOG2E
    tops = []
    for j, kv in enumerate(kv_refs):
        raw = lax.dot_general(
            queries,
            kv[:, :head_dim],
            (((1,), (1,)), ((), ())),
            preferred_element_type=jnp.float32,
        )
        if first and j == 0:
            row = lax.broadcasted_iota(jnp.int32, raw.shape, 0)
            col = lax.broadcasted_iota(jnp.int32, raw.shape, 1)
            raw = jnp.where(col <= row, raw, NEGATIVE)
        s_ref[:, j * rows : (j + 1) * rows] = raw
        top = raw[:, :head_dim]
        for i in range(1, rows // head_dim):
            top = jnp.maximum(top, raw[:, i * head_dim : (i + 1) * head_dim])
        tops.append(top + bias_ref[j])
    if first:
        total = jnp.zeros((rows, 1), jnp.float32)
        mixed = jnp.zeros((rows, head_dim), jnp.float32)
    else:
        stat_in, mixed_in = rest[0], rest[1]
        rest = rest[2:]
        old_max, old_total = stat_in[:, 0:1], stat_in[:, 1:2]
        tops.append(jnp.broadcast_to(old_max, tops[0].shape))
    row_max = jnp.max(functools.reduce(jnp.maximum, tops), axis=1, keepdims=True)
    if not first:
        shrink = jnp.exp2((old_max - row_max) * scale)
        total = old_total * shrink
        mixed = mixed_in[...] * shrink
    sums = jnp.zeros((rows, head_dim), jnp.float32)
    for j, kv in enumerate(kv_refs):
        floor = row_max - bias_ref[j]
        weights = jnp.exp2((s_ref[:, j * rows : (j + 1) * rows] - floor) * scale)
        for i in range(rows // head_dim):
            sums = sums + weights[:, i * head_dim : (i + 1) * head_dim]
        mixed = mixed + jnp.dot(
            weights.astype(jnp.bfloat16), kv[:, head_dim:], preferred_element_type=jnp.float32
        )
    total = total + jnp.sum(sums, axis=1, keepdims=True)
    if last:
        rest[0][...] = (mixed / total).astype(jnp.bfloat16)
    else:
        lane = lax.broadcasted_iota(jnp.int32, (rows, head_dim), 1)
        rest[0][...] = jnp.where(lane == 0, row_max, total)
        rest[1][...] = mixed


def attend(rot_q, head_dim, kv_blocks, bias, state, last):
    rows, wide = rot_q.shape
    blocks = len(kv_blocks)
    column = pl.BlockSpec((rows, head_dim), lambda i: (0, i))
    if last:
        out_shape, out_specs = jax.ShapeDtypeStruct((rows, wide), jnp.bfloat16), column
    else:
        out_shape = (jax.ShapeDtypeStruct((rows, wide), jnp.float32),) * 2
        out_specs = (column, column)
    return pl.pallas_call(
        functools.partial(attend_kernel, head_dim, blocks, not state, last),
        grid=(wide // head_dim,),
        out_shape=out_shape,
        in_specs=[pl.BlockSpec(memory_space=pltpu.SMEM), column]
        + [pl.BlockSpec((rows, 2 * head_dim), lambda i: (0, 0))] * blocks
        + [column] * len(state),
        out_specs=out_specs,
        scratch_shapes=[pltpu.VMEM((rows, blocks * rows), jnp.float32)],
        name="attend",
    )(jnp.stack(bias), rot_q, *kv_blocks, *state)


def expert_kernel(count, up_steps, *refs):
    rows_refs, (wg_ref, wu_ref, wd_ref), out_refs = refs[:count], refs[count : count + 3], refs[count + 3 : -1]
    hidden_ref = refs[-1]
    step = pl.program_id(1)
    rows = rows_refs[0].shape[0]

    for now in range(up_steps):

        @pl.when(step == now)
        def _():
            part = wg_ref.shape[1]
            for i, ref in enumerate(rows_refs):
                gate = jnp.dot(ref[...], wg_ref[...], preferred_element_type=jnp.float32)
                up = jnp.dot(ref[...], wu_ref[...], preferred_element_type=jnp.float32)
                hidden = (gate / (1.0 + jnp.exp(-gate))) * up
                hidden_ref[i * rows : (i + 1) * rows, now * part : (now + 1) * part] = hidden.astype(
                    jnp.bfloat16
                )

    @pl.when(step >= up_steps)
    def _():
        for i, ref in enumerate(out_refs):
            ref[...] = jnp.dot(
                hidden_ref[i * rows : (i + 1) * rows, :],
                wd_ref[...],
                preferred_element_type=jnp.float32,
            ).astype(jnp.bfloat16)


def run_experts(arrived, w_gate, w_up, w_down):
    count = len(arrived)
    experts, rows, width = arrived[0].shape
    ff = w_gate.shape[2]
    part = ff // 3 if ff % 384 == 0 else ff
    out_part = width // 4 if width % 512 == 0 else width
    up_steps, down_steps = ff // part, width // out_part
    return pl.pallas_call(
        functools.partial(expert_kernel, count, up_steps),
        grid=(experts, up_steps + down_steps),
        out_shape=[jax.ShapeDtypeStruct((experts, rows, width), jnp.bfloat16)] * count,
        in_specs=[pl.BlockSpec((None, rows, width), lambda e, i: (e, 0, 0))] * count
        + [pl.BlockSpec((None, width, part), lambda e, i: (e, 0, jnp.minimum(i, up_steps - 1)))] * 2
        + [pl.BlockSpec((None, ff, out_part), lambda e, i: (e, 0, jnp.maximum(i - up_steps, 0)))],
        out_specs=[
            pl.BlockSpec((None, rows, out_part), lambda e, i: (e, 0, jnp.maximum(i - up_steps, 0)))
        ]
        * count,
        scratch_shapes=[pltpu.VMEM((count * rows, ff), jnp.bfloat16)],
        name="experts",
    )(*arrived, w_gate, w_up, w_down)


def pairs(seq_count, head_count, step):
    made = []
    for s in range(seq_count):
        for h in range(head_count):
            to = step(s, h)
            if to is not None:
                made.append((s * head_count + h, to[0] * head_count + to[1]))
    return made


def split_exact(values):
    high = values.astype(jnp.bfloat16)
    low = (values - high.astype(jnp.float32)).astype(jnp.bfloat16)
    return high, low


def body(
    tokens,
    input_gain,
    w_query,
    w_key,
    w_value,
    query_gain,
    key_gain,
    w_out,
    post_gain,
    expert_ids,
    route_weights,
    w_gate,
    w_up,
    w_down,
):
    tok_rows, width = tokens.shape
    head_dim = query_gain.shape[0]
    heads_here = w_query.shape[1] // head_dim
    seq_count = lax.axis_size("seq")
    seq_index = lax.axis_index("seq")
    head_count = lax.axis_size("head")
    head_index = lax.axis_index("head")
    side = 2 if seq_count % 2 == 0 else 1
    line = seq_count // side
    cores = 2 if head_count % 2 == 0 else 1
    towers = head_count // cores
    line_index, side_index = seq_index // side, seq_index % side
    tower_index, core_index = head_index // cores, head_index % cores
    make_pairs = functools.partial(pairs, seq_count, head_count)

    half_dim = head_dim // 2
    offset = seq_index * tok_rows
    positions = (offset + jnp.arange(tok_rows, dtype=jnp.int32)).astype(jnp.float32)
    frequency = THETA ** (-jnp.arange(half_dim, dtype=jnp.float32) * 2.0 / head_dim)
    angles = positions[:, None] * frequency[None, :]
    cosine, sine = jnp.cos(angles), jnp.sin(angles)
    cos_table = jnp.concatenate([cosine, cosine], axis=1)
    sin_table = jnp.concatenate([-sine, sine], axis=1)

    normed, own_kv = pl.pallas_call(
        first_kernel,
        out_shape=(
            jax.ShapeDtypeStruct((tok_rows, width), jnp.bfloat16),
            jax.ShapeDtypeStruct((tok_rows, 2 * head_dim), jnp.bfloat16),
        ),
        in_specs=[VMEM] * 7,
        out_specs=(VMEM, VMEM),
        name="norm_kv",
    )(tokens, input_gain[None], w_key, w_value, key_gain[None], cos_table, sin_table)

    kv_blocks, kv_bias = [own_kv], [jnp.float32(0.0)]
    for k in range(1, line):
        up = make_pairs(
            lambda s, h, k=k: (s + k * side, h) if s + k * side < seq_count else None
        )
        kv_blocks.append(lax.ppermute(own_kv, BOTH, up))
        kv_bias.append(jnp.where(line_index >= k, 0.0, NEGATIVE))
    if side == 2:
        swap = make_pairs(lambda s, h: (s ^ 1, h))
        for k in range(line):
            kv_blocks.append(lax.ppermute(kv_blocks[k], BOTH, swap))
            seen = line_index >= k if k else side_index == 1
            kv_bias.append(jnp.where(seen, 0.0, NEGATIVE))

    rows_here = tok_rows // head_count
    top_count = expert_ids.shape[1]
    halves = 2 if line % 2 == 0 else 1
    local_count = w_gate.shape[0]
    experts_all = local_count * seq_count * head_count
    experts_half = experts_all // halves
    members = seq_count * head_count // halves
    capacity = max(2, 3 * rows_here * top_count // (2 * experts_all))
    slots = experts_half * capacity
    first_expert = (seq_index // (seq_count // halves)) * experts_half
    mirror = make_pairs(lambda s, h: ((line - 1 - s // side) * side + s % side, h))
    mixing = route_weights / jnp.sum(route_weights, axis=1, keepdims=True)
    routes = [(expert_ids, mixing)]
    if halves == 2:
        sent = jnp.concatenate([expert_ids.astype(jnp.float32), mixing], axis=1)
        seen = lax.ppermute(sent, BOTH, mirror)
        routes.append((seen[:, :top_count].astype(jnp.int32), seen[:, top_count:]))

    def slot_tables(ids, weights):
        here = first_expert + jnp.arange(experts_half, dtype=jnp.int32)
        named = ids[:, :, None] == here[None, None, :]
        counts = jnp.sum(named, axis=1).astype(jnp.bfloat16)
        earlier = (
            jnp.arange(rows_here)[:, None] > jnp.arange(rows_here)[None, :]
        ).astype(jnp.bfloat16)
        rank_table = jnp.dot(earlier, counts, preferred_element_type=jnp.float32)
        mix_table = jnp.sum(jnp.where(named, weights[:, :, None], 0.0), axis=1)
        place = jnp.where(counts > 0, rank_table, -1.0).astype(jnp.int32)
        in_slot = place[:, :, None] == jnp.arange(capacity, dtype=jnp.int32)[None, None, :]
        pick = in_slot.astype(jnp.bfloat16).reshape(rows_here, slots)
        mix = jnp.where(in_slot, mix_table[:, :, None], 0.0).reshape(rows_here, slots)
        return pick, jnp.concatenate(split_exact(mix), axis=0)

    tables = [slot_tables(*route) for route in routes]
    query_step = 2 * head_dim if heads_here % 2 == 0 else head_dim
    rot_q = pl.pallas_call(
        functools.partial(query_kernel, head_dim),
        grid=(w_query.shape[1] // query_step,),
        out_shape=jax.ShapeDtypeStruct((tok_rows, w_query.shape[1]), jnp.bfloat16),
        in_specs=[
            pl.BlockSpec((tok_rows, width), lambda i: (0, 0)),
            pl.BlockSpec((width, query_step), lambda i: (0, i)),
            pl.BlockSpec((1, head_dim), lambda i: (0, 0)),
            pl.BlockSpec((tok_rows, head_dim), lambda i: (0, 0)),
            pl.BlockSpec((tok_rows, head_dim), lambda i: (0, 0)),
        ],
        out_specs=pl.BlockSpec((tok_rows, query_step), lambda i: (0, i)),
        name="queries",
    )(normed, w_query, query_gain[None], cos_table, sin_table)

    if side == 2:
        state = attend(rot_q, head_dim, kv_blocks[:line], kv_bias[:line], (), False)
        attended = attend(rot_q, head_dim, kv_blocks[line:], kv_bias[line:], state, True)
    else:
        attended = attend(rot_q, head_dim, kv_blocks, kv_bias, (), True)

    by_tower = attended.reshape(towers, cores * rows_here, attended.shape[1])
    core_swap = make_pairs(lambda s, h: (s, h ^ 1))

    def tower_sum(k):
        rows = lax.dynamic_index_in_dim(
            by_tower, (tower_index + k) % towers, 0, keepdims=False
        )
        part = jnp.dot(rows, w_out, preferred_element_type=jnp.float32).reshape(
            cores, rows_here, width
        )
        if cores == 1:
            return part[0]
        keep = lax.dynamic_index_in_dim(part, core_index, 0, keepdims=False)
        give = lax.dynamic_index_in_dim(part, 1 - core_index, 0, keepdims=False)
        came = lax.ppermute(give.astype(jnp.bfloat16), BOTH, core_swap)
        return keep + came.astype(jnp.float32)

    attn_part = None
    for k in range(1, towers):
        shift = make_pairs(lambda s, h, k=k: (s, (h + k * cores) % head_count))
        came = lax.ppermute(tower_sum(k).astype(jnp.bfloat16), BOTH, shift)
        came = came.astype(jnp.float32)
        attn_part = came if attn_part is None else attn_part + came
    own_sum = tower_sum(0)
    attn_part = own_sum if attn_part is None else own_sum + attn_part

    own_rows = lax.dynamic_slice_in_dim(tokens, head_index * rows_here, rows_here, 0)
    residual = own_rows.astype(jnp.float32) + attn_part
    routed = rms_scale(residual, post_gain).astype(jnp.bfloat16)

    groups = [list(range(g * members, (g + 1) * members)) for g in range(halves)]

    def exchange(rows):
        return lax.all_to_all(
            rows.reshape(members, local_count * capacity, width),
            BOTH,
            split_axis=0,
            concat_axis=0,
            axis_index_groups=groups,
            tiled=True,
        )

    def dispatch(rows, pick):
        outgoing = lax.dot_general(
            pick, rows, (((0,), (0,)), ((), ())), preferred_element_type=jnp.float32
        ).astype(jnp.bfloat16)
        return (
            exchange(outgoing)
            .reshape(members, local_count, capacity, width)
            .transpose(1, 0, 2, 3)
            .reshape(local_count, members * capacity, width)
        )

    def give_back(result, mix):
        came = exchange(
            result.reshape(local_count, members, capacity, width).transpose(1, 0, 2, 3)
        ).reshape(slots, width)
        both = jnp.dot(mix, came, preferred_element_type=jnp.float32)
        return both[:rows_here] + both[rows_here:]

    weights = (w_gate, w_up, w_down)
    if halves == 2:
        mirrored = lax.ppermute(routed, BOTH, mirror)
        own_rows_in = dispatch(routed, tables[0][0])
        far_rows_in = dispatch(mirrored, tables[1][0])
        own_result = run_experts([own_rows_in], *weights)[0]
        far_result = run_experts([far_rows_in], *weights)[0]
        foreign = give_back(far_result, tables[1][1]).astype(jnp.bfloat16)
        far_sum = lax.ppermute(foreign, BOTH, mirror)
        expert_sum = give_back(own_result, tables[0][1])
        expert_sum = expert_sum + far_sum.astype(jnp.float32)
    else:
        result = run_experts([dispatch(routed, tables[0][0])], *weights)[0]
        expert_sum = give_back(result, tables[0][1])
    return (residual + expert_sum).astype(jnp.bfloat16)


def solution(mesh):
    placed = (
        P("seq", None),
        P(),
        P(None, "head"),
        P(None, "head"),
        P(None, "head"),
        P(),
        P(),
        P("head", None),
        P(),
        P(("seq", "head"), None),
        P(("seq", "head"), None),
        P(("seq", "head"), None, None),
        P(("seq", "head"), None, None),
        P(("seq", "head"), None, None),
    )

    return jax.shard_map(
        body, mesh=mesh, in_specs=placed, out_specs=P(("seq", "head"), None), check_vma=False
    )
```

profile of v0, /device:TPU:0, one launch (start us, length us, event | category | flops | bytes accessed | tf_op | source)
XLA Modules:
  0.0 197.9 jit_solution(13575783244454205658)
XLA Ops:
  0.0 0.5 fusion.33
  0.6 0.8 pad_maximum_fusion
  1.4 3.2 %norm_kv.1 = (bf16[256,2048]{1,0:T(8,128)(2,1)}, bf16[256,256]{1,0:T(8,128)(2,1)}) custom-call(bf16[256,2048]{1,0:T(8,128)(2,1)} %x_ref.1, f32[1,2048]{1,0:T(1,128)} %bitcast.92, bf16[2048,128]{1,0:T(8,128)(2,1)} %wk_ref.1, bf16[2048,128]{1,0:T(8,128)(2,1)} %wv_ref.1, f32[1,128]{1,0:T(1,128)} %bitcast.94, f32[256,128]{1,0:T(8,128)} %get-tuple-element.32.cos_ref, ...), custom_call_target="tpu_custom_call" | custom-call | tf_op jit(solution)/shard_map/norm_kv/pallas_call | solution.py:233
  4.6 5.0 %collective-permute-start.1 = (bf16[256,256]{1,0:T(8,128)(2,1)}, bf16[256,256]{1,0:T(8,128)(2,1)S(1)}, u32[]{:S(2)}, u32[]{:S(2)}) collective-permute-start(bf16[256,256]{1,0:T(8,128)(2,1)} %get-tuple-element.10.rest_0_), channel_id=1, source_target_pairs={{0,8},{1,9},{2,10},{3,11},{4,12},{5,13},{6,14},{7,15},{8,16},{9,17... | collective-permute-start | bytes 393224 | tf_op jit(solution)/shard_map/ppermute | solution.py:249
  9.6 4.5 %collective-permute-start.3 = (bf16[256,256]{1,0:T(8,128)(2,1)}, bf16[256,256]{1,0:T(8,128)(2,1)S(1)}, u32[]{:S(2)}, u32[]{:S(2)}) collective-permute-start(bf16[256,256]{1,0:T(8,128)(2,1)} %get-tuple-element.10.rest_0_), channel_id=1, source_target_pairs={{0,16},{1,17},{2,18},{3,19},{4,20},{5,21},{6,22},{7,23},{8,24},{9,... | collective-permute-start | bytes 393224 | tf_op jit(solution)/shard_map/ppermute | solution.py:249
  14.1 1.3 collective-permute-start.5
  15.4 1.6 collective-permute-start
  17.0 0.1 collective-permute-start.10
  17.1 0.6 maximum_maximum_fusion.1.bias_ref
  17.7 0.5 collective-permute-start.2
  18.3 0.0 collective-permute-done.3.rest_2_
  18.3 1.5 collective-permute-start.4
  19.8 0.0 collective-permute-done.5.rest_3_
  19.8 1.5 collective-permute-start.6
  21.3 0.7 maximum_maximum_fusion.bias_ref
  22.0 0.1 eq.81
  22.1 5.5 %queries.1.q_ref = bf16[256,1024]{1,0:T(8,128)(2,1)} custom-call(bf16[256,2048]{1,0:T(8,128)(2,1)} %get-tuple-element.9.normed_ref, bf16[2048,1024]{1,0:T(8,128)(2,1)} %wq_ref.1, f32[1,128]{1,0:T(1,128)} %bitcast.93, f32[256,128]{1,0:T(8,128)} %get-tuple-element.32.cos_ref, f32[256,128]{1,0:T(8,128)} %get-tuple-element.33.sin_ref), custom_call_target="tpu_custom_call" | custom-call | tf_op jit(solution)/shard_map/queries/pallas_call | solution.py:293
  27.6 8.0 %attend.2 = (f32[256,1024]{1,0:T(8,128)}, f32[256,1024]{1,0:T(8,128)}) custom-call(f32[4]{0:T(128)} %maximum_maximum_fusion.1.bias_ref, bf16[256,1024]{1,0:T(8,128)(2,1)} %queries.1.q_ref, bf16[256,256]{1,0:T(8,128)(2,1)} %get-tuple-element.10.rest_0_, bf16[256,256]{1,0:T(8,128)(2,1)} %copy-done.10, bf16[256,256]{1,0:T(8,128)(2,1)} %copy-done.11, ...), custom_call_target="tpu_custom_call" | custom-call | tf_op jit(solution)/shard_map/attend/pallas_call | solution.py:112
  35.7 0.6 copy-done.6
  36.2 0.0 copy-done.7
  36.3 0.1 copy-done.8
  36.3 0.0 copy-done.9
  36.4 10.6 %attend.3 = bf16[256,1024]{1,0:T(8,128)(2,1)} custom-call(f32[4]{0:T(128)} %maximum_maximum_fusion.bias_ref, bf16[256,1024]{1,0:T(8,128)(2,1)} %queries.1.q_ref, bf16[256,256]{1,0:T(8,128)(2,1)} %copy-done.6, bf16[256,256]{1,0:T(8,128)(2,1)} %copy-done.7, bf16[256,256]{1,0:T(8,128)(2,1)} %copy-done.8, bf16[256,256]{1,0:T(8,128)(2,1)} %copy-done.9, ...), custom_call_target="tpu_custom_call" | custom-call | tf_op jit(solution)/shard_map/attend/pallas_call | solution.py:112
  46.9 1.1 constant_dynamic-slice_fusion.1
  48.0 3.1 %fusion = f32[2,64,2048]{2,1,0:T(8,128)S(1)} fusion(bf16[2,64,1024]{2,1,0:T(8,128)(2,1)S(1)} %bitcast.91, bf16[1024,2048]{1,0:T(8,128)(2,1)} %param.21), kind=kOutput, calls=%fused_computation | convolution fusion | flops 536870912 | bytes 5505024 | tf_op jit(solution)/shard_map/dot_general | solution.py:321
  51.1 0.1 collective-permute-start.8
  51.2 0.2 copy-done
  51.5 0.7 fusion.2
  52.2 0.3 collective-permute-start.7
  52.6 0.2 collective-permute-done.8
  52.8 1.6 collective-permute-start.9
  54.4 0.1 fusion.31
  54.5 6.7 %collective-permute-done.9 = bf16[64,2048]{1,0:T(8,128)(2,1)S(1)} collective-permute-done((bf16[64,2048]{1,0:T(8,128)(2,1)S(1)}, bf16[64,2048]{1,0:T(8,128)(2,1)S(1)}, u32[]{:S(2)}, u32[]{:S(2)}) %collective-permute-start.9) | collective-permute-done | bytes 262176 | tf_op jit(solution)/shard_map/ppermute | solution.py:334
  61.2 1.2 multiply_reduce_fusion
  62.4 0.8 copy-done.4
  63.2 0.1 multiply_convert_fusion
  63.3 6.4 %collective-permute-start.11 = (bf16[64,2048]{1,0:T(8,128)(2,1)S(1)}, bf16[64,2048]{1,0:T(8,128)(2,1)S(1)}, u32[]{:S(2)}, u32[]{:S(2)}) collective-permute-start(bf16[64,2048]{1,0:T(8,128)(2,1)S(1)} %multiply_convert_fusion), channel_id=1, source_target_pairs={{0,24},{1,25},{2,26},{3,27},{4,28},{5,29},{6,30},{7,31},{8,16},{9,... | collective-permute-start | bytes 786440 | tf_op jit(solution)/shard_map/ppermute | solution.py:376
  69.8 0.1 fusion.4
  69.9 0.1 fusion.5
  70.0 0.1 bitcast_compare_fusion
  70.2 5.4 %collective-permute-done.11 = bf16[64,2048]{1,0:T(8,128)(2,1)S(1)} collective-permute-done((bf16[64,2048]{1,0:T(8,128)(2,1)S(1)}, bf16[64,2048]{1,0:T(8,128)(2,1)S(1)}, u32[]{:S(2)}, u32[]{:S(2)}) %collective-permute-start.11) | collective-permute-done | bytes 262176 | tf_op jit(solution)/shard_map/ppermute | solution.py:376
  75.6 1.7 convolution_convert_fusion
  77.4 7.8 %all-to-all-start.2 = ((bf16[16,24,2048]{2,1,0:T(8,128)(2,1)}), bf16[16,24,2048]{2,1,0:T(8,128)(2,1)S(1)}, u32[]{:S(2)}, u32[]{:S(2)}) async-start(bf16[16,24,2048]{2,1,0:T(8,128)(2,1)} %bitcast.23), calls=%async_computation.2 | async-start | bytes 3145728 | tf_op jit(solution)/shard_map/all_to_all | solution.py:347
  85.2 1.7 convolution_convert_fusion.1
  86.9 21.0 %all-to-all-done.2 = bf16[16,24,2048]{2,1,0:T(8,128)(2,1)S(1)} async-done(((bf16[16,24,2048]{2,1,0:T(8,128)(2,1)}), bf16[16,24,2048]{2,1,0:T(8,128)(2,1)S(1)}, u32[]{:S(2)}, u32[]{:S(2)}) %all-to-all-start.2) | async-done | bytes 1572896 | tf_op jit(solution)/shard_map/all_to_all | solution.py:347
  107.9 1.2 copy-done.1
  109.1 3.7 %all-to-all-start = ((bf16[16,24,2048]{2,1,0:T(8,128)(2,1)}), bf16[16,24,2048]{2,1,0:T(8,128)(2,1)S(1)}, u32[]{:S(2)}, u32[]{:S(2)}) async-start(bf16[16,24,2048]{2,1,0:T(8,128)(2,1)} %bitcast.85), calls=%async_computation | async-start | bytes 3145728 | tf_op jit(solution)/shard_map/all_to_all | solution.py:347
  112.8 10.9 %experts.3 = bf16[1,384,2048]{2,1,0:T(8,128)(2,1)} custom-call(bf16[1,384,2048]{2,1,0:T(8,128)(2,1)} %bitcast.83, bf16[1,2048,768]{2,1,0:T(8,128)(2,1)} %refs_1_.3, bf16[1,2048,768]{2,1,0:T(8,128)(2,1)} %refs_2_.3, bf16[1,768,2048]{2,1,0:T(8,128)(2,1)} %refs_3_.3), custom_call_target="tpu_custom_call" | custom-call | tf_op jit(solution)/shard_map/experts/pallas_call | solution.py:161
  123.7 11.8 %all-to-all-done = bf16[16,24,2048]{2,1,0:T(8,128)(2,1)S(1)} async-done(((bf16[16,24,2048]{2,1,0:T(8,128)(2,1)}), bf16[16,24,2048]{2,1,0:T(8,128)(2,1)S(1)}, u32[]{:S(2)}, u32[]{:S(2)}) %all-to-all-start) | async-done | bytes 1572896 | tf_op jit(solution)/shard_map/all_to_all | solution.py:347
  135.6 1.2 copy-done.2
  136.7 3.9 %all-to-all-start.3 = ((bf16[16,24,2048]{2,1,0:T(8,128)(2,1)}), bf16[16,24,2048]{2,1,0:T(8,128)(2,1)S(1)}, u32[]{:S(2)}, u32[]{:S(2)}) async-start(bf16[16,24,2048]{2,1,0:T(8,128)(2,1)} %bitcast.86), calls=%async_computation.3 | async-start | bytes 3145728 | tf_op jit(solution)/shard_map/all_to_all | solution.py:347
  140.6 10.9 %experts.2 = bf16[1,384,2048]{2,1,0:T(8,128)(2,1)} custom-call(bf16[1,384,2048]{2,1,0:T(8,128)(2,1)} %bitcast.84, bf16[1,2048,768]{2,1,0:T(8,128)(2,1)} %refs_1_.3, bf16[1,2048,768]{2,1,0:T(8,128)(2,1)} %refs_2_.3, bf16[1,768,2048]{2,1,0:T(8,128)(2,1)} %refs_3_.3), custom_call_target="tpu_custom_call" | custom-call | tf_op jit(solution)/shard_map/experts/pallas_call | solution.py:161
  151.5 11.7 %all-to-all-done.3 = bf16[16,24,2048]{2,1,0:T(8,128)(2,1)S(1)} async-done(((bf16[16,24,2048]{2,1,0:T(8,128)(2,1)}), bf16[16,24,2048]{2,1,0:T(8,128)(2,1)S(1)}, u32[]{:S(2)}, u32[]{:S(2)}) %all-to-all-start.3) | async-done | bytes 1572896 | tf_op jit(solution)/shard_map/all_to_all | solution.py:347
  163.2 1.2 copy-done.3
  164.4 3.7 %all-to-all-start.1 = ((bf16[16,24,2048]{2,1,0:T(8,128)(2,1)}), bf16[16,24,2048]{2,1,0:T(8,128)(2,1)S(1)}, u32[]{:S(2)}, u32[]{:S(2)}) async-start(bf16[16,24,2048]{2,1,0:T(8,128)(2,1)} %bitcast.82), calls=%async_computation.1 | async-start | bytes 3145728 | tf_op jit(solution)/shard_map/all_to_all | solution.py:347
  168.1 0.1 fusion.32
  168.2 0.1 fusion.16
  168.3 0.1 fusion.17
  168.5 2.0 fusion.25
  170.4 0.1 fusion.6
  170.5 1.6 collective-permute-start.12
  172.1 24.3 %all-to-all-done.1 = bf16[16,24,2048]{2,1,0:T(8,128)(2,1)S(1)} async-done(((bf16[16,24,2048]{2,1,0:T(8,128)(2,1)}), bf16[16,24,2048]{2,1,0:T(8,128)(2,1)S(1)}, u32[]{:S(2)}, u32[]{:S(2)}) %all-to-all-start.1) | async-done | bytes 1572896 | tf_op jit(solution)/shard_map/all_to_all | solution.py:347
  196.5 0.5 fusion.21
  197.1 0.8 fusion.9
  (44 shorter events, 0.3 us)
Async XLA Ops:
  0.6 16.4 %copy-start.14 = (f32[64,8]{0,1:T(8,128)S(1)}, f32[64,8]{0,1:T(8,128)}, u32[]{:S(2)}) copy-start(f32[64,8]{0,1:T(8,128)} %param.24) | copy-start | bytes 6148
  0.6 16.4 %copy-start.13 = (s32[64,8]{0,1:T(8,128)S(1)}, s32[64,8]{0,1:T(8,128)}, u32[]{:S(2)}) copy-start(s32[64,8]{0,1:T(8,128)} %param.23) | copy-start | bytes 6148
  4.6 13.1 %collective-permute-start.1 = (bf16[256,256]{1,0:T(8,128)(2,1)}, bf16[256,256]{1,0:T(8,128)(2,1)S(1)}, u32[]{:S(2)}, u32[]{:S(2)}) collective-permute-start(bf16[256,256]{1,0:T(8,128)(2,1)} %get-tuple-element.10.rest_0_), channel_id=1, source_target_pairs={{0,8},{1,9},{2,10},{3,11},{4,12},{5,13},{6,14},{7,15},{8,16},{9,17... | collective-permute-start | bytes 393224 | tf_op jit(solution)/shard_map/ppermute | solution.py:249
  9.6 8.7 %collective-permute-start.3 = (bf16[256,256]{1,0:T(8,128)(2,1)}, bf16[256,256]{1,0:T(8,128)(2,1)S(1)}, u32[]{:S(2)}, u32[]{:S(2)}) collective-permute-start(bf16[256,256]{1,0:T(8,128)(2,1)} %get-tuple-element.10.rest_0_), channel_id=1, source_target_pairs={{0,16},{1,17},{2,18},{3,19},{4,20},{5,21},{6,22},{7,23},{8,24},{9,... | collective-permute-start | bytes 393224 | tf_op jit(solution)/shard_map/ppermute | solution.py:249
  14.1 5.7 %collective-permute-start.5 = (bf16[256,256]{1,0:T(8,128)(2,1)}, bf16[256,256]{1,0:T(8,128)(2,1)S(1)}, u32[]{:S(2)}, u32[]{:S(2)}) collective-permute-start(bf16[256,256]{1,0:T(8,128)(2,1)} %get-tuple-element.10.rest_0_), channel_id=1, source_target_pairs={{0,24},{1,25},{2,26},{3,27},{4,28},{5,29},{6,30},{7,31}} | collective-permute-start | bytes 393224 | tf_op jit(solution)/shard_map/ppermute | solution.py:249
  15.4 20.2 %collective-permute-start = (bf16[256,256]{1,0:T(8,128)(2,1)}, bf16[256,256]{1,0:T(8,128)(2,1)S(1)}, u32[]{:S(2)}, u32[]{:S(2)}) collective-permute-start(bf16[256,256]{1,0:T(8,128)(2,1)} %get-tuple-element.10.rest_0_), channel_id=1, source_target_pairs={{0,4},{1,5},{2,6},{3,7},{4,0},{5,1},{6,2},{7,3},{8,12},{9,13},{10,... | collective-permute-start | bytes 393224 | tf_op jit(solution)/shard_map/ppermute | solution.py:254
  17.0 37.4 %collective-permute-start.10 = (f32[64,16]{0,1:T(8,128)S(1)}, f32[64,16]{0,1:T(8,128)S(1)}, u32[]{:S(2)}, u32[]{:S(2)}) collective-permute-start(f32[64,16]{0,1:T(8,128)S(1)} %pad_maximum_fusion.2), channel_id=1, source_target_pairs={{0,24},{1,25},{2,26},{3,27},{4,28},{5,29},{6,30},{7,31},{8,16},{9,... | collective-permute-start | bytes 12296 | tf_op jit(solution)/shard_map/ppermute | solution.py:273
  17.7 9.9 %copy-start.10 = (bf16[256,256]{1,0:T(8,128)(2,1)}, bf16[256,256]{1,0:T(8,128)(2,1)S(1)}, u32[]{:S(2)}) copy-start(bf16[256,256]{1,0:T(8,128)(2,1)S(1)} %collective-permute-done.1.rest_1_) | copy-start | bytes 393220
  17.7 17.9 %collective-permute-start.2 = (bf16[256,256]{1,0:T(8,128)(2,1)S(1)}, bf16[256,256]{1,0:T(8,128)(2,1)S(1)}, u32[]{:S(2)}, u32[]{:S(2)}) collective-permute-start(bf16[256,256]{1,0:T(8,128)(2,1)S(1)} %collective-permute-done.1.rest_1_), channel_id=1, source_target_pairs={{0,4},{1,5},{2,6},{3,7},{4,0},{5,1},{6,2},{7,3},{8,12},{9,13},{10,... | collective-permute-start | bytes 393224 | tf_op jit(solution)/shard_map/ppermute | solution.py:254
  18.3 9.3 %copy-start.11 = (bf16[256,256]{1,0:T(8,128)(2,1)}, bf16[256,256]{1,0:T(8,128)(2,1)S(1)}, u32[]{:S(2)}) copy-start(bf16[256,256]{1,0:T(8,128)(2,1)S(1)} %collective-permute-done.3.rest_2_) | copy-start | bytes 393220
  18.3 17.3 %collective-permute-start.4 = (bf16[256,256]{1,0:T(8,128)(2,1)S(1)}, bf16[256,256]{1,0:T(8,128)(2,1)S(1)}, u32[]{:S(2)}, u32[]{:S(2)}) collective-permute-start(bf16[256,256]{1,0:T(8,128)(2,1)S(1)} %collective-permute-done.3.rest_2_), channel_id=1, source_target_pairs={{0,4},{1,5},{2,6},{3,7},{4,0},{5,1},{6,2},{7,3},{8,12},{9,13},{10,... | collective-permute-start | bytes 393224 | tf_op jit(solution)/shard_map/ppermute | solution.py:254
  19.8 7.8 %copy-start.12 = (bf16[256,256]{1,0:T(8,128)(2,1)}, bf16[256,256]{1,0:T(8,128)(2,1)S(1)}, u32[]{:S(2)}) copy-start(bf16[256,256]{1,0:T(8,128)(2,1)S(1)} %collective-permute-done.5.rest_3_) | copy-start | bytes 393220
  19.8 15.8 %collective-permute-start.6 = (bf16[256,256]{1,0:T(8,128)(2,1)S(1)}, bf16[256,256]{1,0:T(8,128)(2,1)S(1)}, u32[]{:S(2)}, u32[]{:S(2)}) collective-permute-start(bf16[256,256]{1,0:T(8,128)(2,1)S(1)} %collective-permute-done.5.rest_3_), channel_id=1, source_target_pairs={{0,4},{1,5},{2,6},{3,7},{4,0},{5,1},{6,2},{7,3},{8,12},{9,13},{10,... | collective-permute-start | bytes 393224 | tf_op jit(solution)/shard_map/ppermute | solution.py:254
  35.6 0.7 copy-start.6
  35.6 0.7 copy-start.7
  35.6 0.7 copy-start.8
  35.6 0.7 copy-start.9
  48.0 3.5 %copy-start = (bf16[1024,2048]{1,0:T(8,128)(2,1)S(1)}, bf16[1024,2048]{1,0:T(8,128)(2,1)}, u32[]{:S(2)}) copy-start(bf16[1024,2048]{1,0:T(8,128)(2,1)} %param.21) | copy-start | bytes 12582916
  51.1 1.6 collective-permute-start.8
  52.2 11.0 %copy-start.15 = (f32[2048]{0:T(1024)S(1)}, f32[2048]{0:T(1024)}, u32[]{:S(2)}) copy-start(f32[2048]{0:T(1024)} %param.22) | copy-start | bytes 24580
  52.2 2.2 %collective-permute-start.7 = (bf16[64,2048]{1,0:T(8,128)(2,1)S(1)}, bf16[64,2048]{1,0:T(8,128)(2,1)S(1)}, u32[]{:S(2)}, u32[]{:S(2)}) collective-permute-start(bf16[64,2048]{1,0:T(8,128)(2,1)S(1)} %fusion.13), channel_id=1, source_target_pairs={{0,1},{1,0},{2,3},{3,2},{4,5},{5,4},{6,7},{7,6},{8,9},{9,8},{10,11... | collective-permute-start | bytes 786440 | tf_op jit(solution)/shard_map/ppermute | solution.py:328
  52.8 8.4 %collective-permute-start.9 = (bf16[64,2048]{1,0:T(8,128)(2,1)S(1)}, bf16[64,2048]{1,0:T(8,128)(2,1)S(1)}, u32[]{:S(2)}, u32[]{:S(2)}) collective-permute-start(bf16[64,2048]{1,0:T(8,128)(2,1)S(1)} %fusion.10), channel_id=1, source_target_pairs={{0,2},{1,3},{2,0},{3,1},{4,6},{5,7},{6,4},{7,5},{8,10},{9,11},{10,... | collective-permute-start | bytes 786440 | tf_op jit(solution)/shard_map/ppermute | solution.py:334
  62.4 0.8 copy-start.4
  63.3 12.3 %collective-permute-start.11 = (bf16[64,2048]{1,0:T(8,128)(2,1)S(1)}, bf16[64,2048]{1,0:T(8,128)(2,1)S(1)}, u32[]{:S(2)}, u32[]{:S(2)}) collective-permute-start(bf16[64,2048]{1,0:T(8,128)(2,1)S(1)} %multiply_convert_fusion), channel_id=1, source_target_pairs={{0,24},{1,25},{2,26},{3,27},{4,28},{5,29},{6,30},{7,31},{8,16},{9,... | collective-permute-start | bytes 786440 | tf_op jit(solution)/shard_map/ppermute | solution.py:376
  77.4 30.5 %all-to-all-start.2 = ((bf16[16,24,2048]{2,1,0:T(8,128)(2,1)}), bf16[16,24,2048]{2,1,0:T(8,128)(2,1)S(1)}, u32[]{:S(2)}, u32[]{:S(2)}) async-start(bf16[16,24,2048]{2,1,0:T(8,128)(2,1)} %bitcast.23), calls=%async_computation.2 | async-start | bytes 3145728 | tf_op jit(solution)/shard_map/all_to_all | solution.py:347
  107.9 1.2 copy-start.1
  109.1 26.5 %all-to-all-start = ((bf16[16,24,2048]{2,1,0:T(8,128)(2,1)}), bf16[16,24,2048]{2,1,0:T(8,128)(2,1)S(1)}, u32[]{:S(2)}, u32[]{:S(2)}) async-start(bf16[16,24,2048]{2,1,0:T(8,128)(2,1)} %bitcast.85), calls=%async_computation | async-start | bytes 3145728 | tf_op jit(solution)/shard_map/all_to_all | solution.py:347
  135.6 1.2 copy-start.2
  136.7 26.5 %all-to-all-start.3 = ((bf16[16,24,2048]{2,1,0:T(8,128)(2,1)}), bf16[16,24,2048]{2,1,0:T(8,128)(2,1)S(1)}, u32[]{:S(2)}, u32[]{:S(2)}) async-start(bf16[16,24,2048]{2,1,0:T(8,128)(2,1)} %bitcast.86), calls=%async_computation.3 | async-start | bytes 3145728 | tf_op jit(solution)/shard_map/all_to_all | solution.py:347
  163.2 1.2 copy-start.3
  164.4 32.1 %all-to-all-start.1 = ((bf16[16,24,2048]{2,1,0:T(8,128)(2,1)}), bf16[16,24,2048]{2,1,0:T(8,128)(2,1)S(1)}, u32[]{:S(2)}, u32[]{:S(2)}) async-start(bf16[16,24,2048]{2,1,0:T(8,128)(2,1)} %bitcast.82), calls=%async_computation.1 | async-start | bytes 3145728 | tf_op jit(solution)/shard_map/all_to_all | solution.py:347
  170.5 26.6 %copy-start.5 = (f32[64,2048]{1,0:T(8,128)S(1)}, f32[64,2048]{1,0:T(8,128)}, u32[]{:S(2)}) copy-start(f32[64,2048]{1,0:T(8,128)} %copy-done.4) | copy-start | bytes 1572868
  170.5 26.5 %collective-permute-start.12 = (bf16[64,2048]{1,0:T(8,128)(2,1)S(1)}, bf16[64,2048]{1,0:T(8,128)(2,1)S(1)}, u32[]{:S(2)}, u32[]{:S(2)}) collective-permute-start(bf16[64,2048]{1,0:T(8,128)(2,1)S(1)} %fusion.6), channel_id=1, source_target_pairs={{0,24},{1,25},{2,26},{3,27},{4,28},{5,29},{6,30},{7,31},{8,16},{9,... | collective-permute-start | bytes 786440 | tf_op jit(solution)/shard_map/ppermute | solution.py:382
where the time goes:
time: 199 us; the launch traced here: 198 us
  waiting for transfers between devices  81.3 us (41%)
  Pallas kernels  49.1 us (25%)
  starting transfers between devices  45 us (23%)
  matrix products  10 us (5%)
  local copies, waits for them, and re-layouts  6.56 us (3%)
  other arithmetic  5.44 us (3%)
    all_to_all x4, waiting for transfers between devices, exchange(): lax.all_to_all(rows.reshape(members, local_count * capacity, width), BOTH...  68.9 us
    pallas_call x2, Pallas kernels, run_experts(): pl.pallas_call(functools.partial(expert_kernel, count, up_steps), grid=(e...  21.8 us
    all_to_all x4, starting transfers between devices, exchange(): lax.all_to_all(rows.reshape(members, local_count * capacity, width), BOTH...  19.1 us
    pallas_call x2, Pallas kernels, attend(): pl.pallas_call(functools.partial(attend_kernel, head_dim, blocks, not sta...  18.5 us
    ppermute x3, starting transfers between devices, body(): kv_blocks.append(lax.ppermute(own_kv, BOTH, up))  10.7 us
    ppermute x1, waiting for transfers between devices, body(): came = lax.ppermute(tower_sum(k).astype(jnp.bfloat16), BOTH, shift)  6.72 us
    ppermute x1, starting transfers between devices, body(): mirrored = lax.ppermute(routed, BOTH, mirror)  6.42 us
    pallas_call x1, Pallas kernels, body(): pl.pallas_call(functools.partial(query_kernel, head_dim), grid=(w_query.s...  5.52 us
  transfers between devices with their start and end apart: 17, of which 7 were waited for; matrix products, arithmetic and copies ran while one was open for 6% of the time, Pallas kernels for 23%

commit v1 on v0

--- a/solution.py
+++ b/solution.py
@@ -26,152 +26,145 @@
     return vectors * cos_ref[...] + pltpu.roll(vectors, half, 1) * sin_ref[...]
 
 
+def room(mib):
+    return pltpu.CompilerParams(vmem_limit_bytes=mib * 2**20)
+
+
 def first_kernel(x_ref, gain_ref, wk_ref, wv_ref, kgain_ref, cos_ref, sin_ref, normed_ref, kv_ref):
-    head_dim = wk_ref.shape[1]
+    rows, head_dim = x_ref.shape[0], wk_ref.shape[1]
     normed = rms_scale(x_ref[...].astype(jnp.float32), gain_ref[...]).astype(jnp.bfloat16)
     normed_ref[...] = normed
     keys = jnp.dot(normed, wk_ref[...], preferred_element_type=jnp.float32)
     keys = turn(rms_scale(keys, kgain_ref[...]), cos_ref, sin_ref)
-    kv_ref[:, :head_dim] = keys.astype(jnp.bfloat16)
+    kv_ref[:rows, :] = keys.astype(jnp.bfloat16)
     values = jnp.dot(normed, wv_ref[...], preferred_element_type=jnp.float32)
-    kv_ref[:, head_dim:] = values.astype(jnp.bfloat16)
-
-
-def query_kernel(head_dim, normed_ref, wq_ref, qgain_ref, cos_ref, sin_ref, q_ref):
-    wide = jnp.dot(normed_ref[...], wq_ref[...], preferred_element_type=jnp.float32)
-    for i in range(wide.shape[1] // head_dim):
-        part = slice(i * head_dim, (i + 1) * head_dim)
-        q_ref[:, part] = turn(rms_scale(wide[:, part], qgain_ref[...]), cos_ref, sin_ref).astype(
-            jnp.bfloat16
-        )
+    for i in range(0, rows, head_dim):
+        kv_ref[rows + i : rows + i + head_dim, :] = values[i : i + head_dim, :].T.astype(jnp.bfloat16)
+
+
+def query_kernel(head_dim, step, normed_ref, wq_ref, qgain_ref, cos_ref, sin_ref, q_ref):
+    for start in range(0, wq_ref.shape[1], step):
+        wide = jnp.dot(
+            normed_ref[...], wq_ref[:, start : start + step], preferred_element_type=jnp.float32
+        )
+        for i in range(0, step, head_dim):
+            q_ref[:, start + i : start + i + head_dim] = turn(
+                rms_scale(wide[:, i : i + head_dim], qgain_ref[...]), cos_ref, sin_ref
+            ).astype(jnp.bfloat16)
 
 
 def attend_kernel(head_dim, blocks, first, last, bias_ref, q_ref, *rest):
     kv_refs, rest = rest[:blocks], rest[blocks:]
     s_ref = rest[-1]
-    rows = q_ref.shape[0]
-    queries = q_ref[...]
+    rows, heads = q_ref.shape[0], q_ref.shape[1] // head_dim
     scale = head_dim ** (-0.5) * LOG2E
-    tops = []
-    for j, kv in enumerate(kv_refs):
-        raw = lax.dot_general(
-            queries,
-            kv[:, :head_dim],
-            (((1,), (1,)), ((), ())),
-            preferred_element_type=jnp.float32,
-        )
-        if first and j == 0:
-            row = lax.broadcasted_iota(jnp.int32, raw.shape, 0)
-            col = lax.broadcasted_iota(jnp.int32, raw.shape, 1)
-            raw = jnp.where(col <= row, raw, NEGATIVE)
-        s_ref[:, j * rows : (j + 1) * rows] = raw
-        top = raw[:, :head_dim]
-        for i in range(1, rows // head_dim):
-            top = jnp.maximum(top, raw[:, i * head_dim : (i + 1) * head_dim])
-        tops.append(top + bias_ref[j])
-    if first:
-        total = jnp.zeros((rows, 1), jnp.float32)
-        mixed = jnp.zeros((rows, head_dim), jnp.float32)
-    else:
-        stat_in, mixed_in = rest[0], rest[1]
-        rest = rest[2:]
-        old_max, old_total = stat_in[:, 0:1], stat_in[:, 1:2]
-        tops.append(jnp.broadcast_to(old_max, tops[0].shape))
-    row_max = jnp.max(functools.reduce(jnp.maximum, tops), axis=1, keepdims=True)
-    if not first:
-        shrink = jnp.exp2((old_max - row_max) * scale)
-        total = old_total * shrink
-        mixed = mixed_in[...] * shrink
-    sums = jnp.zeros((rows, head_dim), jnp.float32)
-    for j, kv in enumerate(kv_refs):
-        floor = row_max - bias_ref[j]
-        weights = jnp.exp2((s_ref[:, j * rows : (j + 1) * rows] - floor) * scale)
-        for i in range(rows // head_dim):
-            sums = sums + weights[:, i * head_dim : (i + 1) * head_dim]
-        mixed = mixed + jnp.dot(
-            weights.astype(jnp.bfloat16), kv[:, head_dim:], preferred_element_type=jnp.float32
-        )
-    total = total + jnp.sum(sums, axis=1, keepdims=True)
-    if last:
-        rest[0][...] = (mixed / total).astype(jnp.bfloat16)
-    else:
-        lane = lax.broadcasted_iota(jnp.int32, (rows, head_dim), 1)
-        rest[0][...] = jnp.where(lane == 0, row_max, total)
-        rest[1][...] = mixed
+
+    def values(kv):
+        return jnp.concatenate(
+            [kv[rows + i : rows + i + head_dim, :] for i in range(0, rows, head_dim)], axis=1
+        )
+
+    def score(h):
+        queries = q_ref[:, h * head_dim : (h + 1) * head_dim]
+        tops = []
+        for j, kv in enumerate(kv_refs):
+            raw = lax.dot_general(
+                kv[:rows, :],
+                queries,
+                (((1,), (1,)), ((), ())),
+                preferred_element_type=jnp.float32,
+            )
+            if first and j == 0:
+                key = lax.broadcasted_iota(jnp.int32, raw.shape, 0)
+                asked = lax.broadcasted_iota(jnp.int32, raw.shape, 1)
+                raw = jnp.where(key <= asked, raw, NEGATIVE)
+            s_ref[h % 2, j * rows : (j + 1) * rows, :] = raw
+            tops.append(jnp.max(raw.reshape(rows // 8, 8, rows), axis=0) + bias_ref[j])
+        return jnp.max(functools.reduce(jnp.maximum, tops), axis=0, keepdims=True)
+
+    def mix(h, row_max):
+        if first:
+            total = jnp.zeros((1, rows), jnp.float32)
+            mixed = jnp.zeros((head_dim, rows), jnp.float32)
+        else:
+            old_max, old_total = rest[0][h, 0:1, :], rest[0][h, 1:2, :]
+            row_max = jnp.maximum(row_max, old_max)
+            shrink = jnp.exp2((old_max - row_max) * scale)
+            total = old_total * shrink
+            mixed = rest[1][h] * shrink
+        sums = jnp.zeros((8, rows), jnp.float32)
+        for j, kv in enumerate(kv_refs):
+            floor = row_max - bias_ref[j]
+            weights = jnp.exp2((s_ref[h % 2, j * rows : (j + 1) * rows, :] - floor) * scale)
+            sums = sums + jnp.sum(weights.reshape(rows // 8, 8, rows), axis=0)
+            mixed = mixed + jnp.dot(
+                values(kv), weights.astype(jnp.bfloat16), preferred_element_type=jnp.float32
+            )
+        total = total + jnp.sum(sums, axis=0, keepdims=True)
+        if last:
+            rest[-2][:, h * head_dim : (h + 1) * head_dim] = (mixed / total).T.astype(jnp.bfloat16)
+        else:
+            rest[-3][h] = jnp.concatenate([row_max, total] + [total] * 6, axis=0)
+            rest[-2][h] = mixed
+
+    ahead = score(0)
+    for h in range(heads):
+        now, ahead = ahead, score(h + 1) if h + 1 < heads else None
+        mix(h, now)
 
 
 def attend(rot_q, head_dim, kv_blocks, bias, state, last):
     rows, wide = rot_q.shape
-    blocks = len(kv_blocks)
-    column = pl.BlockSpec((rows, head_dim), lambda i: (0, i))
+    heads, blocks = wide // head_dim, len(kv_blocks)
     if last:
-        out_shape, out_specs = jax.ShapeDtypeStruct((rows, wide), jnp.bfloat16), column
+        out_shape, out_specs = jax.ShapeDtypeStruct((rows, wide), jnp.bfloat16), VMEM
     else:
-        out_shape = (jax.ShapeDtypeStruct((rows, wide), jnp.float32),) * 2
-        out_specs = (column, column)
+        out_shape = (
+            jax.ShapeDtypeStruct((heads, 8, rows), jnp.float32),
+            jax.ShapeDtypeStruct((heads, head_dim, rows), jnp.float32),
+        )
+        out_specs = (VMEM, VMEM)
     return pl.pallas_call(
         functools.partial(attend_kernel, head_dim, blocks, not state, last),
-        grid=(wide // head_dim,),
         out_shape=out_shape,
-        in_specs=[pl.BlockSpec(memory_space=pltpu.SMEM), column]
-        + [pl.BlockSpec((rows, 2 * head_dim), lambda i: (0, 0))] * blocks
-        + [column] * len(state),
+        in_specs=[pl.BlockSpec(memory_space=pltpu.SMEM)] + [VMEM] * (1 + blocks + len(state)),
         out_specs=out_specs,
-        scratch_shapes=[pltpu.VMEM((rows, blocks * rows), jnp.float32)],
+        scratch_shapes=[pltpu.VMEM((2, blocks * rows, rows), jnp.float32)],
+        compiler_params=room(max(16, 2 * blocks)),
         name="attend",
     )(jnp.stack(bias), rot_q, *kv_blocks, *state)
 
 
-def expert_kernel(count, up_steps, *refs):
-    rows_refs, (wg_ref, wu_ref, wd_ref), out_refs = refs[:count], refs[count : count + 3], refs[count + 3 : -1]
-    hidden_ref = refs[-1]
-    step = pl.program_id(1)
-    rows = rows_refs[0].shape[0]
-
-    for now in range(up_steps):
-
-        @pl.when(step == now)
-        def _():
-            part = wg_ref.shape[1]
-            for i, ref in enumerate(rows_refs):
-                gate = jnp.dot(ref[...], wg_ref[...], preferred_element_type=jnp.float32)
-                up = jnp.dot(ref[...], wu_ref[...], preferred_element_type=jnp.float32)
-                hidden = (gate / (1.0 + jnp.exp(-gate))) * up
-                hidden_ref[i * rows : (i + 1) * rows, now * part : (now + 1) * part] = hidden.astype(
-                    jnp.bfloat16
-                )
-
-    @pl.when(step >= up_steps)
-    def _():
-        for i, ref in enumerate(out_refs):
-            ref[...] = jnp.dot(
-                hidden_ref[i * rows : (i + 1) * rows, :],
-                wd_ref[...],
-                preferred_element_type=jnp.float32,
-            ).astype(jnp.bfloat16)
-
-
-def run_experts(arrived, w_gate, w_up, w_down):
-    count = len(arrived)
-    experts, rows, width = arrived[0].shape
-    ff = w_gate.shape[2]
-    part = ff // 3 if ff % 384 == 0 else ff
-    out_part = width // 4 if width % 512 == 0 else width
-    up_steps, down_steps = ff // part, width // out_part
-    return pl.pallas_call(
-        functools.partial(expert_kernel, count, up_steps),
-        grid=(experts, up_steps + down_steps),
-        out_shape=[jax.ShapeDtypeStruct((experts, rows, width), jnp.bfloat16)] * count,
-        in_specs=[pl.BlockSpec((None, rows, width), lambda e, i: (e, 0, 0))] * count
-        + [pl.BlockSpec((None, width, part), lambda e, i: (e, 0, jnp.minimum(i, up_steps - 1)))] * 2
-        + [pl.BlockSpec((None, ff, out_part), lambda e, i: (e, 0, jnp.maximum(i - up_steps, 0)))],
-        out_specs=[
-            pl.BlockSpec((None, rows, out_part), lambda e, i: (e, 0, jnp.maximum(i - up_steps, 0)))
-        ]
-        * count,
-        scratch_shapes=[pltpu.VMEM((count * rows, ff), jnp.bfloat16)],
-        name="experts",
-    )(*arrived, w_gate, w_up, w_down)
+def expert_kernel(x_ref, wg_ref, wu_ref, wd_ref, out_ref, hidden_ref):
+    ff, width = wd_ref.shape
+    part = 256 if ff % 256 == 0 else ff
+    for i in range(0, ff, part):
+        gate = jnp.dot(x_ref[...], wg_ref[:, i : i + part], preferred_element_type=jnp.float32)
+        up = jnp.dot(x_ref[...], wu_ref[:, i : i + part], preferred_element_type=jnp.float32)
+        hidden = (gate / (1.0 + jnp.exp(-gate))) * up
+        hidden_ref[:, i : i + part] = hidden.astype(jnp.bfloat16)
+    part = 512 if width % 512 == 0 else width
+    for i in range(0, width, part):
+        out_ref[:, i : i + part] = jnp.dot(
+            hidden_ref[...], wd_ref[:, i : i + part], preferred_element_type=jnp.float32
+        ).astype(jnp.bfloat16)
+
+
+def run_experts(grouped, w_gate, w_up, w_down):
+    experts, rows, width = grouped.shape
+    made = [
+        pl.pallas_call(
+            expert_kernel,
+            out_shape=jax.ShapeDtypeStruct((rows, width), jnp.bfloat16),
+            in_specs=[VMEM] * 4,
+            out_specs=VMEM,
+            scratch_shapes=[pltpu.VMEM((rows, w_gate.shape[2]), jnp.bfloat16)],
+            compiler_params=room(20),
+            name="experts",
+        )(grouped[e], w_gate[e], w_up[e], w_down[e])
+        for e in range(experts)
+    ]
+    return made[0][None] if experts == 1 else jnp.stack(made)
 
 
 def pairs(seq_count, head_count, step):
@@ -234,10 +227,11 @@
         first_kernel,
         out_shape=(
             jax.ShapeDtypeStruct((tok_rows, width), jnp.bfloat16),
-            jax.ShapeDtypeStruct((tok_rows, 2 * head_dim), jnp.bfloat16),
+            jax.ShapeDtypeStruct((2 * tok_rows, head_dim), jnp.bfloat16),
         ),
         in_specs=[VMEM] * 7,
         out_specs=(VMEM, VMEM),
+        compiler_params=room(12),
         name="norm_kv",
     )(tokens, input_gain[None], w_key, w_value, key_gain[None], cos_table, sin_table)
 
@@ -291,17 +285,11 @@
     tables = [slot_tables(*route) for route in routes]
     query_step = 2 * head_dim if heads_here % 2 == 0 else head_dim
     rot_q = pl.pallas_call(
-        functools.partial(query_kernel, head_dim),
-        grid=(w_query.shape[1] // query_step,),
+        functools.partial(query_kernel, head_dim, query_step),
         out_shape=jax.ShapeDtypeStruct((tok_rows, w_query.shape[1]), jnp.bfloat16),
-        in_specs=[
-            pl.BlockSpec((tok_rows, width), lambda i: (0, 0)),
-            pl.BlockSpec((width, query_step), lambda i: (0, i)),
-            pl.BlockSpec((1, head_dim), lambda i: (0, 0)),
-            pl.BlockSpec((tok_rows, head_dim), lambda i: (0, 0)),
-            pl.BlockSpec((tok_rows, head_dim), lambda i: (0, 0)),
-        ],
-        out_specs=pl.BlockSpec((tok_rows, query_step), lambda i: (0, i)),
+        in_specs=[VMEM] * 5,
+        out_specs=VMEM,
+        compiler_params=room(12),
         name="queries",
     )(normed, w_query, query_gain[None], cos_table, sin_table)
 
@@ -376,14 +364,14 @@
         mirrored = lax.ppermute(routed, BOTH, mirror)
         own_rows_in = dispatch(routed, tables[0][0])
         far_rows_in = dispatch(mirrored, tables[1][0])
-        own_result = run_experts([own_rows_in], *weights)[0]
-        far_result = run_experts([far_rows_in], *weights)[0]
+        own_result = run_experts(own_rows_in, *weights)
+        far_result = run_experts(far_rows_in, *weights)
         foreign = give_back(far_result, tables[1][1]).astype(jnp.bfloat16)
         far_sum = lax.ppermute(foreign, BOTH, mirror)
         expert_sum = give_back(own_result, tables[0][1])
         expert_sum = expert_sum + far_sum.astype(jnp.float32)
     else:
-        result = run_experts([dispatch(routed, tables[0][0])], *weights)[0]
+        result = run_experts(dispatch(routed, tables[0][0]), *weights)
         expert_sum = give_back(result, tables[0][1])
     return (residual + expert_sum).astype(jnp.bfloat16)
 

time: 199 us -> 180 us (0.905)
  Pallas kernels: 49.1 us -> 18.9 us
  local copies, waits for them, and re-layouts: 6.56 us -> 19.5 us
  other arithmetic: 5.44 us -> 2.73 us
  matrix products: 10 us -> 7.67 us
    pallas_call x3, Pallas kernels: 27.3 us -> 10.6 us  [the longest x2 9.05 us: run_experts(): pl.pallas_call(expert_kernel, out_shape=jax.ShapeDtypeStruct((rows, width...]
    unnamed x32 -> x44, local copies, waits for them, and re-layouts: 5.33 us -> 19.3 us
    pallas_call x2, Pallas kernels: 18.5 us -> 7.31 us  [attend(): pl.pallas_call(functools.partial(attend_kernel, head_dim, blocks, not sta...]
    dot_general x2, matrix products: 3.79 us -> 1.45 us  [tower_sum(): jnp.dot(rows, w_out, preferred_element_type=jnp.float32)]
    pallas_call x1, Pallas kernels: 3.22 us -> 1.03 us  [body(): pl.pallas_call(first_kernel, out_shape=(jax.ShapeDtypeStruct((tok_rows, w...]
  transfers between devices with their start and end apart: 17 -> 17, of which waited for: 7 -> 8; matrix products, arithmetic and copies ran while one was open for 6% -> 4% of each run, Pallas kernels for 23% -> 10%
where the time goes in v1:
time: 180 us; the launch traced here: 179 us
  waiting for transfers between devices  83 us (46%)
  starting transfers between devices  46.9 us (26%)
  local copies, waits for them, and re-layouts  19.5 us (11%)
  Pallas kernels  18.9 us (10%)
  matrix products  7.67 us (4%)
  other arithmetic  2.73 us (2%)
    all_to_all x4, waiting for transfers between devices, exchange(): lax.all_to_all(rows.reshape(members, local_count * capacity, width), BOTH...  70.4 us
    all_to_all x4, starting transfers between devices, exchange(): lax.all_to_all(rows.reshape(members, local_count * capacity, width), BOTH...  20.6 us
    unnamed x44, local copies, waits for them, and re-layouts  19.3 us
    ppermute x3, starting transfers between devices, body(): kv_blocks.append(lax.ppermute(own_kv, BOTH, up))  10.8 us
    pallas_call x2, Pallas kernels, run_experts(): pl.pallas_call(expert_kernel, out_shape=jax.ShapeDtypeStruct((rows, width...  9.05 us
    pallas_call x2, Pallas kernels, attend(): pl.pallas_call(functools.partial(attend_kernel, head_dim, blocks, not sta...  7.31 us
    ppermute x1, waiting for transfers between devices, body(): came = lax.ppermute(tower_sum(k).astype(jnp.bfloat16), BOTH, shift)  6.72 us
    ppermute x1, starting transfers between devices, body(): mirrored = lax.ppermute(routed, BOTH, mirror)  6.52 us
  transfers between devices with their start and end apart: 17, of which 8 were waited for; matrix products, arithmetic and copies ran while one was open for 4% of the time, Pallas kernels for 10%

profile of v1, /device:TPU:0, one launch (start us, length us, event | category | flops | bytes accessed | tf_op | source)
XLA Modules:
  0.0 179.3 jit_solution(15405849294834111794)
XLA Ops:
  0.0 0.5 fusion.33
  0.6 0.1 pad_maximum_fusion
  0.7 0.5 copy-done.10
  1.2 1.0 copy-done.11
  2.3 1.0 copy-done.12
  3.3 0.7 copy-done.13
  4.0 0.7 copy-done.15
  4.7 1.0 norm_kv.1
  5.7 5.0 %collective-permute-start.1 = (bf16[512,128]{1,0:T(8,128)(2,1)S(1)}, bf16[512,128]{1,0:T(8,128)(2,1)S(1)}, u32[]{:S(2)}, u32[]{:S(2)}) collective-permute-start(bf16[512,128]{1,0:T(8,128)(2,1)S(1)} %get-tuple-element.10.rest_0_), channel_id=1, source_target_pairs={{0,8},{1,9},{2,10},{3,11},{4,12},{5,13},{6,14},{7,15},{8,16},{9,17... | collective-permute-start | bytes 393224 | tf_op jit(solution)/shard_map/ppermute | solution.py:243
  10.7 4.5 %collective-permute-start.3 = (bf16[512,128]{1,0:T(8,128)(2,1)S(1)}, bf16[512,128]{1,0:T(8,128)(2,1)S(1)}, u32[]{:S(2)}, u32[]{:S(2)}) collective-permute-start(bf16[512,128]{1,0:T(8,128)(2,1)S(1)} %get-tuple-element.10.rest_0_), channel_id=1, source_target_pairs={{0,16},{1,17},{2,18},{3,19},{4,20},{5,21},{6,22},{7,23},{8,24},{9,... | collective-permute-start | bytes 393224 | tf_op jit(solution)/shard_map/ppermute | solution.py:243
  15.2 1.3 collective-permute-start.5
  16.5 1.6 collective-permute-start
  18.2 0.1 maximum_maximum_fusion.1.bias_ref
  18.3 0.6 collective-permute-start.2
  18.8 0.2 collective-permute-done.3.rest_2_
  19.0 1.5 collective-permute-start.4
  20.6 1.5 collective-permute-start.6
  22.2 0.1 eq.81
  22.3 2.2 %copy-done.9 = bf16[2048,1024]{1,0:T(8,128)(2,1)S(1)} copy-done((bf16[2048,1024]{1,0:T(8,128)(2,1)S(1)}, bf16[2048,1024]{1,0:T(8,128)(2,1)}, u32[]{:S(2)}) %copy-start.9) | copy-done | bytes 4194328
  24.5 1.5 queries.1.q_ref
  26.0 3.6 %attend.2 = (f32[8,8,256]{2,1,0:T(8,128)S(1)}, f32[8,128,256]{2,1,0:T(8,128)S(1)}) custom-call(f32[4]{0:T(128)S(1)} %maximum_maximum_fusion.1.bias_ref, bf16[256,1024]{1,0:T(8,128)(2,1)S(1)} %queries.1.q_ref, bf16[512,128]{1,0:T(8,128)(2,1)S(1)} %get-tuple-element.10.rest_0_, bf16[512,128]{1,0:T(8,128)(2,1)S(1)} %collective-permute-done.1.rest_1_, ...), custom_call_target="tpu_custom_call" | custom-call | tf_op jit(solution)/shard_map/attend/pallas_call | solution.py:127
  29.7 3.7 %attend.3 = bf16[256,1024]{1,0:T(8,128)(2,1)S(1)} custom-call(f32[4]{0:T(128)S(1)} %maximum_maximum_fusion.bias_ref, bf16[256,1024]{1,0:T(8,128)(2,1)S(1)} %queries.1.q_ref, bf16[512,128]{1,0:T(8,128)(2,1)S(1)} %collective-permute-done.rest_0_, bf16[512,128]{1,0:T(8,128)(2,1)S(1)} %collective-permute-done.2.rest_1_, ...), custom_call_target="tpu_custom_call" | custom-call | tf_op jit(solution)/shard_map/attend/pallas_call | solution.py:127
  33.5 0.7 fusion
  34.3 0.7 fusion.2
  35.1 0.6 collective-permute-start.7
  35.7 0.2 collective-permute-done.8
  35.9 1.6 collective-permute-start.9
  37.5 0.1 fusion.31
  37.6 6.7 %collective-permute-done.9 = bf16[64,2048]{1,0:T(8,128)(2,1)S(1)} collective-permute-done((bf16[64,2048]{1,0:T(8,128)(2,1)S(1)}, bf16[64,2048]{1,0:T(8,128)(2,1)S(1)}, u32[]{:S(2)}, u32[]{:S(2)}) %collective-permute-start.9) | collective-permute-done | bytes 262176 | tf_op jit(solution)/shard_map/ppermute | solution.py:322
  44.3 0.3 multiply_reduce_fusion
  44.6 0.8 copy-done.17
  45.4 0.1 multiply_convert_fusion
  45.5 6.5 %collective-permute-start.11 = (bf16[64,2048]{1,0:T(8,128)(2,1)S(1)}, bf16[64,2048]{1,0:T(8,128)(2,1)S(1)}, u32[]{:S(2)}, u32[]{:S(2)}) collective-permute-start(bf16[64,2048]{1,0:T(8,128)(2,1)S(1)} %multiply_convert_fusion), channel_id=1, source_target_pairs={{0,24},{1,25},{2,26},{3,27},{4,28},{5,29},{6,30},{7,31},{8,16},{9,... | collective-permute-start | bytes 786440 | tf_op jit(solution)/shard_map/ppermute | solution.py:364
  52.0 0.1 fusion.4
  52.2 0.1 fusion.5
  52.3 0.1 bitcast_compare_fusion
  52.5 5.4 %collective-permute-done.11 = bf16[64,2048]{1,0:T(8,128)(2,1)S(1)} collective-permute-done((bf16[64,2048]{1,0:T(8,128)(2,1)S(1)}, bf16[64,2048]{1,0:T(8,128)(2,1)S(1)}, u32[]{:S(2)}, u32[]{:S(2)}) %collective-permute-start.11) | collective-permute-done | bytes 262176 | tf_op jit(solution)/shard_map/ppermute | solution.py:364
  57.9 1.7 convolution_convert_fusion
  59.6 7.7 %all-to-all-start.2 = ((bf16[16,24,2048]{2,1,0:T(8,128)(2,1)}), bf16[16,24,2048]{2,1,0:T(8,128)(2,1)S(1)}, u32[]{:S(2)}, u32[]{:S(2)}) async-start(bf16[16,24,2048]{2,1,0:T(8,128)(2,1)} %bitcast.26), calls=%async_computation.2 | async-start | bytes 3145728 | tf_op jit(solution)/shard_map/all_to_all | solution.py:335
  67.3 1.7 convolution_convert_fusion.1
  69.1 21.0 %all-to-all-done.2 = bf16[16,24,2048]{2,1,0:T(8,128)(2,1)S(1)} async-done(((bf16[16,24,2048]{2,1,0:T(8,128)(2,1)}), bf16[16,24,2048]{2,1,0:T(8,128)(2,1)S(1)}, u32[]{:S(2)}, u32[]{:S(2)}) %all-to-all-start.2) | async-done | bytes 1572896 | tf_op jit(solution)/shard_map/all_to_all | solution.py:335
  90.0 1.1 copy-done.6
  91.2 4.8 %all-to-all-start = ((bf16[16,24,2048]{2,1,0:T(8,128)(2,1)}), bf16[16,24,2048]{2,1,0:T(8,128)(2,1)}, u32[]{:S(2)}, u32[]{:S(2)}) async-start(bf16[16,24,2048]{2,1,0:T(8,128)(2,1)} %bitcast.98), calls=%async_computation | async-start | bytes 3145728 | tf_op jit(solution)/shard_map/all_to_all | solution.py:335
  96.1 1.9 %copy-done.1 = bf16[1,2048,768]{2,1,0:T(8,128)(2,1)S(1)} copy-done((bf16[1,2048,768]{2,1,0:T(8,128)(2,1)S(1)}, bf16[1,2048,768]{2,1,0:T(8,128)(2,1)}, u32[]{:S(2)}) %copy-start.1) | copy-done | bytes 3145752
  98.0 1.9 %copy-done.3 = bf16[1,768,2048]{2,1,0:T(8,128)(2,1)S(1)} copy-done((bf16[1,768,2048]{2,1,0:T(8,128)(2,1)S(1)}, bf16[1,768,2048]{2,1,0:T(8,128)(2,1)}, u32[]{:S(2)}) %copy-start.3) | copy-done | bytes 3145752
  99.8 1.4 copy-done.7
  101.2 3.8 %experts.3 = bf16[384,2048]{1,0:T(8,128)(2,1)S(1)} custom-call(bf16[384,2048]{1,0:T(8,128)(2,1)S(1)} %bitcast.92, bf16[2048,768]{1,0:T(8,128)(2,1)S(1)} %bitcast.85, bf16[2048,768]{1,0:T(8,128)(2,1)S(1)} %bitcast.87, bf16[768,2048]{1,0:T(8,128)(2,1)S(1)} %bitcast.89), custom_call_target="tpu_custom_call" | custom-call | tf_op jit(solution)/shard_map/experts/pallas_call | solution.py:156
  105.1 1.1 copy-done.8
  106.2 12.4 %all-to-all-done = bf16[16,24,2048]{2,1,0:T(8,128)(2,1)} async-done(((bf16[16,24,2048]{2,1,0:T(8,128)(2,1)}), bf16[16,24,2048]{2,1,0:T(8,128)(2,1)}, u32[]{:S(2)}, u32[]{:S(2)}) %all-to-all-start) | async-done | bytes 1572896 | tf_op jit(solution)/shard_map/all_to_all | solution.py:335
  118.7 4.4 %all-to-all-start.3 = ((bf16[16,24,2048]{2,1,0:T(8,128)(2,1)}), bf16[16,24,2048]{2,1,0:T(8,128)(2,1)}, u32[]{:S(2)}, u32[]{:S(2)}) async-start(bf16[16,24,2048]{2,1,0:T(8,128)(2,1)} %bitcast.93), calls=%async_computation.3 | async-start | bytes 3145728 | tf_op jit(solution)/shard_map/all_to_all | solution.py:335
  123.1 1.9 %copy-done.2 = bf16[1,2048,768]{2,1,0:T(8,128)(2,1)S(1)} copy-done((bf16[1,2048,768]{2,1,0:T(8,128)(2,1)S(1)}, bf16[1,2048,768]{2,1,0:T(8,128)(2,1)}, u32[]{:S(2)}) %copy-start.2) | copy-done | bytes 3145752
  125.0 1.9 %copy-done.4 = bf16[1,768,2048]{2,1,0:T(8,128)(2,1)S(1)} copy-done((bf16[1,768,2048]{2,1,0:T(8,128)(2,1)S(1)}, bf16[1,768,2048]{2,1,0:T(8,128)(2,1)}, u32[]{:S(2)}) %copy-start.4) | copy-done | bytes 3145752
  126.9 5.2 %experts.2 = bf16[384,2048]{1,0:T(8,128)(2,1)S(1)} custom-call(bf16[384,2048]{1,0:T(8,128)(2,1)} %bitcast.18.x_ref, bf16[2048,768]{1,0:T(8,128)(2,1)S(1)} %bitcast.86, bf16[2048,768]{1,0:T(8,128)(2,1)S(1)} %bitcast.88, bf16[768,2048]{1,0:T(8,128)(2,1)S(1)} %bitcast.90), custom_call_target="tpu_custom_call" | custom-call | tf_op jit(solution)/shard_map/experts/pallas_call | solution.py:156
  132.1 1.1 copy-done.5
  133.3 12.6 %all-to-all-done.3 = bf16[16,24,2048]{2,1,0:T(8,128)(2,1)} async-done(((bf16[16,24,2048]{2,1,0:T(8,128)(2,1)}), bf16[16,24,2048]{2,1,0:T(8,128)(2,1)}, u32[]{:S(2)}, u32[]{:S(2)}) %all-to-all-start.3) | async-done | bytes 1572896 | tf_op jit(solution)/shard_map/all_to_all | solution.py:335
  145.9 3.7 %all-to-all-start.1 = ((bf16[16,24,2048]{2,1,0:T(8,128)(2,1)}), bf16[16,24,2048]{2,1,0:T(8,128)(2,1)S(1)}, u32[]{:S(2)}, u32[]{:S(2)}) async-start(bf16[16,24,2048]{2,1,0:T(8,128)(2,1)} %bitcast.91), calls=%async_computation.1 | async-start | bytes 3145728 | tf_op jit(solution)/shard_map/all_to_all | solution.py:335
  149.6 0.1 fusion.32
  149.7 0.1 fusion.16
  149.8 0.1 fusion.17
  149.9 2.0 %fusion.25 = f32[128,2048]{1,0:T(8,128)S(1)} fusion(bf16[384,2048]{1,0:T(8,128)(2,1)} %bitcast.29, bf16[64,384]{0,1:T(8,128)(2,1)S(1)} %get-tuple-element.25, bf16[64,384]{0,1:T(8,128)(2,1)S(1)} %get-tuple-element.23), kind=kOutput, calls=%fused_computation.45 | convolution fusion | flops 201523200 | bytes 2719744 | tf_op jit(solution)/shard_map/dot_general | solution.py:359
  152.0 1.6 collective-permute-start.12
  153.6 24.4 %all-to-all-done.1 = bf16[16,24,2048]{2,1,0:T(8,128)(2,1)S(1)} async-done(((bf16[16,24,2048]{2,1,0:T(8,128)(2,1)}), bf16[16,24,2048]{2,1,0:T(8,128)(2,1)S(1)}, u32[]{:S(2)}, u32[]{:S(2)}) %all-to-all-start.1) | async-done | bytes 1572896 | tf_op jit(solution)/shard_map/all_to_all | solution.py:335
  178.0 0.5 fusion.21
  178.5 0.8 fusion.9
  (56 shorter events, 0.7 us)
Async XLA Ops:
  0.0 1.2 copy-start.10
  0.6 17.5 %copy-start.20 = (f32[64,8]{0,1:T(8,128)S(1)}, f32[64,8]{0,1:T(8,128)}, u32[]{:S(2)}) copy-start(f32[64,8]{0,1:T(8,128)} %param.24) | copy-start | bytes 6148
  0.6 17.5 %copy-start.19 = (s32[64,8]{0,1:T(8,128)S(1)}, s32[64,8]{0,1:T(8,128)}, u32[]{:S(2)}) copy-start(s32[64,8]{0,1:T(8,128)} %param.23) | copy-start | bytes 6148
  0.6 21.7 %copy-start.14 = (f32[128]{0:T(128)S(1)}, f32[128]{0:T(128)}, u32[]{:S(2)}) copy-start(f32[128]{0:T(128)} %param.19) | copy-start | bytes 1540
  1.2 1.0 copy-start.11
  2.3 1.0 copy-start.12
  3.3 0.7 copy-start.13
  4.0 0.7 copy-start.15
  5.7 12.6 %collective-permute-start.1 = (bf16[512,128]{1,0:T(8,128)(2,1)S(1)}, bf16[512,128]{1,0:T(8,128)(2,1)S(1)}, u32[]{:S(2)}, u32[]{:S(2)}) collective-permute-start(bf16[512,128]{1,0:T(8,128)(2,1)S(1)} %get-tuple-element.10.rest_0_), channel_id=1, source_target_pairs={{0,8},{1,9},{2,10},{3,11},{4,12},{5,13},{6,14},{7,15},{8,16},{9,17... | collective-permute-start | bytes 393224 | tf_op jit(solution)/shard_map/ppermute | solution.py:243
  10.7 8.4 %collective-permute-start.3 = (bf16[512,128]{1,0:T(8,128)(2,1)S(1)}, bf16[512,128]{1,0:T(8,128)(2,1)S(1)}, u32[]{:S(2)}, u32[]{:S(2)}) collective-permute-start(bf16[512,128]{1,0:T(8,128)(2,1)S(1)} %get-tuple-element.10.rest_0_), channel_id=1, source_target_pairs={{0,16},{1,17},{2,18},{3,19},{4,20},{5,21},{6,22},{7,23},{8,24},{9,... | collective-permute-start | bytes 393224 | tf_op jit(solution)/shard_map/ppermute | solution.py:243
  15.2 5.4 %collective-permute-start.5 = (bf16[512,128]{1,0:T(8,128)(2,1)S(1)}, bf16[512,128]{1,0:T(8,128)(2,1)S(1)}, u32[]{:S(2)}, u32[]{:S(2)}) collective-permute-start(bf16[512,128]{1,0:T(8,128)(2,1)S(1)} %get-tuple-element.10.rest_0_), channel_id=1, source_target_pairs={{0,24},{1,25},{2,26},{3,27},{4,28},{5,29},{6,30},{7,31}} | collective-permute-start | bytes 393224 | tf_op jit(solution)/shard_map/ppermute | solution.py:243
  16.5 13.2 %collective-permute-start = (bf16[512,128]{1,0:T(8,128)(2,1)S(1)}, bf16[512,128]{1,0:T(8,128)(2,1)S(1)}, u32[]{:S(2)}, u32[]{:S(2)}) collective-permute-start(bf16[512,128]{1,0:T(8,128)(2,1)S(1)} %get-tuple-element.10.rest_0_), channel_id=1, source_target_pairs={{0,4},{1,5},{2,6},{3,7},{4,0},{5,1},{6,2},{7,3},{8,12},{9,13},{10,... | collective-permute-start | bytes 393224 | tf_op jit(solution)/shard_map/ppermute | solution.py:248
  18.1 19.4 %collective-permute-start.10 = (f32[64,16]{0,1:T(8,128)S(1)}, f32[64,16]{0,1:T(8,128)S(1)}, u32[]{:S(2)}, u32[]{:S(2)}) collective-permute-start(f32[64,16]{0,1:T(8,128)S(1)} %pad_maximum_fusion.2), channel_id=1, source_target_pairs={{0,24},{1,25},{2,26},{3,27},{4,28},{5,29},{6,30},{7,31},{8,16},{9,... | collective-permute-start | bytes 12296 | tf_op jit(solution)/shard_map/ppermute | solution.py:267
  18.3 11.4 %collective-permute-start.2 = (bf16[512,128]{1,0:T(8,128)(2,1)S(1)}, bf16[512,128]{1,0:T(8,128)(2,1)S(1)}, u32[]{:S(2)}, u32[]{:S(2)}) collective-permute-start(bf16[512,128]{1,0:T(8,128)(2,1)S(1)} %collective-permute-done.1.rest_1_), channel_id=1, source_target_pairs={{0,4},{1,5},{2,6},{3,7},{4,0},{5,1},{6,2},{7,3},{8,12},{9,13},{10,... | collective-permute-start | bytes 393224 | tf_op jit(solution)/shard_map/ppermute | solution.py:248
  19.0 10.7 %collective-permute-start.4 = (bf16[512,128]{1,0:T(8,128)(2,1)S(1)}, bf16[512,128]{1,0:T(8,128)(2,1)S(1)}, u32[]{:S(2)}, u32[]{:S(2)}) collective-permute-start(bf16[512,128]{1,0:T(8,128)(2,1)S(1)} %collective-permute-done.3.rest_2_), channel_id=1, source_target_pairs={{0,4},{1,5},{2,6},{3,7},{4,0},{5,1},{6,2},{7,3},{8,12},{9,13},{10,... | collective-permute-start | bytes 393224 | tf_op jit(solution)/shard_map/ppermute | solution.py:248
  20.6 9.2 %collective-permute-start.6 = (bf16[512,128]{1,0:T(8,128)(2,1)S(1)}, bf16[512,128]{1,0:T(8,128)(2,1)S(1)}, u32[]{:S(2)}, u32[]{:S(2)}) collective-permute-start(bf16[512,128]{1,0:T(8,128)(2,1)S(1)} %collective-permute-done.5.rest_3_), channel_id=1, source_target_pairs={{0,4},{1,5},{2,6},{3,7},{4,0},{5,1},{6,2},{7,3},{8,12},{9,13},{10,... | collective-permute-start | bytes 393224 | tf_op jit(solution)/shard_map/ppermute | solution.py:248
  22.3 2.2 %copy-start.9 = (bf16[2048,1024]{1,0:T(8,128)(2,1)S(1)}, bf16[2048,1024]{1,0:T(8,128)(2,1)}, u32[]{:S(2)}) copy-start(bf16[2048,1024]{1,0:T(8,128)(2,1)} %wq_ref.1) | copy-start | bytes 12582916
  26.0 7.4 %copy-start.16 = (bf16[1024,2048]{1,0:T(8,128)(2,1)S(1)}, bf16[1024,2048]{1,0:T(8,128)(2,1)}, u32[]{:S(2)}) copy-start(bf16[1024,2048]{1,0:T(8,128)(2,1)} %param.21) | copy-start | bytes 12582916
  34.2 1.6 collective-permute-start.8
  35.1 10.3 %copy-start.21 = (f32[2048]{0:T(1024)S(1)}, f32[2048]{0:T(1024)}, u32[]{:S(2)}) copy-start(f32[2048]{0:T(1024)} %param.22) | copy-start | bytes 24580
  35.1 2.5 %collective-permute-start.7 = (bf16[64,2048]{1,0:T(8,128)(2,1)S(1)}, bf16[64,2048]{1,0:T(8,128)(2,1)S(1)}, u32[]{:S(2)}, u32[]{:S(2)}) collective-permute-start(bf16[64,2048]{1,0:T(8,128)(2,1)S(1)} %fusion.13), channel_id=1, source_target_pairs={{0,1},{1,0},{2,3},{3,2},{4,5},{5,4},{6,7},{7,6},{8,9},{9,8},{10,11... | collective-permute-start | bytes 786440 | tf_op jit(solution)/shard_map/ppermute | solution.py:316
  35.9 8.4 %collective-permute-start.9 = (bf16[64,2048]{1,0:T(8,128)(2,1)S(1)}, bf16[64,2048]{1,0:T(8,128)(2,1)S(1)}, u32[]{:S(2)}, u32[]{:S(2)}) collective-permute-start(bf16[64,2048]{1,0:T(8,128)(2,1)S(1)} %fusion.10), channel_id=1, source_target_pairs={{0,2},{1,3},{2,0},{3,1},{4,6},{5,7},{6,4},{7,5},{8,10},{9,11},{10,... | collective-permute-start | bytes 786440 | tf_op jit(solution)/shard_map/ppermute | solution.py:322
  44.6 0.8 copy-start.17
  45.5 12.4 %collective-permute-start.11 = (bf16[64,2048]{1,0:T(8,128)(2,1)S(1)}, bf16[64,2048]{1,0:T(8,128)(2,1)S(1)}, u32[]{:S(2)}, u32[]{:S(2)}) collective-permute-start(bf16[64,2048]{1,0:T(8,128)(2,1)S(1)} %multiply_convert_fusion), channel_id=1, source_target_pairs={{0,24},{1,25},{2,26},{3,27},{4,28},{5,29},{6,30},{7,31},{8,16},{9,... | collective-permute-start | bytes 786440 | tf_op jit(solution)/shard_map/ppermute | solution.py:364
  59.6 30.4 %all-to-all-start.2 = ((bf16[16,24,2048]{2,1,0:T(8,128)(2,1)}), bf16[16,24,2048]{2,1,0:T(8,128)(2,1)S(1)}, u32[]{:S(2)}, u32[]{:S(2)}) async-start(bf16[16,24,2048]{2,1,0:T(8,128)(2,1)} %bitcast.26), calls=%async_computation.2 | async-start | bytes 3145728 | tf_op jit(solution)/shard_map/all_to_all | solution.py:335
  90.0 1.1 copy-start.6
  91.2 4.9 %copy-start = (bf16[1,2048,768]{2,1,0:T(8,128)(2,1)S(1)}, bf16[1,2048,768]{2,1,0:T(8,128)(2,1)}, u32[]{:S(2)}) copy-start(bf16[1,2048,768]{2,1,0:T(8,128)(2,1)} %param.25) | copy-start | bytes 9437188
  91.2 27.5 %all-to-all-start = ((bf16[16,24,2048]{2,1,0:T(8,128)(2,1)}), bf16[16,24,2048]{2,1,0:T(8,128)(2,1)}, u32[]{:S(2)}, u32[]{:S(2)}) async-start(bf16[16,24,2048]{2,1,0:T(8,128)(2,1)} %bitcast.98), calls=%async_computation | async-start | bytes 3145728 | tf_op jit(solution)/shard_map/all_to_all | solution.py:335
  96.1 1.9 %copy-start.1 = (bf16[1,2048,768]{2,1,0:T(8,128)(2,1)S(1)}, bf16[1,2048,768]{2,1,0:T(8,128)(2,1)}, u32[]{:S(2)}) copy-start(bf16[1,2048,768]{2,1,0:T(8,128)(2,1)} %param.26) | copy-start | bytes 9437188
  98.0 1.9 %copy-start.3 = (bf16[1,768,2048]{2,1,0:T(8,128)(2,1)S(1)}, bf16[1,768,2048]{2,1,0:T(8,128)(2,1)}, u32[]{:S(2)}) copy-start(bf16[1,768,2048]{2,1,0:T(8,128)(2,1)} %param.27) | copy-start | bytes 9437188
  99.8 1.4 copy-start.7
  105.1 1.1 copy-start.8
  118.7 27.2 %all-to-all-start.3 = ((bf16[16,24,2048]{2,1,0:T(8,128)(2,1)}), bf16[16,24,2048]{2,1,0:T(8,128)(2,1)}, u32[]{:S(2)}, u32[]{:S(2)}) async-start(bf16[16,24,2048]{2,1,0:T(8,128)(2,1)} %bitcast.93), calls=%async_computation.3 | async-start | bytes 3145728 | tf_op jit(solution)/shard_map/all_to_all | solution.py:335
  123.1 1.9 %copy-start.2 = (bf16[1,2048,768]{2,1,0:T(8,128)(2,1)S(1)}, bf16[1,2048,768]{2,1,0:T(8,128)(2,1)}, u32[]{:S(2)}) copy-start(bf16[1,2048,768]{2,1,0:T(8,128)(2,1)} %param.26) | copy-start | bytes 9437188
  125.0 1.9 %copy-start.4 = (bf16[1,768,2048]{2,1,0:T(8,128)(2,1)S(1)}, bf16[1,768,2048]{2,1,0:T(8,128)(2,1)}, u32[]{:S(2)}) copy-start(bf16[1,768,2048]{2,1,0:T(8,128)(2,1)} %param.27) | copy-start | bytes 9437188
  132.1 1.2 copy-start.5
  145.9 32.1 %all-to-all-start.1 = ((bf16[16,24,2048]{2,1,0:T(8,128)(2,1)}), bf16[16,24,2048]{2,1,0:T(8,128)(2,1)S(1)}, u32[]{:S(2)}, u32[]{:S(2)}) async-start(bf16[16,24,2048]{2,1,0:T(8,128)(2,1)} %bitcast.91), calls=%async_computation.1 | async-start | bytes 3145728 | tf_op jit(solution)/shard_map/all_to_all | solution.py:335
  152.0 26.6 %copy-start.18 = (f32[64,2048]{1,0:T(8,128)S(1)}, f32[64,2048]{1,0:T(8,128)}, u32[]{:S(2)}) copy-start(f32[64,2048]{1,0:T(8,128)} %copy-done.17) | copy-start | bytes 1572868
  152.0 26.5 %collective-permute-start.12 = (bf16[64,2048]{1,0:T(8,128)(2,1)S(1)}, bf16[64,2048]{1,0:T(8,128)(2,1)S(1)}, u32[]{:S(2)}, u32[]{:S(2)}) collective-permute-start(bf16[64,2048]{1,0:T(8,128)(2,1)S(1)} %fusion.6), channel_id=1, source_target_pairs={{0,24},{1,25},{2,26},{3,27},{4,28},{5,29},{6,30},{7,31},{8,16},{9,... | collective-permute-start | bytes 786440 | tf_op jit(solution)/shard_map/ppermute | solution.py:370

commit v2 on v1

--- a/solution.py
+++ b/solution.py
@@ -14,6 +14,7 @@
 LOG2E = 1.4426950408889634
 BOTH = ("seq", "head")
 VMEM = pl.BlockSpec(memory_space=pltpu.VMEM)
+ANY = pl.BlockSpec(memory_space=pl.ANY)
 
 
 def rms_scale(vectors, gain_vector):
@@ -30,13 +31,31 @@
     return pltpu.CompilerParams(vmem_limit_bytes=mib * 2**20)
 
 
-def first_kernel(x_ref, gain_ref, wk_ref, wv_ref, kgain_ref, cos_ref, sin_ref, normed_ref, kv_ref):
+def first_kernel(
+    x_hbm, wk_hbm, wv_hbm, gain_ref, kgain_ref, cos_ref, sin_ref, normed_ref, kv_ref, x_ref, wk_ref, wv_ref, sems
+):
     rows, head_dim = x_ref.shape[0], wk_ref.shape[1]
-    normed = rms_scale(x_ref[...].astype(jnp.float32), gain_ref[...]).astype(jnp.bfloat16)
-    normed_ref[...] = normed
+    half = rows // 2
+    copies = [
+        pltpu.make_async_copy(x_hbm.at[pl.ds(0, half)], x_ref.at[pl.ds(0, half)], sems.at[0]),
+        pltpu.make_async_copy(x_hbm.at[pl.ds(half, half)], x_ref.at[pl.ds(half, half)], sems.at[1]),
+        pltpu.make_async_copy(wk_hbm, wk_ref, sems.at[2]),
+        pltpu.make_async_copy(wv_hbm, wv_ref, sems.at[3]),
+    ]
+    for copy in copies:
+        copy.start()
+    for i in range(2):
+        copies[i].wait()
+        part = slice(i * half, (i + 1) * half)
+        normed_ref[part, :] = rms_scale(x_ref[part, :].astype(jnp.float32), gain_ref[...]).astype(
+            jnp.bfloat16
+        )
+    normed = normed_ref[...]
+    copies[2].wait()
     keys = jnp.dot(normed, wk_ref[...], preferred_element_type=jnp.float32)
     keys = turn(rms_scale(keys, kgain_ref[...]), cos_ref, sin_ref)
     kv_ref[:rows, :] = keys.astype(jnp.bfloat16)
+    copies[3].wait()
     values = jnp.dot(normed, wv_ref[...], preferred_element_type=jnp.float32)
     for i in range(0, rows, head_dim):
         kv_ref[rows + i : rows + i + head_dim, :] = values[i : i + head_dim, :].T.astype(jnp.bfloat16)
@@ -135,31 +154,59 @@
     )(jnp.stack(bias), rot_q, *kv_blocks, *state)
 
 
-def expert_kernel(x_ref, wg_ref, wu_ref, wd_ref, out_ref, hidden_ref):
-    ff, width = wd_ref.shape
-    part = 256 if ff % 256 == 0 else ff
-    for i in range(0, ff, part):
-        gate = jnp.dot(x_ref[...], wg_ref[:, i : i + part], preferred_element_type=jnp.float32)
-        up = jnp.dot(x_ref[...], wu_ref[:, i : i + part], preferred_element_type=jnp.float32)
-        hidden = (gate / (1.0 + jnp.exp(-gate))) * up
-        hidden_ref[:, i : i + part] = hidden.astype(jnp.bfloat16)
+def expert_kernel(
+    x_hbm, wg_hbm, wu_hbm, wd_hbm, out_hbm, x_ref, wg_ref, wu_ref, wd_ref, hidden_ref, out_ref, sems
+):
+    rows, width = x_hbm.shape
+    ins = [
+        pltpu.make_async_copy(hbm, ref, sems.at[i])
+        for i, (hbm, ref) in enumerate(
+            ((x_hbm, x_ref), (wg_hbm, wg_ref), (wu_hbm, wu_ref), (wd_hbm, wd_ref))
+        )
+    ]
+    for copy in ins:
+        copy.start()
+    ins[0].wait()
+    ins[1].wait()
+    gate = jnp.dot(x_ref[...], wg_ref[...], preferred_element_type=jnp.float32)
+    gate = gate / (1.0 + jnp.exp(-gate))
+    ins[2].wait()
+    up = jnp.dot(x_ref[...], wu_ref[...], preferred_element_type=jnp.float32)
+    hidden_ref[...] = (gate * up).astype(jnp.bfloat16)
+    ins[3].wait()
+    halves = 2 if rows % 32 == 0 else 1
+    half = rows // halves
     part = 512 if width % 512 == 0 else width
-    for i in range(0, width, part):
-        out_ref[:, i : i + part] = jnp.dot(
-            hidden_ref[...], wd_ref[:, i : i + part], preferred_element_type=jnp.float32
-        ).astype(jnp.bfloat16)
+    outs = []
+    for k in range(halves):
+        for i in range(0, width, part):
+            out_ref[k * half : (k + 1) * half, i : i + part] = jnp.dot(
+                hidden_ref[k * half : (k + 1) * half, :],
+                wd_ref[:, i : i + part],
+                preferred_element_type=jnp.float32,
+            ).astype(jnp.bfloat16)
+        outs.append(
+            pltpu.make_async_copy(
+                out_ref.at[pl.ds(k * half, half)], out_hbm.at[pl.ds(k * half, half)], sems.at[4 + k]
+            )
+        )
+        outs[-1].start()
+    for copy in outs:
+        copy.wait()
 
 
 def run_experts(grouped, w_gate, w_up, w_down):
     experts, rows, width = grouped.shape
+    ff = w_gate.shape[2]
+    held = ((rows, width), (width, ff), (width, ff), (ff, width), (rows, ff), (rows, width))
     made = [
         pl.pallas_call(
             expert_kernel,
             out_shape=jax.ShapeDtypeStruct((rows, width), jnp.bfloat16),
-            in_specs=[VMEM] * 4,
-            out_specs=VMEM,
-            scratch_shapes=[pltpu.VMEM((rows, w_gate.shape[2]), jnp.bfloat16)],
-            compiler_params=room(20),
+            in_specs=[ANY] * 4,
+            out_specs=ANY,
+            scratch_shapes=[pltpu.VMEM(shape, jnp.bfloat16) for shape in held]
+            + [pltpu.SemaphoreType.DMA((6,))],
             name="experts",
         )(grouped[e], w_gate[e], w_up[e], w_down[e])
         for e in range(experts)
@@ -229,11 +276,16 @@
             jax.ShapeDtypeStruct((tok_rows, width), jnp.bfloat16),
             jax.ShapeDtypeStruct((2 * tok_rows, head_dim), jnp.bfloat16),
         ),
-        in_specs=[VMEM] * 7,
+        in_specs=[ANY] * 3 + [VMEM] * 4,
         out_specs=(VMEM, VMEM),
-        compiler_params=room(12),
+        scratch_shapes=[
+            pltpu.VMEM(tokens.shape, tokens.dtype),
+            pltpu.VMEM(w_key.shape, w_key.dtype),
+            pltpu.VMEM(w_value.shape, w_value.dtype),
+            pltpu.SemaphoreType.DMA((4,)),
+        ],
         name="norm_kv",
-    )(tokens, input_gain[None], w_key, w_value, key_gain[None], cos_table, sin_table)
+    )(tokens, w_key, w_value, input_gain[None], key_gain[None], cos_table, sin_table)
 
     kv_blocks, kv_bias = [own_kv], [jnp.float32(0.0)]
     for k in range(1, line):

time: 180 us -> 182 us (1.011)
  local copies, waits for them, and re-layouts: 19.5 us -> 6.8 us
  Pallas kernels: 18.9 us -> 30 us
  waiting for transfers between devices: 83 us -> 88.2 us
    unnamed x44 -> x28, local copies, waits for them, and re-layouts: 19.3 us -> 6.6 us
    pallas_call x2, Pallas kernels: 9.05 us -> 16.6 us  [run_experts(): pl.pallas_call(expert_kernel, out_shape=jax.ShapeDtypeStruct((rows, width...]
    all_to_all x4, waiting for transfers between devices: 70.4 us -> 75.4 us  [exchange(): lax.all_to_all(rows.reshape(members, local_count * capacity, width), BOTH...]
    pallas_call x1, Pallas kernels: 1.03 us -> 4.33 us  [body(): pl.pallas_call(first_kernel, out_shape=(jax.ShapeDtypeStruct((tok_rows, w...]
  transfers between devices with their start and end apart: 17 -> 17, of which waited for: 8 -> 8; matrix products, arithmetic and copies ran while one was open for 4% -> 3% of each run, Pallas kernels for 10% -> 14%
where the time goes in v2:
time: 182 us
  waiting for transfers between devices  88.2 us (48%)
  starting transfers between devices  45.5 us (25%)
  Pallas kernels  30 us (16%)
  local copies, waits for them, and re-layouts  6.8 us (4%)
  matrix products  6.22 us (3%)
  other arithmetic  4.34 us (2%)
    all_to_all x4, waiting for transfers between devices, exchange(): lax.all_to_all(rows.reshape(members, local_count * capacity, width), BOTH...  75.4 us
    all_to_all x4, starting transfers between devices, exchange(): lax.all_to_all(rows.reshape(members, local_count * capacity, width), BOTH...  19.2 us
    pallas_call x2, Pallas kernels, run_experts(): pl.pallas_call(expert_kernel, out_shape=jax.ShapeDtypeStruct((rows, width...  16.6 us
    ppermute x3, starting transfers between devices, body(): kv_blocks.append(lax.ppermute(own_kv, BOTH, up))  10.9 us
    pallas_call x2, Pallas kernels, attend(): pl.pallas_call(functools.partial(attend_kernel, head_dim, blocks, not sta...  7.46 us
    ppermute x1, waiting for transfers between devices, body(): came = lax.ppermute(tower_sum(k).astype(jnp.bfloat16), BOTH, shift)  6.72 us
    unnamed x28, local copies, waits for them, and re-layouts  6.6 us
    ppermute x1, starting transfers between devices, body(): mirrored = lax.ppermute(routed, BOTH, mirror)  6.41 us
  transfers between devices with their start and end apart: 17, of which 8 were waited for; matrix products, arithmetic and copies ran while one was open for 3% of the time, Pallas kernels for 14%

profile of v2, /device:TPU:0, one launch (start us, length us, event | category | flops | bytes accessed | tf_op | source)
XLA Modules:
  0.0 181.6 jit_solution(11056510219359110354)
XLA Ops:
  0.0 0.5 fusion.33
  0.6 0.0 copy-start.11
  0.6 0.0 copy-start.5
  0.6 0.8 pad_maximum_fusion
  1.4 4.3 %norm_kv.1 = (bf16[256,2048]{1,0:T(8,128)(2,1)}, bf16[512,128]{1,0:T(8,128)(2,1)}) custom-call(bf16[256,2048]{1,0:T(8,128)(2,1)} %x_hbm.1, bf16[2048,128]{1,0:T(8,128)(2,1)} %wk_hbm.1, bf16[2048,128]{1,0:T(8,128)(2,1)} %wv_hbm.1, f32[1,2048]{1,0:T(1,128)} %bitcast.102, f32[1,128]{1,0:T(1,128)} %bitcast.103, f32[256,128]{1,0:T(8,128)} %get-tuple-element.32.cos_ref, ...), custom_call_target="tpu_custom_call" | custom-call | tf_op jit(solution)/shard_map/norm_kv/pallas_call | solution.py:273
  5.8 5.0 %collective-permute-start.1 = (bf16[512,128]{1,0:T(8,128)(2,1)}, bf16[512,128]{1,0:T(8,128)(2,1)S(1)}, u32[]{:S(2)}, u32[]{:S(2)}) collective-permute-start(bf16[512,128]{1,0:T(8,128)(2,1)} %get-tuple-element.10.rest_0_), channel_id=1, source_target_pairs={{0,8},{1,9},{2,10},{3,11},{4,12},{5,13},{6,14},{7,15},{8,16},{9,17... | collective-permute-start | bytes 393224 | tf_op jit(solution)/shard_map/ppermute | solution.py:295
  10.7 4.5 %collective-permute-start.3 = (bf16[512,128]{1,0:T(8,128)(2,1)}, bf16[512,128]{1,0:T(8,128)(2,1)S(1)}, u32[]{:S(2)}, u32[]{:S(2)}) collective-permute-start(bf16[512,128]{1,0:T(8,128)(2,1)} %get-tuple-element.10.rest_0_), channel_id=1, source_target_pairs={{0,16},{1,17},{2,18},{3,19},{4,20},{5,21},{6,22},{7,23},{8,24},{9,... | collective-permute-start | bytes 393224 | tf_op jit(solution)/shard_map/ppermute | solution.py:295
  15.2 1.5 collective-permute-start.5
  16.7 1.6 collective-permute-start
  18.4 0.1 collective-permute-start.10
  18.5 0.1 maximum_maximum_fusion.1.bias_ref
  18.5 0.6 collective-permute-start.2
  19.1 0.3 collective-permute-done.3.rest_2_
  19.4 1.5 collective-permute-start.4
  20.9 0.0 collective-permute-done.5.rest_3_
  21.0 1.5 collective-permute-start.6
  22.4 0.1 maximum_maximum_fusion.bias_ref
  22.5 0.1 eq.81
  22.7 0.0 copy-start
  22.7 2.2 %copy-done = bf16[2048,1024]{1,0:T(8,128)(2,1)S(1)} copy-done((bf16[2048,1024]{1,0:T(8,128)(2,1)S(1)}, bf16[2048,1024]{1,0:T(8,128)(2,1)}, u32[]{:S(2)}) %copy-start) | copy-done | bytes 4194328
  24.9 1.2 copy-done.3
  26.1 1.6 queries.1.q_ref
  27.7 0.0 copy-start.6
  27.7 3.7 %attend.2 = (f32[8,8,256]{2,1,0:T(8,128)S(1)}, f32[8,128,256]{2,1,0:T(8,128)S(1)}) custom-call(f32[4]{0:T(128)S(1)} %maximum_maximum_fusion.1.bias_ref, bf16[256,1024]{1,0:T(8,128)(2,1)S(1)} %queries.1.q_ref, bf16[512,128]{1,0:T(8,128)(2,1)S(1)} %copy-done.4, bf16[512,128]{1,0:T(8,128)(2,1)S(1)} %collective-permute-done.1.rest_1_, ...), custom_call_target="tpu_custom_call" | custom-call | tf_op jit(solution)/shard_map/attend/pallas_call | solution.py:146
  31.5 3.7 %attend.3 = bf16[256,1024]{1,0:T(8,128)(2,1)S(1)} custom-call(f32[4]{0:T(128)S(1)} %maximum_maximum_fusion.bias_ref, bf16[256,1024]{1,0:T(8,128)(2,1)S(1)} %queries.1.q_ref, bf16[512,128]{1,0:T(8,128)(2,1)S(1)} %collective-permute-done.rest_0_, bf16[512,128]{1,0:T(8,128)(2,1)S(1)} %collective-permute-done.2.rest_1_, ...), custom_call_target="tpu_custom_call" | custom-call | tf_op jit(solution)/shard_map/attend/pallas_call | solution.py:146
  35.3 0.7 fusion
  36.1 0.1 collective-permute-start.8
  36.2 0.7 fusion.2
  36.9 0.0 copy-start.13
  36.9 0.6 collective-permute-start.7
  37.5 0.2 collective-permute-done.8
  37.7 1.6 collective-permute-start.9
  39.3 0.1 fusion.31
  39.4 6.7 %collective-permute-done.9 = bf16[64,2048]{1,0:T(8,128)(2,1)S(1)} collective-permute-done((bf16[64,2048]{1,0:T(8,128)(2,1)S(1)}, bf16[64,2048]{1,0:T(8,128)(2,1)S(1)}, u32[]{:S(2)}, u32[]{:S(2)}) %collective-permute-start.9) | collective-permute-done | bytes 262176 | tf_op jit(solution)/shard_map/ppermute | solution.py:374
  46.1 1.2 multiply_reduce_fusion
  47.4 0.8 copy-done.9
  48.2 0.1 multiply_convert_fusion
  48.3 6.4 %collective-permute-start.11 = (bf16[64,2048]{1,0:T(8,128)(2,1)S(1)}, bf16[64,2048]{1,0:T(8,128)(2,1)S(1)}, u32[]{:S(2)}, u32[]{:S(2)}) collective-permute-start(bf16[64,2048]{1,0:T(8,128)(2,1)S(1)} %multiply_convert_fusion), channel_id=1, source_target_pairs={{0,24},{1,25},{2,26},{3,27},{4,28},{5,29},{6,30},{7,31},{8,16},{9,... | collective-permute-start | bytes 786440 | tf_op jit(solution)/shard_map/ppermute | solution.py:416
  54.7 0.1 fusion.4
  54.8 0.1 fusion.5
  54.9 0.1 bitcast_compare_fusion
  55.1 5.4 %collective-permute-done.11 = bf16[64,2048]{1,0:T(8,128)(2,1)S(1)} collective-permute-done((bf16[64,2048]{1,0:T(8,128)(2,1)S(1)}, bf16[64,2048]{1,0:T(8,128)(2,1)S(1)}, u32[]{:S(2)}, u32[]{:S(2)}) %collective-permute-start.11) | collective-permute-done | bytes 262176 | tf_op jit(solution)/shard_map/ppermute | solution.py:416
  60.5 1.7 convolution_convert_fusion
  62.3 7.8 %all-to-all-start.2 = ((bf16[16,24,2048]{2,1,0:T(8,128)(2,1)}), bf16[16,24,2048]{2,1,0:T(8,128)(2,1)S(1)}, u32[]{:S(2)}, u32[]{:S(2)}) async-start(bf16[16,24,2048]{2,1,0:T(8,128)(2,1)} %bitcast.26), calls=%async_computation.2 | async-start | bytes 3145728 | tf_op jit(solution)/shard_map/all_to_all | solution.py:387
  70.1 1.7 convolution_convert_fusion.1
  71.8 21.0 %all-to-all-done.2 = bf16[16,24,2048]{2,1,0:T(8,128)(2,1)S(1)} async-done(((bf16[16,24,2048]{2,1,0:T(8,128)(2,1)}), bf16[16,24,2048]{2,1,0:T(8,128)(2,1)S(1)}, u32[]{:S(2)}, u32[]{:S(2)}) %all-to-all-start.2) | async-done | bytes 1572896 | tf_op jit(solution)/shard_map/all_to_all | solution.py:387
  92.8 1.2 copy-done.7
  94.0 3.9 %all-to-all-start = ((bf16[16,24,2048]{2,1,0:T(8,128)(2,1)}), bf16[16,24,2048]{2,1,0:T(8,128)(2,1)S(1)}, u32[]{:S(2)}, u32[]{:S(2)}) async-start(bf16[16,24,2048]{2,1,0:T(8,128)(2,1)} %bitcast.96), calls=%async_computation | async-start | bytes 3145728 | tf_op jit(solution)/shard_map/all_to_all | solution.py:387
  97.9 8.3 %experts.3 = bf16[384,2048]{1,0:T(8,128)(2,1)} custom-call(bf16[384,2048]{1,0:T(8,128)(2,1)} %bitcast.94, bf16[2048,768]{1,0:T(8,128)(2,1)} %bitcast.87, bf16[2048,768]{1,0:T(8,128)(2,1)} %bitcast.89, bf16[768,2048]{1,0:T(8,128)(2,1)} %bitcast.91), custom_call_target="tpu_custom_call" | custom-call | tf_op jit(solution)/shard_map/experts/pallas_call | solution.py:203
  106.3 14.2 %all-to-all-done = bf16[16,24,2048]{2,1,0:T(8,128)(2,1)S(1)} async-done(((bf16[16,24,2048]{2,1,0:T(8,128)(2,1)}), bf16[16,24,2048]{2,1,0:T(8,128)(2,1)S(1)}, u32[]{:S(2)}, u32[]{:S(2)}) %all-to-all-start) | async-done | bytes 1572896 | tf_op jit(solution)/shard_map/all_to_all | solution.py:387
  120.5 1.2 copy-done.8
  121.6 3.7 %all-to-all-start.3 = ((bf16[16,24,2048]{2,1,0:T(8,128)(2,1)}), bf16[16,24,2048]{2,1,0:T(8,128)(2,1)S(1)}, u32[]{:S(2)}, u32[]{:S(2)}) async-start(bf16[16,24,2048]{2,1,0:T(8,128)(2,1)} %bitcast.97), calls=%async_computation.3 | async-start | bytes 3145728 | tf_op jit(solution)/shard_map/all_to_all | solution.py:387
  125.4 8.3 %experts.2 = bf16[384,2048]{1,0:T(8,128)(2,1)} custom-call(bf16[384,2048]{1,0:T(8,128)(2,1)} %bitcast.95, bf16[2048,768]{1,0:T(8,128)(2,1)} %bitcast.88, bf16[2048,768]{1,0:T(8,128)(2,1)} %bitcast.90, bf16[768,2048]{1,0:T(8,128)(2,1)} %bitcast.92), custom_call_target="tpu_custom_call" | custom-call | tf_op jit(solution)/shard_map/experts/pallas_call | solution.py:203
  133.6 14.5 %all-to-all-done.3 = bf16[16,24,2048]{2,1,0:T(8,128)(2,1)S(1)} async-done(((bf16[16,24,2048]{2,1,0:T(8,128)(2,1)}), bf16[16,24,2048]{2,1,0:T(8,128)(2,1)S(1)}, u32[]{:S(2)}, u32[]{:S(2)}) %all-to-all-start.3) | async-done | bytes 1572896 | tf_op jit(solution)/shard_map/all_to_all | solution.py:387
  148.1 3.7 %all-to-all-start.1 = ((bf16[16,24,2048]{2,1,0:T(8,128)(2,1)}), bf16[16,24,2048]{2,1,0:T(8,128)(2,1)S(1)}, u32[]{:S(2)}, u32[]{:S(2)}) async-start(bf16[16,24,2048]{2,1,0:T(8,128)(2,1)} %bitcast.93), calls=%async_computation.1 | async-start | bytes 3145728 | tf_op jit(solution)/shard_map/all_to_all | solution.py:387
  151.8 0.1 fusion.32
  151.9 0.1 fusion.16
  152.0 0.1 fusion.17
  152.2 0.5 fusion.25
  152.7 0.1 fusion.6
  152.8 1.6 collective-permute-start.12
  154.4 25.8 %all-to-all-done.1 = bf16[16,24,2048]{2,1,0:T(8,128)(2,1)S(1)} async-done(((bf16[16,24,2048]{2,1,0:T(8,128)(2,1)}), bf16[16,24,2048]{2,1,0:T(8,128)(2,1)S(1)}, u32[]{:S(2)}, u32[]{:S(2)}) %all-to-all-start.1) | async-done | bytes 1572896 | tf_op jit(solution)/shard_map/all_to_all | solution.py:387
  180.2 0.5 fusion.21
  180.8 0.8 fusion.9
  (40 shorter events, 0.3 us)
Async XLA Ops:
  0.6 17.7 %copy-start.12 = (f32[64,8]{0,1:T(8,128)S(1)}, f32[64,8]{0,1:T(8,128)}, u32[]{:S(2)}) copy-start(f32[64,8]{0,1:T(8,128)} %param.24) | copy-start | bytes 6148
  0.6 17.7 %copy-start.11 = (s32[64,8]{0,1:T(8,128)S(1)}, s32[64,8]{0,1:T(8,128)}, u32[]{:S(2)}) copy-start(s32[64,8]{0,1:T(8,128)} %param.23) | copy-start | bytes 6148
  0.6 22.1 %copy-start.5 = (f32[128]{0:T(128)S(1)}, f32[128]{0:T(128)}, u32[]{:S(2)}) copy-start(f32[128]{0:T(128)} %param.19) | copy-start | bytes 1540
  1.4 21.3 %copy-start.1 = (f32[256,128]{1,0:T(8,128)S(1)}, f32[256,128]{1,0:T(8,128)}, u32[]{:S(2)}) copy-start(f32[256,128]{1,0:T(8,128)} %get-tuple-element.32.cos_ref) | copy-start | bytes 393220
  1.4 21.3 %copy-start.2 = (f32[256,128]{1,0:T(8,128)S(1)}, f32[256,128]{1,0:T(8,128)}, u32[]{:S(2)}) copy-start(f32[256,128]{1,0:T(8,128)} %get-tuple-element.33.sin_ref) | copy-start | bytes 393220
  5.8 12.8 %collective-permute-start.1 = (bf16[512,128]{1,0:T(8,128)(2,1)}, bf16[512,128]{1,0:T(8,128)(2,1)S(1)}, u32[]{:S(2)}, u32[]{:S(2)}) collective-permute-start(bf16[512,128]{1,0:T(8,128)(2,1)} %get-tuple-element.10.rest_0_), channel_id=1, source_target_pairs={{0,8},{1,9},{2,10},{3,11},{4,12},{5,13},{6,14},{7,15},{8,16},{9,17... | collective-permute-start | bytes 393224 | tf_op jit(solution)/shard_map/ppermute | solution.py:295
  10.7 8.7 %collective-permute-start.3 = (bf16[512,128]{1,0:T(8,128)(2,1)}, bf16[512,128]{1,0:T(8,128)(2,1)S(1)}, u32[]{:S(2)}, u32[]{:S(2)}) collective-permute-start(bf16[512,128]{1,0:T(8,128)(2,1)} %get-tuple-element.10.rest_0_), channel_id=1, source_target_pairs={{0,16},{1,17},{2,18},{3,19},{4,20},{5,21},{6,22},{7,23},{8,24},{9,... | collective-permute-start | bytes 393224 | tf_op jit(solution)/shard_map/ppermute | solution.py:295
  15.2 5.7 %collective-permute-start.5 = (bf16[512,128]{1,0:T(8,128)(2,1)}, bf16[512,128]{1,0:T(8,128)(2,1)S(1)}, u32[]{:S(2)}, u32[]{:S(2)}) collective-permute-start(bf16[512,128]{1,0:T(8,128)(2,1)} %get-tuple-element.10.rest_0_), channel_id=1, source_target_pairs={{0,24},{1,25},{2,26},{3,27},{4,28},{5,29},{6,30},{7,31}} | collective-permute-start | bytes 393224 | tf_op jit(solution)/shard_map/ppermute | solution.py:295
  16.7 14.7 %collective-permute-start = (bf16[512,128]{1,0:T(8,128)(2,1)}, bf16[512,128]{1,0:T(8,128)(2,1)S(1)}, u32[]{:S(2)}, u32[]{:S(2)}) collective-permute-start(bf16[512,128]{1,0:T(8,128)(2,1)} %get-tuple-element.10.rest_0_), channel_id=1, source_target_pairs={{0,4},{1,5},{2,6},{3,7},{4,0},{5,1},{6,2},{7,3},{8,12},{9,13},{10,... | collective-permute-start | bytes 393224 | tf_op jit(solution)/shard_map/ppermute | solution.py:300
  18.4 21.0 %collective-permute-start.10 = (f32[64,16]{0,1:T(8,128)S(1)}, f32[64,16]{0,1:T(8,128)S(1)}, u32[]{:S(2)}, u32[]{:S(2)}) collective-permute-start(f32[64,16]{0,1:T(8,128)S(1)} %pad_maximum_fusion.2), channel_id=1, source_target_pairs={{0,24},{1,25},{2,26},{3,27},{4,28},{5,29},{6,30},{7,31},{8,16},{9,... | collective-permute-start | bytes 12296 | tf_op jit(solution)/shard_map/ppermute | solution.py:319
  18.5 12.9 %collective-permute-start.2 = (bf16[512,128]{1,0:T(8,128)(2,1)S(1)}, bf16[512,128]{1,0:T(8,128)(2,1)S(1)}, u32[]{:S(2)}, u32[]{:S(2)}) collective-permute-start(bf16[512,128]{1,0:T(8,128)(2,1)S(1)} %collective-permute-done.1.rest_1_), channel_id=1, source_target_pairs={{0,4},{1,5},{2,6},{3,7},{4,0},{5,1},{6,2},{7,3},{8,12},{9,13},{10,... | collective-permute-start | bytes 393224 | tf_op jit(solution)/shard_map/ppermute | solution.py:300
  19.4 12.0 %collective-permute-start.4 = (bf16[512,128]{1,0:T(8,128)(2,1)S(1)}, bf16[512,128]{1,0:T(8,128)(2,1)S(1)}, u32[]{:S(2)}, u32[]{:S(2)}) collective-permute-start(bf16[512,128]{1,0:T(8,128)(2,1)S(1)} %collective-permute-done.3.rest_2_), channel_id=1, source_target_pairs={{0,4},{1,5},{2,6},{3,7},{4,0},{5,1},{6,2},{7,3},{8,12},{9,13},{10,... | collective-permute-start | bytes 393224 | tf_op jit(solution)/shard_map/ppermute | solution.py:300
  21.0 10.5 %collective-permute-start.6 = (bf16[512,128]{1,0:T(8,128)(2,1)S(1)}, bf16[512,128]{1,0:T(8,128)(2,1)S(1)}, u32[]{:S(2)}, u32[]{:S(2)}) collective-permute-start(bf16[512,128]{1,0:T(8,128)(2,1)S(1)} %collective-permute-done.5.rest_3_), channel_id=1, source_target_pairs={{0,4},{1,5},{2,6},{3,7},{4,0},{5,1},{6,2},{7,3},{8,12},{9,13},{10,... | collective-permute-start | bytes 393224 | tf_op jit(solution)/shard_map/ppermute | solution.py:300
  22.7 2.2 %copy-start = (bf16[2048,1024]{1,0:T(8,128)(2,1)S(1)}, bf16[2048,1024]{1,0:T(8,128)(2,1)}, u32[]{:S(2)}) copy-start(bf16[2048,1024]{1,0:T(8,128)(2,1)} %wq_ref.1) | copy-start | bytes 12582916
  24.9 1.2 copy-start.3
  26.1 1.6 copy-start.4
  27.7 7.6 %copy-start.6 = (bf16[1024,2048]{1,0:T(8,128)(2,1)S(1)}, bf16[1024,2048]{1,0:T(8,128)(2,1)}, u32[]{:S(2)}) copy-start(bf16[1024,2048]{1,0:T(8,128)(2,1)} %param.21) | copy-start | bytes 12582916
  36.1 1.6 collective-permute-start.8
  36.9 11.2 %copy-start.13 = (f32[2048]{0:T(1024)S(1)}, f32[2048]{0:T(1024)}, u32[]{:S(2)}) copy-start(f32[2048]{0:T(1024)} %param.22) | copy-start | bytes 24580
  36.9 2.5 %collective-permute-start.7 = (bf16[64,2048]{1,0:T(8,128)(2,1)S(1)}, bf16[64,2048]{1,0:T(8,128)(2,1)S(1)}, u32[]{:S(2)}, u32[]{:S(2)}) collective-permute-start(bf16[64,2048]{1,0:T(8,128)(2,1)S(1)} %fusion.13), channel_id=1, source_target_pairs={{0,1},{1,0},{2,3},{3,2},{4,5},{5,4},{6,7},{7,6},{8,9},{9,8},{10,11... | collective-permute-start | bytes 786440 | tf_op jit(solution)/shard_map/ppermute | solution.py:368
  37.7 8.4 %collective-permute-start.9 = (bf16[64,2048]{1,0:T(8,128)(2,1)S(1)}, bf16[64,2048]{1,0:T(8,128)(2,1)S(1)}, u32[]{:S(2)}, u32[]{:S(2)}) collective-permute-start(bf16[64,2048]{1,0:T(8,128)(2,1)S(1)} %fusion.10), channel_id=1, source_target_pairs={{0,2},{1,3},{2,0},{3,1},{4,6},{5,7},{6,4},{7,5},{8,10},{9,11},{10,... | collective-permute-start | bytes 786440 | tf_op jit(solution)/shard_map/ppermute | solution.py:374
  47.3 0.8 copy-start.9
  48.3 12.3 %collective-permute-start.11 = (bf16[64,2048]{1,0:T(8,128)(2,1)S(1)}, bf16[64,2048]{1,0:T(8,128)(2,1)S(1)}, u32[]{:S(2)}, u32[]{:S(2)}) collective-permute-start(bf16[64,2048]{1,0:T(8,128)(2,1)S(1)} %multiply_convert_fusion), channel_id=1, source_target_pairs={{0,24},{1,25},{2,26},{3,27},{4,28},{5,29},{6,30},{7,31},{8,16},{9,... | collective-permute-start | bytes 786440 | tf_op jit(solution)/shard_map/ppermute | solution.py:416
  62.3 30.5 %all-to-all-start.2 = ((bf16[16,24,2048]{2,1,0:T(8,128)(2,1)}), bf16[16,24,2048]{2,1,0:T(8,128)(2,1)S(1)}, u32[]{:S(2)}, u32[]{:S(2)}) async-start(bf16[16,24,2048]{2,1,0:T(8,128)(2,1)} %bitcast.26), calls=%async_computation.2 | async-start | bytes 3145728 | tf_op jit(solution)/shard_map/all_to_all | solution.py:387
  92.8 1.2 copy-start.7
  94.0 26.5 %all-to-all-start = ((bf16[16,24,2048]{2,1,0:T(8,128)(2,1)}), bf16[16,24,2048]{2,1,0:T(8,128)(2,1)S(1)}, u32[]{:S(2)}, u32[]{:S(2)}) async-start(bf16[16,24,2048]{2,1,0:T(8,128)(2,1)} %bitcast.96), calls=%async_computation | async-start | bytes 3145728 | tf_op jit(solution)/shard_map/all_to_all | solution.py:387
  120.5 1.2 copy-start.8
  121.6 26.5 %all-to-all-start.3 = ((bf16[16,24,2048]{2,1,0:T(8,128)(2,1)}), bf16[16,24,2048]{2,1,0:T(8,128)(2,1)S(1)}, u32[]{:S(2)}, u32[]{:S(2)}) async-start(bf16[16,24,2048]{2,1,0:T(8,128)(2,1)} %bitcast.97), calls=%async_computation.3 | async-start | bytes 3145728 | tf_op jit(solution)/shard_map/all_to_all | solution.py:387
  148.1 32.1 %all-to-all-start.1 = ((bf16[16,24,2048]{2,1,0:T(8,128)(2,1)}), bf16[16,24,2048]{2,1,0:T(8,128)(2,1)S(1)}, u32[]{:S(2)}, u32[]{:S(2)}) async-start(bf16[16,24,2048]{2,1,0:T(8,128)(2,1)} %bitcast.93), calls=%async_computation.1 | async-start | bytes 3145728 | tf_op jit(solution)/shard_map/all_to_all | solution.py:387
  152.8 28.0 %copy-start.10 = (f32[64,2048]{1,0:T(8,128)S(1)}, f32[64,2048]{1,0:T(8,128)}, u32[]{:S(2)}) copy-start(f32[64,2048]{1,0:T(8,128)} %copy-done.9) | copy-start | bytes 1572868
  152.8 27.9 %collective-permute-start.12 = (bf16[64,2048]{1,0:T(8,128)(2,1)S(1)}, bf16[64,2048]{1,0:T(8,128)(2,1)S(1)}, u32[]{:S(2)}, u32[]{:S(2)}) collective-permute-start(bf16[64,2048]{1,0:T(8,128)(2,1)S(1)} %fusion.6), channel_id=1, source_target_pairs={{0,24},{1,25},{2,26},{3,27},{4,28},{5,29},{6,30},{7,31},{8,16},{9,... | collective-permute-start | bytes 786440 | tf_op jit(solution)/shard_map/ppermute | solution.py:422

commit v3 on v2

--- a/solution.py
+++ b/solution.py
@@ -31,40 +31,32 @@
     return pltpu.CompilerParams(vmem_limit_bytes=mib * 2**20)
 
 
-def first_kernel(
-    x_hbm, wk_hbm, wv_hbm, gain_ref, kgain_ref, cos_ref, sin_ref, normed_ref, kv_ref, x_ref, wk_ref, wv_ref, sems
-):
+def first_kernel(*refs):
+    hbm, (kv_ref,), held, sems = refs[:7], refs[7:8], refs[8:15], refs[15]
+    x_ref, wk_ref, wv_ref, gain_ref, kgain_ref, cos_ref, sin_ref = held
     rows, head_dim = x_ref.shape[0], wk_ref.shape[1]
-    half = rows // 2
-    copies = [
-        pltpu.make_async_copy(x_hbm.at[pl.ds(0, half)], x_ref.at[pl.ds(0, half)], sems.at[0]),
-        pltpu.make_async_copy(x_hbm.at[pl.ds(half, half)], x_ref.at[pl.ds(half, half)], sems.at[1]),
-        pltpu.make_async_copy(wk_hbm, wk_ref, sems.at[2]),
-        pltpu.make_async_copy(wv_hbm, wv_ref, sems.at[3]),
-    ]
-    for copy in copies:
-        copy.start()
-    for i in range(2):
+    copies = [pltpu.make_async_copy(a, b, sems.at[i]) for i, (a, b) in enumerate(zip(hbm, held))]
+    for i in (0, 3, 1, 4, 5, 6, 2):
+        copies[i].start()
+    copies[0].wait()
+    copies[3].wait()
+    normed = rms_scale(x_ref[...].astype(jnp.float32), gain_ref[...]).astype(jnp.bfloat16)
+    for i in (1, 4, 5, 6):
         copies[i].wait()
-        part = slice(i * half, (i + 1) * half)
-        normed_ref[part, :] = rms_scale(x_ref[part, :].astype(jnp.float32), gain_ref[...]).astype(
-            jnp.bfloat16
-        )
-    normed = normed_ref[...]
-    copies[2].wait()
     keys = jnp.dot(normed, wk_ref[...], preferred_element_type=jnp.float32)
     keys = turn(rms_scale(keys, kgain_ref[...]), cos_ref, sin_ref)
     kv_ref[:rows, :] = keys.astype(jnp.bfloat16)
-    copies[3].wait()
+    copies[2].wait()
     values = jnp.dot(normed, wv_ref[...], preferred_element_type=jnp.float32)
     for i in range(0, rows, head_dim):
         kv_ref[rows + i : rows + i + head_dim, :] = values[i : i + head_dim, :].T.astype(jnp.bfloat16)
 
 
-def query_kernel(head_dim, step, normed_ref, wq_ref, qgain_ref, cos_ref, sin_ref, q_ref):
+def query_kernel(head_dim, step, x_ref, gain_ref, wq_ref, qgain_ref, cos_ref, sin_ref, q_ref):
+    normed = rms_scale(x_ref[...].astype(jnp.float32), gain_ref[...]).astype(jnp.bfloat16)
     for start in range(0, wq_ref.shape[1], step):
         wide = jnp.dot(
-            normed_ref[...], wq_ref[:, start : start + step], preferred_element_type=jnp.float32
+            normed, wq_ref[:, start : start + step], preferred_element_type=jnp.float32
         )
         for i in range(0, step, head_dim):
             q_ref[:, start + i : start + i + head_dim] = turn(
@@ -155,25 +147,22 @@
 
 
 def expert_kernel(
-    x_hbm, wg_hbm, wu_hbm, wd_hbm, out_hbm, x_ref, wg_ref, wu_ref, wd_ref, hidden_ref, out_ref, sems
+    x_hbm, wg_ref, wu_hbm, wd_hbm, out_hbm, x_ref, wu_ref, wd_ref, hidden_ref, out_ref, sems
 ):
     rows, width = x_hbm.shape
     ins = [
         pltpu.make_async_copy(hbm, ref, sems.at[i])
-        for i, (hbm, ref) in enumerate(
-            ((x_hbm, x_ref), (wg_hbm, wg_ref), (wu_hbm, wu_ref), (wd_hbm, wd_ref))
-        )
+        for i, (hbm, ref) in enumerate(((x_hbm, x_ref), (wu_hbm, wu_ref), (wd_hbm, wd_ref)))
     ]
     for copy in ins:
         copy.start()
     ins[0].wait()
-    ins[1].wait()
     gate = jnp.dot(x_ref[...], wg_ref[...], preferred_element_type=jnp.float32)
     gate = gate / (1.0 + jnp.exp(-gate))
-    ins[2].wait()
+    ins[1].wait()
     up = jnp.dot(x_ref[...], wu_ref[...], preferred_element_type=jnp.float32)
     hidden_ref[...] = (gate * up).astype(jnp.bfloat16)
-    ins[3].wait()
+    ins[2].wait()
     halves = 2 if rows % 32 == 0 else 1
     half = rows // halves
     part = 512 if width % 512 == 0 else width
@@ -187,7 +176,7 @@
             ).astype(jnp.bfloat16)
         outs.append(
             pltpu.make_async_copy(
-                out_ref.at[pl.ds(k * half, half)], out_hbm.at[pl.ds(k * half, half)], sems.at[4 + k]
+                out_ref.at[pl.ds(k * half, half)], out_hbm.at[pl.ds(k * half, half)], sems.at[3 + k]
             )
         )
         outs[-1].start()
@@ -198,20 +187,34 @@
 def run_experts(grouped, w_gate, w_up, w_down):
     experts, rows, width = grouped.shape
     ff = w_gate.shape[2]
-    held = ((rows, width), (width, ff), (width, ff), (ff, width), (rows, ff), (rows, width))
+    held = ((rows, width), (width, ff), (ff, width), (rows, ff), (rows, width))
+    gates = [pltpu.with_memory_space_constraint(w_gate[e], pltpu.VMEM) for e in range(experts)]
     made = [
         pl.pallas_call(
             expert_kernel,
             out_shape=jax.ShapeDtypeStruct((rows, width), jnp.bfloat16),
-            in_specs=[ANY] * 4,
+            in_specs=[ANY, VMEM, ANY, ANY],
             out_specs=ANY,
             scratch_shapes=[pltpu.VMEM(shape, jnp.bfloat16) for shape in held]
-            + [pltpu.SemaphoreType.DMA((6,))],
+            + [pltpu.SemaphoreType.DMA((5,))],
             name="experts",
-        )(grouped[e], w_gate[e], w_up[e], w_down[e])
+        )(grouped[e], gates[e], w_up[e], w_down[e])
         for e in range(experts)
     ]
     return made[0][None] if experts == 1 else jnp.stack(made)
+
+
+def route_kernel(*refs):
+    parts, (rows_ref, gain_ref, pick_ref, residual_ref, routed_ref, out_ref) = refs[:-6], refs[-6:]
+    residual = rows_ref[...].astype(jnp.float32)
+    for ref in parts:
+        residual = residual + ref[...].astype(jnp.float32)
+    residual_ref[...] = residual
+    routed = rms_scale(residual, gain_ref[...]).astype(jnp.bfloat16)
+    routed_ref[...] = routed
+    out_ref[...] = jnp.dot(
+        pick_ref[...], routed, preferred_element_type=jnp.float32
+    ).astype(jnp.bfloat16)
 
 
 def pairs(seq_count, head_count, step):
@@ -270,22 +273,18 @@
     cos_table = jnp.concatenate([cosine, cosine], axis=1)
     sin_table = jnp.concatenate([-sine, sine], axis=1)
 
-    normed, own_kv = pl.pallas_call(
+    first_in = (
+        tokens, w_key, w_value, input_gain[None], key_gain[None], cos_table, sin_table
+    )
+    own_kv = pl.pallas_call(
         first_kernel,
-        out_shape=(
-            jax.ShapeDtypeStruct((tok_rows, width), jnp.bfloat16),
-            jax.ShapeDtypeStruct((2 * tok_rows, head_dim), jnp.bfloat16),
-        ),
-        in_specs=[ANY] * 3 + [VMEM] * 4,
-        out_specs=(VMEM, VMEM),
-        scratch_shapes=[
-            pltpu.VMEM(tokens.shape, tokens.dtype),
-            pltpu.VMEM(w_key.shape, w_key.dtype),
-            pltpu.VMEM(w_value.shape, w_value.dtype),
-            pltpu.SemaphoreType.DMA((4,)),
-        ],
+        out_shape=jax.ShapeDtypeStruct((2 * tok_rows, head_dim), jnp.bfloat16),
+        in_specs=[ANY] * len(first_in),
+        out_specs=VMEM,
+        scratch_shapes=[pltpu.VMEM(x.shape, x.dtype) for x in first_in]
+        + [pltpu.SemaphoreType.DMA((len(first_in),))],
         name="norm_kv",
-    )(tokens, w_key, w_value, input_gain[None], key_gain[None], cos_table, sin_table)
+    )(*first_in)
 
     kv_blocks, kv_bias = [own_kv], [jnp.float32(0.0)]
     for k in range(1, line):
@@ -330,7 +329,7 @@
         mix_table = jnp.sum(jnp.where(named, weights[:, :, None], 0.0), axis=1)
         place = jnp.where(counts > 0, rank_table, -1.0).astype(jnp.int32)
         in_slot = place[:, :, None] == jnp.arange(capacity, dtype=jnp.int32)[None, None, :]
-        pick = in_slot.astype(jnp.bfloat16).reshape(rows_here, slots)
+        pick = in_slot.astype(jnp.bfloat16).reshape(rows_here, slots).T
         mix = jnp.where(in_slot, mix_table[:, :, None], 0.0).reshape(rows_here, slots)
         return pick, jnp.concatenate(split_exact(mix), axis=0)
 
@@ -339,17 +338,33 @@
     rot_q = pl.pallas_call(
         functools.partial(query_kernel, head_dim, query_step),
         out_shape=jax.ShapeDtypeStruct((tok_rows, w_query.shape[1]), jnp.bfloat16),
-        in_specs=[VMEM] * 5,
+        in_specs=[VMEM] * 6,
         out_specs=VMEM,
         compiler_params=room(12),
         name="queries",
-    )(normed, w_query, query_gain[None], cos_table, sin_table)
-
+    )(tokens, input_gain[None], w_query, query_gain[None], cos_table, sin_table)
+
+    near = line // 2
     if side == 2:
-        state = attend(rot_q, head_dim, kv_blocks[:line], kv_bias[:line], (), False)
-        attended = attend(rot_q, head_dim, kv_blocks[line:], kv_bias[line:], state, True)
+        parts = [
+            [*range(near), *range(line, line + near - 1)],
+            [*range(near, line), *range(line + near - 1, line + near)],
+            [*range(line + near, 2 * line)],
+        ]
     else:
-        attended = attend(rot_q, head_dim, kv_blocks, kv_bias, (), True)
+        parts = [[*range(near)], [*range(near, line)]]
+    parts = [part for part in parts if part]
+    state = ()
+    for n, part in enumerate(parts):
+        state = attend(
+            rot_q,
+            head_dim,
+            [kv_blocks[k] for k in part],
+            [kv_bias[k] for k in part],
+            state,
+            n == len(parts) - 1,
+        )
+    attended = state
 
     by_tower = attended.reshape(towers, cores * rows_here, attended.shape[1])
     core_swap = make_pairs(lambda s, h: (s, h ^ 1))
@@ -368,18 +383,24 @@
         came = lax.ppermute(give.astype(jnp.bfloat16), BOTH, core_swap)
         return keep + came.astype(jnp.float32)
 
-    attn_part = None
+    summed = []
     for k in range(1, towers):
         shift = make_pairs(lambda s, h, k=k: (s, (h + k * cores) % head_count))
-        came = lax.ppermute(tower_sum(k).astype(jnp.bfloat16), BOTH, shift)
-        came = came.astype(jnp.float32)
-        attn_part = came if attn_part is None else attn_part + came
-    own_sum = tower_sum(0)
-    attn_part = own_sum if attn_part is None else own_sum + attn_part
+        summed.append(lax.ppermute(tower_sum(k).astype(jnp.bfloat16), BOTH, shift))
+    summed.append(tower_sum(0))
 
     own_rows = lax.dynamic_slice_in_dim(tokens, head_index * rows_here, rows_here, 0)
-    residual = own_rows.astype(jnp.float32) + attn_part
-    routed = rms_scale(residual, post_gain).astype(jnp.bfloat16)
+    residual, routed, outgoing = pl.pallas_call(
+        route_kernel,
+        out_shape=(
+            jax.ShapeDtypeStruct((rows_here, width), jnp.float32),
+            jax.ShapeDtypeStruct((rows_here, width), jnp.bfloat16),
+            jax.ShapeDtypeStruct((slots, width), jnp.bfloat16),
+        ),
+        in_specs=[VMEM] * (len(summed) + 3),
+        out_specs=(VMEM,) * 3,
+        name="route",
+    )(*summed, own_rows, post_gain[None], tables[0][0])
 
     groups = [list(range(g * members, (g + 1) * members)) for g in range(halves)]
 
@@ -393,10 +414,7 @@
             tiled=True,
         )
 
-    def dispatch(rows, pick):
-        outgoing = lax.dot_general(
-            pick, rows, (((0,), (0,)), ((), ())), preferred_element_type=jnp.float32
-        ).astype(jnp.bfloat16)
+    def dispatch(outgoing):
         return (
             exchange(outgoing)
             .reshape(members, local_count, capacity, width)
@@ -414,8 +432,10 @@
     weights = (w_gate, w_up, w_down)
     if halves == 2:
         mirrored = lax.ppermute(routed, BOTH, mirror)
-        own_rows_in = dispatch(routed, tables[0][0])
-        far_rows_in = dispatch(mirrored, tables[1][0])
+        own_rows_in = dispatch(outgoing)
+        far_rows_in = dispatch(
+            jnp.dot(tables[1][0], mirrored, preferred_element_type=jnp.float32).astype(jnp.bfloat16)
+        )
         own_result = run_experts(own_rows_in, *weights)
         far_result = run_experts(far_rows_in, *weights)
         foreign = give_back(far_result, tables[1][1]).astype(jnp.bfloat16)
@@ -423,7 +443,7 @@
         expert_sum = give_back(own_result, tables[0][1])
         expert_sum = expert_sum + far_sum.astype(jnp.float32)
     else:
-        result = run_experts(dispatch(routed, tables[0][0]), *weights)
+        result = run_experts(dispatch(outgoing), *weights)
         expert_sum = give_back(result, tables[0][1])
     return (residual + expert_sum).astype(jnp.bfloat16)
 

time: 182 us -> 178 us (0.978)
  blocking collectives: 0 us -> 30.9 us
  waiting for transfers between devices: 88.2 us -> 64.4 us
  starting transfers between devices: 45.5 us -> 36.9 us
  local copies, waits for them, and re-layouts: 6.8 us -> 3.86 us
    all_to_all x0 -> x1, blocking collectives: none -> 30.9 us  [exchange(): lax.all_to_all(rows.reshape(members, local_count * capacity, width), BOTH...]
    all_to_all x4 -> x3, waiting for transfers between devices: 75.4 us -> 47.3 us  [exchange(): lax.all_to_all(rows.reshape(members, local_count * capacity, width), BOTH...]
    all_to_all x4 -> x3, starting transfers between devices: 19.2 us -> 13 us  [exchange(): lax.all_to_all(rows.reshape(members, local_count * capacity, width), BOTH...]
    ppermute x1, waiting for transfers between devices: 0.01 us -> 4.13 us  [body(): far_sum = lax.ppermute(foreign, BOTH, mirror)]
    unnamed x28 -> x26, local copies, waits for them, and re-layouts: 6.6 us -> 2.93 us
    ppermute x1, starting transfers between devices: 6.41 us -> 3.48 us  [body(): mirrored = lax.ppermute(routed, BOTH, mirror)]
    dot_general x2 -> x1, matrix products: 3.43 us -> 0.55 us  [body(): jnp.dot(tables[1][0], mirrored, preferred_element_type=jnp.float32)]
    pallas_call x1 -> x2, Pallas kernels: 4.33 us -> 6.62 us  [the longest x1 3.48 us: body(): pl.pallas_call(first_kernel, out_shape=jax.ShapeDtypeStruct((2 * tok_rows...]
  transfers between devices with their start and end apart: 17 -> 16, of which waited for: 8 -> 10; matrix products, arithmetic and copies ran while one was open for 3% -> 4% of each run, Pallas kernels for 14% -> 13%
where the time goes in v3:
time: 178 us; the launch traced here: 177 us
  waiting for transfers between devices  64.4 us (36%)
  starting transfers between devices  36.9 us (21%)
  Pallas kernels  31.4 us (18%)
  blocking collectives  30.9 us (17%)
  matrix products  4.77 us (3%)
  other arithmetic  4.61 us (3%)
  local copies, waits for them, and re-layouts  3.86 us (2%)
    all_to_all x3, waiting for transfers between devices, exchange(): lax.all_to_all(rows.reshape(members, local_count * capacity, width), BOTH...  47.3 us
    all_to_all x1, blocking collectives, exchange(): lax.all_to_all(rows.reshape(members, local_count * capacity, width), BOTH...  30.9 us
    pallas_call x2, Pallas kernels, run_experts(): pl.pallas_call(expert_kernel, out_shape=jax.ShapeDtypeStruct((rows, width...  14.7 us
    all_to_all x3, starting transfers between devices, exchange(): lax.all_to_all(rows.reshape(members, local_count * capacity, width), BOTH...  13 us
    ppermute x3, starting transfers between devices, body(): kv_blocks.append(lax.ppermute(own_kv, BOTH, up))  8.82 us
    pallas_call x3, Pallas kernels, attend(): pl.pallas_call(functools.partial(attend_kernel, head_dim, blocks, not sta...  8.37 us
    ppermute x1, waiting for transfers between devices, body(): mirrored = lax.ppermute(routed, BOTH, mirror)  6.12 us
    ppermute x1, waiting for transfers between devices, body(): summed.append(lax.ppermute(tower_sum(k).astype(jnp.bfloat16), BOTH, shift))  5.95 us
  transfers between devices with their start and end apart: 16, of which 10 were waited for; matrix products, arithmetic and copies ran while one was open for 4% of the time, Pallas kernels for 13%

profile of v3, /device:TPU:0, one launch (start us, length us, event | category | flops | bytes accessed | tf_op | source)
XLA Modules:
  0.0 177.3 jit_solution(15532267980376080714)
XLA Ops:
  0.0 0.5 fusion.32
  0.6 0.0 copy-start.12
  0.6 0.0 copy-start.11
  0.6 0.0 copy-start.1
  0.6 0.8 pad_maximum_fusion
  1.4 3.5 %norm_kv.1.rest_0_ = bf16[512,128]{1,0:T(8,128)(2,1)} custom-call(bf16[256,2048]{1,0:T(8,128)(2,1)} %refs_0_.1, bf16[2048,128]{1,0:T(8,128)(2,1)} %refs_1_.1, bf16[2048,128]{1,0:T(8,128)(2,1)} %refs_2_.1, f32[1,2048]{1,0:T(1,128)} %bitcast.85, f32[1,128]{1,0:T(1,128)} %bitcast.102, f32[256,128]{1,0:T(8,128)} %get-tuple-element.36.cos_ref.refs_5_, ...), custom_call_target="tpu_custom_call" | custom-call | tf_op jit(solution)/shard_map/norm_kv/pallas_call | solution.py:279
  4.9 3.0 %collective-permute-start.6 = (bf16[512,128]{1,0:T(8,128)(2,1)}, bf16[512,128]{1,0:T(8,128)(2,1)S(1)}, u32[]{:S(2)}, u32[]{:S(2)}) collective-permute-start(bf16[512,128]{1,0:T(8,128)(2,1)} %norm_kv.1.rest_0_), channel_id=1, source_target_pairs={{0,4},{1,5},{2,6},{3,7},{4,0},{5,1},{6,2},{7,3},{8,12},{9,13},{10,... | collective-permute-start | bytes 393224 | tf_op jit(solution)/shard_map/ppermute | solution.py:299
  8.0 3.5 %collective-permute-start.4 = (bf16[512,128]{1,0:T(8,128)(2,1)}, bf16[512,128]{1,0:T(8,128)(2,1)S(1)}, u32[]{:S(2)}, u32[]{:S(2)}) collective-permute-start(bf16[512,128]{1,0:T(8,128)(2,1)} %norm_kv.1.rest_0_), channel_id=1, source_target_pairs={{0,8},{1,9},{2,10},{3,11},{4,12},{5,13},{6,14},{7,15},{8,16},{9,17... | collective-permute-start | bytes 393224 | tf_op jit(solution)/shard_map/ppermute | solution.py:294
  11.4 3.3 %collective-permute-start.2 = (bf16[512,128]{1,0:T(8,128)(2,1)}, bf16[512,128]{1,0:T(8,128)(2,1)S(1)}, u32[]{:S(2)}, u32[]{:S(2)}) collective-permute-start(bf16[512,128]{1,0:T(8,128)(2,1)} %norm_kv.1.rest_0_), channel_id=1, source_target_pairs={{0,24},{1,25},{2,26},{3,27},{4,28},{5,29},{6,30},{7,31}} | collective-permute-start | bytes 393224 | tf_op jit(solution)/shard_map/ppermute | solution.py:294
  14.8 2.0 %collective-permute-start = (bf16[512,128]{1,0:T(8,128)(2,1)}, bf16[512,128]{1,0:T(8,128)(2,1)S(1)}, u32[]{:S(2)}, u32[]{:S(2)}) collective-permute-start(bf16[512,128]{1,0:T(8,128)(2,1)} %norm_kv.1.rest_0_), channel_id=1, source_target_pairs={{0,16},{1,17},{2,18},{3,19},{4,20},{5,21},{6,22},{7,23},{8,24},{9,... | collective-permute-start | bytes 393224 | tf_op jit(solution)/shard_map/ppermute | solution.py:294
  16.9 0.1 collective-permute-start.10
  17.0 0.1 pad_maximum_fusion.3.bias_ref
  17.1 0.1 pad_maximum_fusion.4.bias_ref
  17.2 0.7 constant_dynamic-slice_fusion.refs_2_
  17.9 0.1 pad_maximum_fusion.5.bias_ref
  18.0 0.1 eq.81
  18.1 0.0 copy-start.2
  18.1 2.2 %copy-done.2 = bf16[2048,1024]{1,0:T(8,128)(2,1)S(1)} copy-done((bf16[2048,1024]{1,0:T(8,128)(2,1)S(1)}, bf16[2048,1024]{1,0:T(8,128)(2,1)}, u32[]{:S(2)}) %copy-start.2) | copy-done | bytes 4194328
  20.3 1.8 queries.1.q_ref
  22.1 0.3 collective-permute-done.10
  22.4 0.1 fusion.30
  22.5 0.1 fusion.4
  22.6 0.5 collective-permute-start.5
  23.2 1.5 collective-permute-start.3
  24.7 0.5 collective-permute-start.1
  25.2 0.1 fusion.5
  25.3 0.8 bitcast_compare_fusion
  26.1 2.8 %attend.3 = (f32[8,8,256]{2,1,0:T(8,128)S(1)}, f32[8,128,256]{2,1,0:T(8,128)S(1)}) custom-call(f32[3]{0:T(128)S(1)} %pad_maximum_fusion.5.bias_ref, bf16[256,1024]{1,0:T(8,128)(2,1)S(1)} %queries.1.q_ref, bf16[512,128]{1,0:T(8,128)(2,1)S(1)} %copy-done.5, bf16[512,128]{1,0:T(8,128)(2,1)S(1)} %collective-permute-done.4.rest_1_, ...), custom_call_target="tpu_custom_call" | custom-call | tf_op jit(solution)/shard_map/attend/pallas_call | solution.py:138
  29.0 0.1 collective-permute-done.5.rest_2_
  29.0 3.0 %attend.4 = (f32[8,8,256]{2,1,0:T(8,128)S(1)}, f32[8,128,256]{2,1,0:T(8,128)S(1)}) custom-call(f32[3]{0:T(128)S(1)} %pad_maximum_fusion.4.bias_ref, bf16[256,1024]{1,0:T(8,128)(2,1)S(1)} %queries.1.q_ref, bf16[512,128]{1,0:T(8,128)(2,1)S(1)} %collective-permute-done.rest_0_, bf16[512,128]{1,0:T(8,128)(2,1)S(1)} %collective-permute-done.2.rest_1_, ...), custom_call_target="tpu_custom_call" | custom-call | tf_op jit(solution)/shard_map/attend/pallas_call | solution.py:138
  32.1 0.3 collective-permute-done.1.rest_0_
  32.4 2.5 %attend.5 = bf16[256,1024]{1,0:T(8,128)(2,1)S(1)} custom-call(f32[2]{0:T(128)S(1)} %pad_maximum_fusion.3.bias_ref, bf16[256,1024]{1,0:T(8,128)(2,1)S(1)} %queries.1.q_ref, bf16[512,128]{1,0:T(8,128)(2,1)S(1)} %collective-permute-done.1.rest_0_, bf16[512,128]{1,0:T(8,128)(2,1)S(1)} %collective-permute-done.3.rest_1_, ...), custom_call_target="tpu_custom_call" | custom-call | tf_op jit(solution)/shard_map/attend/pallas_call | solution.py:138
  34.9 0.7 fusion.2
  35.7 0.1 collective-permute-start.7
  35.8 0.7 fusion
  36.6 0.6 collective-permute-start.9
  37.1 0.2 collective-permute-done.7
  37.3 0.1 fusion.10
  37.4 1.6 collective-permute-start.8
  39.0 0.9 bitcast_add_fusion.refs_1_
  39.8 5.9 %collective-permute-done.8.refs_0_ = bf16[64,2048]{1,0:T(8,128)(2,1)S(1)} collective-permute-done((bf16[64,2048]{1,0:T(8,128)(2,1)S(1)}, bf16[64,2048]{1,0:T(8,128)(2,1)S(1)}, u32[]{:S(2)}, u32[]{:S(2)}) %collective-permute-start.8) | collective-permute-done | bytes 262176 | tf_op jit(solution)/shard_map/ppermute | solution.py:389
  45.8 0.7 copy-done.10
  46.5 3.1 %route.1 = (f32[64,2048]{1,0:T(8,128)}, bf16[64,2048]{1,0:T(8,128)(2,1)}, bf16[384,2048]{1,0:T(8,128)(2,1)}) custom-call(bf16[64,2048]{1,0:T(8,128)(2,1)} %copy-done.10, f32[64,2048]{1,0:T(8,128)} %bitcast_add_fusion.refs_1_, bf16[64,2048]{1,0:T(8,128)(2,1)} %constant_dynamic-slice_fusion.refs_2_, f32[1,2048]{1,0:T(1,128)} %bitcast.101, ...), custom_call_target="tpu_custom_call" | custom-call | tf_op jit(solution)/shard_map/route/pallas_call | solution.py:393
  49.6 3.5 %collective-permute-start.11 = (bf16[64,2048]{1,0:T(8,128)(2,1)}, bf16[64,2048]{1,0:T(8,128)(2,1)S(1)}, u32[]{:S(2)}, u32[]{:S(2)}) collective-permute-start(bf16[64,2048]{1,0:T(8,128)(2,1)} %get-tuple-element.18), channel_id=1, source_target_pairs={{0,24},{1,25},{2,26},{3,27},{4,28},{5,29},{6,30},{7,31},{8,16},{9,... | collective-permute-start | bytes 786440 | tf_op jit(solution)/shard_map/ppermute | solution.py:434
  53.1 6.1 %collective-permute-done.11 = bf16[64,2048]{1,0:T(8,128)(2,1)S(1)} collective-permute-done((bf16[64,2048]{1,0:T(8,128)(2,1)}, bf16[64,2048]{1,0:T(8,128)(2,1)S(1)}, u32[]{:S(2)}, u32[]{:S(2)}) %collective-permute-start.11) | collective-permute-done | bytes 262176 | tf_op jit(solution)/shard_map/ppermute | solution.py:434
  59.2 0.6 convolution_convert_fusion
  59.8 30.9 %all_to_all.20 = bf16[16,24,2048]{2,1,0:T(8,128)(2,1)} all-to-all(bf16[16,24,2048]{2,1,0:T(8,128)(2,1)S(1)} %bitcast.95), channel_id=1, replica_groups={{0,1,2,3,4,5,6,7,8,9,10,11,12,13,14,15},{16,17,18,19,20,21,22,23,24,25,..., dimensions={0} | all-to-all | bytes 3145728 | tf_op jit(solution)/shard_map/all_to_all | solution.py:408
  90.7 4.9 %all-to-all-start = ((bf16[16,24,2048]{2,1,0:T(8,128)(2,1)}), bf16[16,24,2048]{2,1,0:T(8,128)(2,1)}, u32[]{:S(2)}, u32[]{:S(2)}) async-start(bf16[16,24,2048]{2,1,0:T(8,128)(2,1)} %bitcast.97), calls=%async_computation | async-start | bytes 3145728 | tf_op jit(solution)/shard_map/all_to_all | solution.py:408
  95.6 7.3 %experts.3 = bf16[384,2048]{1,0:T(8,128)(2,1)} custom-call(bf16[384,2048]{1,0:T(8,128)(2,1)} %bitcast.94, bf16[2048,768]{1,0:T(8,128)(2,1)S(1)} %bitcast.82, bf16[2048,768]{1,0:T(8,128)(2,1)} %bitcast.88, bf16[768,2048]{1,0:T(8,128)(2,1)} %bitcast.90), custom_call_target="tpu_custom_call" | custom-call | tf_op jit(solution)/shard_map/experts/pallas_call | solution.py:193
  102.9 15.2 %all-to-all-done = bf16[16,24,2048]{2,1,0:T(8,128)(2,1)} async-done(((bf16[16,24,2048]{2,1,0:T(8,128)(2,1)}), bf16[16,24,2048]{2,1,0:T(8,128)(2,1)}, u32[]{:S(2)}, u32[]{:S(2)}) %all-to-all-start) | async-done | bytes 1572896 | tf_op jit(solution)/shard_map/all_to_all | solution.py:408
  118.1 4.4 %all-to-all-start.3 = ((bf16[16,24,2048]{2,1,0:T(8,128)(2,1)}), bf16[16,24,2048]{2,1,0:T(8,128)(2,1)}, u32[]{:S(2)}, u32[]{:S(2)}) async-start(bf16[16,24,2048]{2,1,0:T(8,128)(2,1)} %bitcast.93), calls=%async_computation.3 | async-start | bytes 3145728 | tf_op jit(solution)/shard_map/all_to_all | solution.py:408
  122.5 7.3 %experts.2 = bf16[384,2048]{1,0:T(8,128)(2,1)} custom-call(bf16[384,2048]{1,0:T(8,128)(2,1)} %bitcast.20.x_hbm, bf16[2048,768]{1,0:T(8,128)(2,1)S(1)} %bitcast.83, bf16[2048,768]{1,0:T(8,128)(2,1)} %bitcast.89, bf16[768,2048]{1,0:T(8,128)(2,1)} %bitcast.91), custom_call_target="tpu_custom_call" | custom-call | tf_op jit(solution)/shard_map/experts/pallas_call | solution.py:193
  129.9 15.5 %all-to-all-done.3 = bf16[16,24,2048]{2,1,0:T(8,128)(2,1)} async-done(((bf16[16,24,2048]{2,1,0:T(8,128)(2,1)}), bf16[16,24,2048]{2,1,0:T(8,128)(2,1)}, u32[]{:S(2)}, u32[]{:S(2)}) %all-to-all-start.3) | async-done | bytes 1572896 | tf_op jit(solution)/shard_map/all_to_all | solution.py:408
  145.3 3.7 %all-to-all-start.1 = ((bf16[16,24,2048]{2,1,0:T(8,128)(2,1)}), bf16[16,24,2048]{2,1,0:T(8,128)(2,1)S(1)}, u32[]{:S(2)}, u32[]{:S(2)}) async-start(bf16[16,24,2048]{2,1,0:T(8,128)(2,1)} %bitcast.92), calls=%async_computation.1 | async-start | bytes 3145728 | tf_op jit(solution)/shard_map/all_to_all | solution.py:408
  149.1 0.1 fusion.31
  149.2 0.1 fusion.15
  149.3 0.1 fusion.14
  149.4 2.0 %fusion.24 = f32[128,2048]{1,0:T(8,128)S(1)} fusion(bf16[384,2048]{1,0:T(8,128)(2,1)} %bitcast.31, bf16[64,384]{0,1:T(8,128)(2,1)S(1)} %get-tuple-element.29, bf16[64,384]{0,1:T(8,128)(2,1)S(1)} %get-tuple-element.27), kind=kOutput, calls=%fused_computation.41 | convolution fusion | flops 201523200 | bytes 2719744 | tf_op jit(solution)/shard_map/dot_general | solution.py:429
  151.4 0.1 fusion.6
  151.4 3.7 %collective-permute-start.12 = (bf16[64,2048]{1,0:T(8,128)(2,1)S(1)}, bf16[64,2048]{1,0:T(8,128)(2,1)S(1)}, u32[]{:S(2)}, u32[]{:S(2)}) collective-permute-start(bf16[64,2048]{1,0:T(8,128)(2,1)S(1)} %fusion.6), channel_id=1, source_target_pairs={{0,24},{1,25},{2,26},{3,27},{4,28},{5,29},{6,30},{7,31},{8,16},{9,... | collective-permute-start | bytes 786440 | tf_op jit(solution)/shard_map/ppermute | solution.py:442
  155.2 16.6 %all-to-all-done.1 = bf16[16,24,2048]{2,1,0:T(8,128)(2,1)S(1)} async-done(((bf16[16,24,2048]{2,1,0:T(8,128)(2,1)}), bf16[16,24,2048]{2,1,0:T(8,128)(2,1)S(1)}, u32[]{:S(2)}, u32[]{:S(2)}) %all-to-all-start.1) | async-done | bytes 1572896 | tf_op jit(solution)/shard_map/all_to_all | solution.py:408
  171.8 0.5 fusion.20
  172.4 4.1 %collective-permute-done.12 = bf16[64,2048]{1,0:T(8,128)(2,1)S(1)} collective-permute-done((bf16[64,2048]{1,0:T(8,128)(2,1)S(1)}, bf16[64,2048]{1,0:T(8,128)(2,1)S(1)}, u32[]{:S(2)}, u32[]{:S(2)}) %collective-permute-start.12) | collective-permute-done | bytes 262176 | tf_op jit(solution)/shard_map/ppermute | solution.py:442
  176.5 0.8 fusion.9
  (38 shorter events, 0.2 us)
Async XLA Ops:
  0.6 16.2 %copy-start.12 = (f32[64,8]{0,1:T(8,128)S(1)}, f32[64,8]{0,1:T(8,128)}, u32[]{:S(2)}) copy-start(f32[64,8]{0,1:T(8,128)} %param.24) | copy-start | bytes 6148
  0.6 16.3 %copy-start.11 = (s32[64,8]{0,1:T(8,128)S(1)}, s32[64,8]{0,1:T(8,128)}, u32[]{:S(2)}) copy-start(s32[64,8]{0,1:T(8,128)} %param.23) | copy-start | bytes 6148
  0.6 16.6 %copy-start.1 = (bf16[256,2048]{1,0:T(8,128)(2,1)S(1)}, bf16[256,2048]{1,0:T(8,128)(2,1)}, u32[]{:S(2)}) copy-start(bf16[256,2048]{1,0:T(8,128)(2,1)} %refs_0_.1) | copy-start | bytes 3145732
  1.4 16.7 %copy-start.3 = (f32[256,128]{1,0:T(8,128)S(1)}, f32[256,128]{1,0:T(8,128)}, u32[]{:S(2)}) copy-start(f32[256,128]{1,0:T(8,128)} %get-tuple-element.36.cos_ref.refs_5_) | copy-start | bytes 393220
  1.4 16.7 %copy-start.4 = (f32[256,128]{1,0:T(8,128)S(1)}, f32[256,128]{1,0:T(8,128)}, u32[]{:S(2)}) copy-start(f32[256,128]{1,0:T(8,128)} %get-tuple-element.37.sin_ref.refs_6_) | copy-start | bytes 393220
  1.4 16.7 %copy-start.6 = (f32[2048]{0:T(1024)S(1)}, f32[2048]{0:T(1024)}, u32[]{:S(2)}) copy-start(f32[2048]{0:T(1024)} %param.15) | copy-start | bytes 24580
  1.4 16.7 %copy-start.7 = (f32[128]{0:T(128)S(1)}, f32[128]{0:T(128)}, u32[]{:S(2)}) copy-start(f32[128]{0:T(128)} %param.19) | copy-start | bytes 1540
  4.9 21.2 %collective-permute-start.6 = (bf16[512,128]{1,0:T(8,128)(2,1)}, bf16[512,128]{1,0:T(8,128)(2,1)S(1)}, u32[]{:S(2)}, u32[]{:S(2)}) collective-permute-start(bf16[512,128]{1,0:T(8,128)(2,1)} %norm_kv.1.rest_0_), channel_id=1, source_target_pairs={{0,4},{1,5},{2,6},{3,7},{4,0},{5,1},{6,2},{7,3},{8,12},{9,13},{10,... | collective-permute-start | bytes 393224 | tf_op jit(solution)/shard_map/ppermute | solution.py:299
  8.0 14.7 %collective-permute-start.4 = (bf16[512,128]{1,0:T(8,128)(2,1)}, bf16[512,128]{1,0:T(8,128)(2,1)S(1)}, u32[]{:S(2)}, u32[]{:S(2)}) collective-permute-start(bf16[512,128]{1,0:T(8,128)(2,1)} %norm_kv.1.rest_0_), channel_id=1, source_target_pairs={{0,8},{1,9},{2,10},{3,11},{4,12},{5,13},{6,14},{7,15},{8,16},{9,17... | collective-permute-start | bytes 393224 | tf_op jit(solution)/shard_map/ppermute | solution.py:294
  11.4 11.7 %collective-permute-start.2 = (bf16[512,128]{1,0:T(8,128)(2,1)}, bf16[512,128]{1,0:T(8,128)(2,1)S(1)}, u32[]{:S(2)}, u32[]{:S(2)}) collective-permute-start(bf16[512,128]{1,0:T(8,128)(2,1)} %norm_kv.1.rest_0_), channel_id=1, source_target_pairs={{0,24},{1,25},{2,26},{3,27},{4,28},{5,29},{6,30},{7,31}} | collective-permute-start | bytes 393224 | tf_op jit(solution)/shard_map/ppermute | solution.py:294
  14.8 9.9 %collective-permute-start = (bf16[512,128]{1,0:T(8,128)(2,1)}, bf16[512,128]{1,0:T(8,128)(2,1)S(1)}, u32[]{:S(2)}, u32[]{:S(2)}) collective-permute-start(bf16[512,128]{1,0:T(8,128)(2,1)} %norm_kv.1.rest_0_), channel_id=1, source_target_pairs={{0,16},{1,17},{2,18},{3,19},{4,20},{5,21},{6,22},{7,23},{8,24},{9,... | collective-permute-start | bytes 393224 | tf_op jit(solution)/shard_map/ppermute | solution.py:294
  16.9 5.5 %collective-permute-start.10 = (f32[64,16]{0,1:T(8,128)S(1)}, f32[64,16]{0,1:T(8,128)S(1)}, u32[]{:S(2)}, u32[]{:S(2)}) collective-permute-start(f32[64,16]{0,1:T(8,128)S(1)} %pad_maximum_fusion.2), channel_id=1, source_target_pairs={{0,24},{1,25},{2,26},{3,27},{4,28},{5,29},{6,30},{7,31},{8,16},{9,... | collective-permute-start | bytes 12296 | tf_op jit(solution)/shard_map/ppermute | solution.py:318
  18.1 2.2 %copy-start.2 = (bf16[2048,1024]{1,0:T(8,128)(2,1)S(1)}, bf16[2048,1024]{1,0:T(8,128)(2,1)}, u32[]{:S(2)}) copy-start(bf16[2048,1024]{1,0:T(8,128)(2,1)} %wq_ref.1) | copy-start | bytes 12582916
  20.3 5.8 %copy-start.5 = (bf16[512,128]{1,0:T(8,128)(2,1)S(1)}, bf16[512,128]{1,0:T(8,128)(2,1)}, u32[]{:S(2)}) copy-start(bf16[512,128]{1,0:T(8,128)(2,1)} %norm_kv.1.rest_0_) | copy-start | bytes 393220
  22.6 6.4 %collective-permute-start.5 = (bf16[512,128]{1,0:T(8,128)(2,1)S(1)}, bf16[512,128]{1,0:T(8,128)(2,1)S(1)}, u32[]{:S(2)}, u32[]{:S(2)}) collective-permute-start(bf16[512,128]{1,0:T(8,128)(2,1)S(1)} %collective-permute-done.4.rest_1_), channel_id=1, source_target_pairs={{0,4},{1,5},{2,6},{3,7},{4,0},{5,1},{6,2},{7,3},{8,12},{9,13},{10,... | collective-permute-start | bytes 393224 | tf_op jit(solution)/shard_map/ppermute | solution.py:299
  23.2 8.9 %collective-permute-start.3 = (bf16[512,128]{1,0:T(8,128)(2,1)S(1)}, bf16[512,128]{1,0:T(8,128)(2,1)S(1)}, u32[]{:S(2)}, u32[]{:S(2)}) collective-permute-start(bf16[512,128]{1,0:T(8,128)(2,1)S(1)} %collective-permute-done.2.rest_1_), channel_id=1, source_target_pairs={{0,4},{1,5},{2,6},{3,7},{4,0},{5,1},{6,2},{7,3},{8,12},{9,13},{10,... | collective-permute-start | bytes 393224 | tf_op jit(solution)/shard_map/ppermute | solution.py:299
  24.7 7.7 %collective-permute-start.1 = (bf16[512,128]{1,0:T(8,128)(2,1)S(1)}, bf16[512,128]{1,0:T(8,128)(2,1)S(1)}, u32[]{:S(2)}, u32[]{:S(2)}) collective-permute-start(bf16[512,128]{1,0:T(8,128)(2,1)S(1)} %collective-permute-done.rest_0_), channel_id=1, source_target_pairs={{0,4},{1,5},{2,6},{3,7},{4,0},{5,1},{6,2},{7,3},{8,12},{9,13},{10,... | collective-permute-start | bytes 393224 | tf_op jit(solution)/shard_map/ppermute | solution.py:299
  29.0 5.9 %copy-start.8 = (bf16[1024,2048]{1,0:T(8,128)(2,1)S(1)}, bf16[1024,2048]{1,0:T(8,128)(2,1)}, u32[]{:S(2)}) copy-start(bf16[1024,2048]{1,0:T(8,128)(2,1)} %param.21) | copy-start | bytes 12582916
  35.7 1.6 collective-permute-start.7
  36.6 2.4 %collective-permute-start.9 = (bf16[64,2048]{1,0:T(8,128)(2,1)S(1)}, bf16[64,2048]{1,0:T(8,128)(2,1)S(1)}, u32[]{:S(2)}, u32[]{:S(2)}) collective-permute-start(bf16[64,2048]{1,0:T(8,128)(2,1)S(1)} %fusion.12), channel_id=1, source_target_pairs={{0,1},{1,0},{2,3},{3,2},{4,5},{5,4},{6,7},{7,6},{8,9},{9,8},{10,11... | collective-permute-start | bytes 786440 | tf_op jit(solution)/shard_map/ppermute | solution.py:383
  37.4 8.4 %collective-permute-start.8 = (bf16[64,2048]{1,0:T(8,128)(2,1)S(1)}, bf16[64,2048]{1,0:T(8,128)(2,1)S(1)}, u32[]{:S(2)}, u32[]{:S(2)}) collective-permute-start(bf16[64,2048]{1,0:T(8,128)(2,1)S(1)} %fusion.10), channel_id=1, source_target_pairs={{0,2},{1,3},{2,0},{3,1},{4,6},{5,7},{6,4},{7,5},{8,10},{9,11},{10,... | collective-permute-start | bytes 786440 | tf_op jit(solution)/shard_map/ppermute | solution.py:389
  45.8 0.7 copy-start.10
  49.6 9.6 %collective-permute-start.11 = (bf16[64,2048]{1,0:T(8,128)(2,1)}, bf16[64,2048]{1,0:T(8,128)(2,1)S(1)}, u32[]{:S(2)}, u32[]{:S(2)}) collective-permute-start(bf16[64,2048]{1,0:T(8,128)(2,1)} %get-tuple-element.18), channel_id=1, source_target_pairs={{0,24},{1,25},{2,26},{3,27},{4,28},{5,29},{6,30},{7,31},{8,16},{9,... | collective-permute-start | bytes 786440 | tf_op jit(solution)/shard_map/ppermute | solution.py:434
  90.7 4.9 %copy-start = (bf16[1,2048,768]{2,1,0:T(8,128)(2,1)S(1)}, bf16[1,2048,768]{2,1,0:T(8,128)(2,1)}, u32[]{:S(2)}) copy-start(bf16[1,2048,768]{2,1,0:T(8,128)(2,1)} %param.25) | copy-start | bytes 9437188
  90.7 27.5 %all-to-all-start = ((bf16[16,24,2048]{2,1,0:T(8,128)(2,1)}), bf16[16,24,2048]{2,1,0:T(8,128)(2,1)}, u32[]{:S(2)}, u32[]{:S(2)}) async-start(bf16[16,24,2048]{2,1,0:T(8,128)(2,1)} %bitcast.97), calls=%async_computation | async-start | bytes 3145728 | tf_op jit(solution)/shard_map/all_to_all | solution.py:408
  118.1 27.2 %all-to-all-start.3 = ((bf16[16,24,2048]{2,1,0:T(8,128)(2,1)}), bf16[16,24,2048]{2,1,0:T(8,128)(2,1)}, u32[]{:S(2)}, u32[]{:S(2)}) async-start(bf16[16,24,2048]{2,1,0:T(8,128)(2,1)} %bitcast.93), calls=%async_computation.3 | async-start | bytes 3145728 | tf_op jit(solution)/shard_map/all_to_all | solution.py:408
  145.3 26.5 %all-to-all-start.1 = ((bf16[16,24,2048]{2,1,0:T(8,128)(2,1)}), bf16[16,24,2048]{2,1,0:T(8,128)(2,1)S(1)}, u32[]{:S(2)}, u32[]{:S(2)}) async-start(bf16[16,24,2048]{2,1,0:T(8,128)(2,1)} %bitcast.92), calls=%async_computation.1 | async-start | bytes 3145728 | tf_op jit(solution)/shard_map/all_to_all | solution.py:408
  151.4 25.1 %copy-start.9 = (f32[64,2048]{1,0:T(8,128)S(1)}, f32[64,2048]{1,0:T(8,128)}, u32[]{:S(2)}) copy-start(f32[64,2048]{1,0:T(8,128)} %get-tuple-element.16) | copy-start | bytes 1572868
  151.4 25.0 %collective-permute-start.12 = (bf16[64,2048]{1,0:T(8,128)(2,1)S(1)}, bf16[64,2048]{1,0:T(8,128)(2,1)S(1)}, u32[]{:S(2)}, u32[]{:S(2)}) collective-permute-start(bf16[64,2048]{1,0:T(8,128)(2,1)S(1)} %fusion.6), channel_id=1, source_target_pairs={{0,24},{1,25},{2,26},{3,27},{4,28},{5,29},{6,30},{7,31},{8,16},{9,... | collective-permute-start | bytes 786440 | tf_op jit(solution)/shard_map/ppermute | solution.py:442

commit v4 on v3

--- a/solution.py
+++ b/solution.py
@@ -35,12 +35,20 @@
     hbm, (kv_ref,), held, sems = refs[:7], refs[7:8], refs[8:15], refs[15]
     x_ref, wk_ref, wv_ref, gain_ref, kgain_ref, cos_ref, sin_ref = held
     rows, head_dim = x_ref.shape[0], wk_ref.shape[1]
+    half = rows // 2
+    upper, lower = pl.ds(0, half), pl.ds(half, half)
     copies = [pltpu.make_async_copy(a, b, sems.at[i]) for i, (a, b) in enumerate(zip(hbm, held))]
-    for i in (0, 3, 1, 4, 5, 6, 2):
+    copies[0] = pltpu.make_async_copy(hbm[0].at[upper], x_ref.at[upper], sems.at[0])
+    copies.append(pltpu.make_async_copy(hbm[0].at[lower], x_ref.at[lower], sems.at[7]))
+    for i in (3, 0, 7, 1, 4, 5, 6, 2):
         copies[i].start()
-    copies[0].wait()
     copies[3].wait()
-    normed = rms_scale(x_ref[...].astype(jnp.float32), gain_ref[...]).astype(jnp.bfloat16)
+    normed = []
+    for i in (0, 7):
+        copies[i].wait()
+        part = x_ref[upper if i == 0 else lower, :].astype(jnp.float32)
+        normed.append(rms_scale(part, gain_ref[...]).astype(jnp.bfloat16))
+    normed = jnp.concatenate(normed, axis=0)
     for i in (1, 4, 5, 6):
         copies[i].wait()
     keys = jnp.dot(normed, wk_ref[...], preferred_element_type=jnp.float32)
@@ -184,11 +192,10 @@
         copy.wait()
 
 
-def run_experts(grouped, w_gate, w_up, w_down):
+def run_experts(grouped, gates, w_up, w_down):
     experts, rows, width = grouped.shape
-    ff = w_gate.shape[2]
+    ff = w_up.shape[2]
     held = ((rows, width), (width, ff), (ff, width), (rows, ff), (rows, width))
-    gates = [pltpu.with_memory_space_constraint(w_gate[e], pltpu.VMEM) for e in range(experts)]
     made = [
         pl.pallas_call(
             expert_kernel,
@@ -198,22 +205,18 @@
             scratch_shapes=[pltpu.VMEM(shape, jnp.bfloat16) for shape in held]
             + [pltpu.SemaphoreType.DMA((5,))],
             name="experts",
-        )(grouped[e], gates[e], w_up[e], w_down[e])
+        )(
+            pltpu.with_memory_space_constraint(grouped[e], pltpu.HBM), gates[e], w_up[e], w_down[e]
+        )
         for e in range(experts)
     ]
     return made[0][None] if experts == 1 else jnp.stack(made)
 
 
-def route_kernel(*refs):
-    parts, (rows_ref, gain_ref, pick_ref, residual_ref, routed_ref, out_ref) = refs[:-6], refs[-6:]
-    residual = rows_ref[...].astype(jnp.float32)
-    for ref in parts:
-        residual = residual + ref[...].astype(jnp.float32)
-    residual_ref[...] = residual
-    routed = rms_scale(residual, gain_ref[...]).astype(jnp.bfloat16)
-    routed_ref[...] = routed
-    out_ref[...] = jnp.dot(
-        pick_ref[...], routed, preferred_element_type=jnp.float32
+def fill_kernel(rows_ref, pick_ref, gate_ref, out_ref):
+    del gate_ref
+    out_ref[...] = lax.dot_general(
+        pick_ref[...], rows_ref[...], (((0,), (0,)), ((), ())), preferred_element_type=jnp.float32
     ).astype(jnp.bfloat16)
 
 
@@ -282,7 +285,7 @@
         in_specs=[ANY] * len(first_in),
         out_specs=VMEM,
         scratch_shapes=[pltpu.VMEM(x.shape, x.dtype) for x in first_in]
-        + [pltpu.SemaphoreType.DMA((len(first_in),))],
+        + [pltpu.SemaphoreType.DMA((len(first_in) + 1,))],
         name="norm_kv",
     )(*first_in)
 
@@ -312,14 +315,9 @@
     first_expert = (seq_index // (seq_count // halves)) * experts_half
     mirror = make_pairs(lambda s, h: ((line - 1 - s // side) * side + s % side, h))
     mixing = route_weights / jnp.sum(route_weights, axis=1, keepdims=True)
-    routes = [(expert_ids, mixing)]
-    if halves == 2:
-        sent = jnp.concatenate([expert_ids.astype(jnp.float32), mixing], axis=1)
-        seen = lax.ppermute(sent, BOTH, mirror)
-        routes.append((seen[:, :top_count].astype(jnp.int32), seen[:, top_count:]))
-
-    def slot_tables(ids, weights):
-        here = first_expert + jnp.arange(experts_half, dtype=jnp.int32)
+
+    def slot_tables(ids, weights, zero):
+        here = first_expert + zero + jnp.arange(experts_half, dtype=jnp.int32)
         named = ids[:, :, None] == here[None, None, :]
         counts = jnp.sum(named, axis=1).astype(jnp.bfloat16)
         earlier = (
@@ -328,12 +326,13 @@
         rank_table = jnp.dot(earlier, counts, preferred_element_type=jnp.float32)
         mix_table = jnp.sum(jnp.where(named, weights[:, :, None], 0.0), axis=1)
         place = jnp.where(counts > 0, rank_table, -1.0).astype(jnp.int32)
-        in_slot = place[:, :, None] == jnp.arange(capacity, dtype=jnp.int32)[None, None, :]
-        pick = in_slot.astype(jnp.bfloat16).reshape(rows_here, slots).T
+        in_slot = place[:, :, None] == (zero + jnp.arange(capacity, dtype=jnp.int32))[None, None, :]
+        pick = in_slot.astype(jnp.bfloat16).reshape(rows_here, slots)
         mix = jnp.where(in_slot, mix_table[:, :, None], 0.0).reshape(rows_here, slots)
         return pick, jnp.concatenate(split_exact(mix), axis=0)
 
-    tables = [slot_tables(*route) for route in routes]
+    tables = [slot_tables(expert_ids, mixing, jnp.int32(0))]
+
     query_step = 2 * head_dim if heads_here % 2 == 0 else head_dim
     rot_q = pl.pallas_call(
         functools.partial(query_kernel, head_dim, query_step),
@@ -348,8 +347,9 @@
     if side == 2:
         parts = [
             [*range(near), *range(line, line + near - 1)],
-            [*range(near, line), *range(line + near - 1, line + near)],
-            [*range(line + near, 2 * line)],
+            [*range(near, line - 1), *range(line + near - 1, line + near)],
+            [line - 1, *range(line + near, 2 * line - 1)],
+            [2 * line - 1],
         ]
     else:
         parts = [[*range(near)], [*range(near, line)]]
@@ -383,24 +383,18 @@
         came = lax.ppermute(give.astype(jnp.bfloat16), BOTH, core_swap)
         return keep + came.astype(jnp.float32)
 
-    summed = []
+    attn_part = None
     for k in range(1, towers):
         shift = make_pairs(lambda s, h, k=k: (s, (h + k * cores) % head_count))
-        summed.append(lax.ppermute(tower_sum(k).astype(jnp.bfloat16), BOTH, shift))
-    summed.append(tower_sum(0))
+        given = tower_sum(k).astype(jnp.bfloat16)
+        came = lax.ppermute(given, BOTH, shift).astype(jnp.float32)
+        attn_part = came if attn_part is None else attn_part + came
+    own_sum = tower_sum(0)
+    attn_part = own_sum if attn_part is None else own_sum + attn_part
 
     own_rows = lax.dynamic_slice_in_dim(tokens, head_index * rows_here, rows_here, 0)
-    residual, routed, outgoing = pl.pallas_call(
-        route_kernel,
-        out_shape=(
-            jax.ShapeDtypeStruct((rows_here, width), jnp.float32),
-            jax.ShapeDtypeStruct((rows_here, width), jnp.bfloat16),
-            jax.ShapeDtypeStruct((slots, width), jnp.bfloat16),
-        ),
-        in_specs=[VMEM] * (len(summed) + 3),
-        out_specs=(VMEM,) * 3,
-        name="route",
-    )(*summed, own_rows, post_gain[None], tables[0][0])
+    residual = own_rows.astype(jnp.float32) + attn_part
+    routed = rms_scale(residual, post_gain).astype(jnp.bfloat16)
 
     groups = [list(range(g * members, (g + 1) * members)) for g in range(halves)]
 
@@ -422,6 +416,11 @@
             .reshape(local_count, members * capacity, width)
         )
 
+    def fill_slots(rows, pick):
+        return lax.dot_general(
+            pick, rows, (((0,), (0,)), ((), ())), preferred_element_type=jnp.float32
+        ).astype(jnp.bfloat16)
+
     def give_back(result, mix):
         came = exchange(
             result.reshape(local_count, members, capacity, width).transpose(1, 0, 2, 3)
@@ -429,13 +428,38 @@
         both = jnp.dot(mix, came, preferred_element_type=jnp.float32)
         return both[:rows_here] + both[rows_here:]
 
-    weights = (w_gate, w_up, w_down)
+    gates = [pltpu.with_memory_space_constraint(w_gate[e], pltpu.VMEM) for e in range(local_count)]
+    weights = (gates, w_up, w_down)
     if halves == 2:
-        mirrored = lax.ppermute(routed, BOTH, mirror)
-        own_rows_in = dispatch(outgoing)
-        far_rows_in = dispatch(
-            jnp.dot(tables[1][0], mirrored, preferred_element_type=jnp.float32).astype(jnp.bfloat16)
-        )
+        spare = -3 * top_count % head_dim
+        sent = jnp.concatenate(
+            [
+                routed,
+                expert_ids.astype(jnp.bfloat16),
+                *split_exact(mixing),
+                jnp.zeros((rows_here, spare), jnp.bfloat16),
+            ],
+            axis=1,
+        )
+        came = lax.ppermute(sent, BOTH, mirror)
+        own_rows_in = dispatch(fill_slots(routed, tables[0][0]))
+        mirrored, beside = came[:, :width], came[:, width:].astype(jnp.float32)
+        tables.append(
+            slot_tables(
+                beside[:, :top_count].astype(jnp.int32),
+                beside[:, top_count : 2 * top_count]
+                + beside[:, 2 * top_count : 3 * top_count],
+                lax.optimization_barrier(jnp.int32(0)),
+            )
+        )
+        filled = pl.pallas_call(
+            fill_kernel,
+            out_shape=jax.ShapeDtypeStruct((slots, width), jnp.bfloat16),
+            in_specs=[VMEM] * 3,
+            out_specs=VMEM,
+            name="fill",
+        )(mirrored, tables[1][0], gates[0])
+        far_rows_in = dispatch(filled)
         own_result = run_experts(own_rows_in, *weights)
         far_result = run_experts(far_rows_in, *weights)
         foreign = give_back(far_result, tables[1][1]).astype(jnp.bfloat16)
@@ -443,7 +467,7 @@
         expert_sum = give_back(own_result, tables[0][1])
         expert_sum = expert_sum + far_sum.astype(jnp.float32)
     else:
-        result = run_experts(dispatch(outgoing), *weights)
+        result = run_experts(dispatch(fill_slots(routed, tables[0][0])), *weights)
         expert_sum = give_back(result, tables[0][1])
     return (residual + expert_sum).astype(jnp.bfloat16)
 

time: 178 us -> 189 us (1.062)
  blocking collectives: 30.9 us -> 0 us
  waiting for transfers between devices: 64.4 us -> 78.2 us
  local copies, waits for them, and re-layouts: 3.86 us -> 16.4 us
  starting transfers between devices: 36.9 us -> 47.2 us
  other arithmetic: 4.61 us -> 8.53 us
    all_to_all x1 -> x0, blocking collectives: 30.9 us -> none  [exchange(): lax.all_to_all(rows.reshape(members, local_count * capacity, width), BOTH...]
    all_to_all x3 -> x4, waiting for transfers between devices: 47.3 us -> 62.5 us  [exchange(): lax.all_to_all(rows.reshape(members, local_count * capacity, width), BOTH...]
    all_to_all x3 -> x4, starting transfers between devices: 13 us -> 20.9 us  [exchange(): lax.all_to_all(rows.reshape(members, local_count * capacity, width), BOTH...]
    eq x2 -> x8, local copies, waits for them, and re-layouts: 0.09 us -> 5.54 us  [slot_tables(): place[:, :, None]]
    broadcast_in_dim x0 -> x5, local copies, waits for them, and re-layouts: none -> 4.11 us  [the longest x4 4.11 us: slot_tables(): jnp.where(in_slot, mix_table[:, :, None], 0.0).reshape(rows_here, slots)]
    convert_element_type x1 -> x2, other arithmetic: 0.12 us -> 3.11 us  [split_exact(): high = values.astype(jnp.bfloat16)]
    ppermute x3 -> x2, starting transfers between devices: 5.15 us -> 7.75 us  [the longest x1 6.17 us: body(): came = lax.ppermute(sent, BOTH, mirror)]
    ppermute x3, starting transfers between devices: 8.82 us -> 10.8 us  [body(): kv_blocks.append(lax.ppermute(own_kv, BOTH, up))]
  transfers between devices with their start and end apart: 16 -> 16, of which waited for: 10 -> 9; matrix products, arithmetic and copies ran while one was open for 4% -> 8% of each run, Pallas kernels for 13% -> 13%
where the time goes in v4:
time: 189 us; the launch traced here: 188 us
  waiting for transfers between devices  78.2 us (41%)
  starting transfers between devices  47.2 us (25%)
  Pallas kernels  31.8 us (17%)
  local copies, waits for them, and re-layouts  16.4 us (9%)
  other arithmetic  8.53 us (5%)
  matrix products  5.8 us (3%)
    all_to_all x4, waiting for transfers between devices, exchange(): lax.all_to_all(rows.reshape(members, local_count * capacity, width), BOTH...  62.5 us
    all_to_all x4, starting transfers between devices, exchange(): lax.all_to_all(rows.reshape(members, local_count * capacity, width), BOTH...  20.9 us
    pallas_call x2, Pallas kernels, run_experts(): pl.pallas_call(expert_kernel, out_shape=jax.ShapeDtypeStruct((rows, width...  14.7 us
    ppermute x3, starting transfers between devices, body(): kv_blocks.append(lax.ppermute(own_kv, BOTH, up))  10.8 us
    pallas_call x4, Pallas kernels, attend(): pl.pallas_call(functools.partial(attend_kernel, head_dim, blocks, not sta...  9.26 us
    ppermute x1, waiting for transfers between devices, body(): came = lax.ppermute(sent, BOTH, mirror)  6.4 us
    ppermute x1, starting transfers between devices, body(): came = lax.ppermute(sent, BOTH, mirror)  6.17 us
    ppermute x1, waiting for transfers between devices, body(): came = lax.ppermute(given, BOTH, shift).astype(jnp.float32)  5.92 us
  transfers between devices with their start and end apart: 16, of which 9 were waited for; matrix products, arithmetic and copies ran while one was open for 8% of the time, Pallas kernels for 13%

profile of v4, /device:TPU:0, one launch (start us, length us, event | category | flops | bytes accessed | tf_op | source)
XLA Modules:
  0.0 188.4 jit_solution(15912514646451683579)
XLA Ops:
  0.0 0.5 fusion.27
  0.6 0.8 pad_maximum_fusion
  1.4 3.3 %norm_kv.1.rest_0_ = bf16[512,128]{1,0:T(8,128)(2,1)} custom-call(bf16[256,2048]{1,0:T(8,128)(2,1)} %refs_0_.1, bf16[2048,128]{1,0:T(8,128)(2,1)} %refs_1_.1, bf16[2048,128]{1,0:T(8,128)(2,1)} %refs_2_.1, f32[1,2048]{1,0:T(1,128)} %bitcast.55, f32[1,128]{1,0:T(1,128)} %bitcast.73, f32[256,128]{1,0:T(8,128)} %get-tuple-element.33.cos_ref.refs_5_, ...), custom_call_target="tpu_custom_call" | custom-call | tf_op jit(solution)/shard_map/norm_kv/pallas_call | solution.py:282
  4.8 5.0 %collective-permute-start.4 = (bf16[512,128]{1,0:T(8,128)(2,1)}, bf16[512,128]{1,0:T(8,128)(2,1)S(1)}, u32[]{:S(2)}, u32[]{:S(2)}) collective-permute-start(bf16[512,128]{1,0:T(8,128)(2,1)} %norm_kv.1.rest_0_), channel_id=1, source_target_pairs={{0,8},{1,9},{2,10},{3,11},{4,12},{5,13},{6,14},{7,15},{8,16},{9,17... | collective-permute-start | bytes 393224 | tf_op jit(solution)/shard_map/ppermute | solution.py:297
  9.7 4.5 %collective-permute-start.2 = (bf16[512,128]{1,0:T(8,128)(2,1)}, bf16[512,128]{1,0:T(8,128)(2,1)S(1)}, u32[]{:S(2)}, u32[]{:S(2)}) collective-permute-start(bf16[512,128]{1,0:T(8,128)(2,1)} %norm_kv.1.rest_0_), channel_id=1, source_target_pairs={{0,16},{1,17},{2,18},{3,19},{4,20},{5,21},{6,22},{7,23},{8,24},{9,... | collective-permute-start | bytes 393224 | tf_op jit(solution)/shard_map/ppermute | solution.py:297
  14.3 1.3 collective-permute-start
  15.6 1.6 collective-permute-start.6
  17.2 0.5 collective-permute-start.5
  17.7 0.7 collective-permute-done.2.rest_0_
  18.4 1.5 collective-permute-start.3
  19.9 1.4 collective-permute-start.1
  21.5 2.2 %copy-done.2 = bf16[2048,1024]{1,0:T(8,128)(2,1)S(1)} copy-done((bf16[2048,1024]{1,0:T(8,128)(2,1)S(1)}, bf16[2048,1024]{1,0:T(8,128)(2,1)}, u32[]{:S(2)}) %copy-start.2) | copy-done | bytes 4194328
  23.7 1.8 queries.1.q_ref
  25.6 2.8 %attend.4 = (f32[8,8,256]{2,1,0:T(8,128)S(1)}, f32[8,128,256]{2,1,0:T(8,128)S(1)}) custom-call(f32[3]{0:T(128)S(1)} %pad_maximum_fusion.4.bias_ref, bf16[256,1024]{1,0:T(8,128)(2,1)S(1)} %queries.1.q_ref, bf16[512,128]{1,0:T(8,128)(2,1)S(1)} %copy-done.5, bf16[512,128]{1,0:T(8,128)(2,1)S(1)} %collective-permute-done.4.rest_1_, ...), custom_call_target="tpu_custom_call" | custom-call | tf_op jit(solution)/shard_map/attend/pallas_call | solution.py:146
  28.4 2.4 %attend.5 = (f32[8,8,256]{2,1,0:T(8,128)S(1)}, f32[8,128,256]{2,1,0:T(8,128)S(1)}) custom-call(f32[2]{0:T(128)S(1)} %pad_maximum_fusion.3.bias_ref, bf16[256,1024]{1,0:T(8,128)(2,1)S(1)} %queries.1.q_ref, bf16[512,128]{1,0:T(8,128)(2,1)S(1)} %collective-permute-done.2.rest_0_, bf16[512,128]{1,0:T(8,128)(2,1)S(1)} %collective-permute-done.5.rest_1_, ...), custom_call_target="tpu_custom_call" | custom-call | tf_op jit(solution)/shard_map/attend/pallas_call | solution.py:146
  30.9 2.4 %attend.6 = (f32[8,8,256]{2,1,0:T(8,128)S(1)}, f32[8,128,256]{2,1,0:T(8,128)S(1)}) custom-call(f32[2]{0:T(128)S(1)} %pad_maximum_fusion.2.bias_ref, bf16[256,1024]{1,0:T(8,128)(2,1)S(1)} %queries.1.q_ref, bf16[512,128]{1,0:T(8,128)(2,1)S(1)} %collective-permute-done.rest_0_, bf16[512,128]{1,0:T(8,128)(2,1)S(1)} %collective-permute-done.3.rest_1_, ...), custom_call_target="tpu_custom_call" | custom-call | tf_op jit(solution)/shard_map/attend/pallas_call | solution.py:146
  33.4 1.5 attend.7
  35.0 0.7 fusion
  35.8 0.7 fusion.2
  36.7 0.6 collective-permute-start.7
  37.2 0.1 collective-permute-done.8
  37.4 1.6 collective-permute-start.9
  39.2 0.7 subtract_convert_fusion.2
  39.9 5.9 %collective-permute-done.9 = bf16[64,2048]{1,0:T(8,128)(2,1)S(1)} collective-permute-done((bf16[64,2048]{1,0:T(8,128)(2,1)S(1)}, bf16[64,2048]{1,0:T(8,128)(2,1)S(1)}, u32[]{:S(2)}, u32[]{:S(2)}) %collective-permute-start.9) | collective-permute-done | bytes 262176 | tf_op jit(solution)/shard_map/ppermute | solution.py:390
  45.8 0.2 multiply_reduce_fusion
  46.1 0.8 copy-done.9
  46.9 0.1 multiply_convert_fusion
  47.0 0.8 concatenate.18
  47.8 6.2 %collective-permute-start.10 = (bf16[64,2176]{1,0:T(8,128)(2,1)}, bf16[64,2176]{1,0:T(8,128)(2,1)}, u32[]{:S(2)}, u32[]{:S(2)}) collective-permute-start(bf16[64,2176]{1,0:T(8,128)(2,1)} %concatenate.18), channel_id=1, source_target_pairs={{0,24},{1,25},{2,26},{3,27},{4,28},{5,29},{6,30},{7,31},{8,16},{9,... | collective-permute-start | bytes 835592 | tf_op jit(solution)/shard_map/ppermute | solution.py:444
  54.1 6.4 %collective-permute-done.10 = bf16[64,2176]{1,0:T(8,128)(2,1)} collective-permute-done((bf16[64,2176]{1,0:T(8,128)(2,1)}, bf16[64,2176]{1,0:T(8,128)(2,1)}, u32[]{:S(2)}, u32[]{:S(2)}) %collective-permute-start.10) | collective-permute-done | bytes 278560 | tf_op jit(solution)/shard_map/ppermute | solution.py:444
  60.5 0.7 slice_convert_fusion.1
  61.7 0.7 broadcast_in_dim.90
  62.3 1.0 copy.45
  63.4 0.1 fusion.4
  63.5 0.7 eq.89
  64.2 1.7 copy.43
  65.9 1.5 select_convert_fusion
  67.4 0.6 convert_element_type.140.pick_ref
  68.1 1.7 slice.42.rows_ref
  69.7 2.7 %fill.1 = bf16[384,2048]{1,0:T(8,128)(2,1)} custom-call(bf16[64,2048]{1,0:T(8,128)(2,1)} %slice.42.rows_ref, bf16[64,384]{1,0:T(8,128)(2,1)} %convert_element_type.140.pick_ref, bf16[2048,768]{1,0:T(8,128)(2,1)S(1)} %bitcast.51), custom_call_target="tpu_custom_call" | custom-call | tf_op jit(solution)/shard_map/fill/pallas_call | solution.py:455
  72.4 8.2 %all-to-all-start.2 = ((bf16[16,24,2048]{2,1,0:T(8,128)(2,1)}), bf16[16,24,2048]{2,1,0:T(8,128)(2,1)}, u32[]{:S(2)}, u32[]{:S(2)}) async-start(bf16[16,24,2048]{2,1,0:T(8,128)(2,1)} %bitcast.62), calls=%async_computation.2 | async-start | bytes 3145728 | tf_op jit(solution)/shard_map/all_to_all | solution.py:402
  80.6 0.8 copy.39
  81.5 0.7 broadcast_in_dim.85
  82.2 1.7 copy.40
  84.0 0.1 fusion.5
  84.1 0.7 eq.80
  84.8 1.7 copy.36
  86.5 0.7 eq.83
  87.2 1.6 select_convert_fusion.1
  88.8 1.8 convolution_convert_fusion
  90.6 12.8 %all-to-all-done.2 = bf16[16,24,2048]{2,1,0:T(8,128)(2,1)} async-done(((bf16[16,24,2048]{2,1,0:T(8,128)(2,1)}), bf16[16,24,2048]{2,1,0:T(8,128)(2,1)}, u32[]{:S(2)}, u32[]{:S(2)}) %all-to-all-start.2) | async-done | bytes 1572896 | tf_op jit(solution)/shard_map/all_to_all | solution.py:402
  103.4 4.4 %all-to-all-start = ((bf16[16,24,2048]{2,1,0:T(8,128)(2,1)}), bf16[16,24,2048]{2,1,0:T(8,128)(2,1)}, u32[]{:S(2)}, u32[]{:S(2)}) async-start(bf16[16,24,2048]{2,1,0:T(8,128)(2,1)} %bitcast.64), calls=%async_computation | async-start | bytes 3145728 | tf_op jit(solution)/shard_map/all_to_all | solution.py:402
  107.8 7.3 %experts.3 = bf16[384,2048]{1,0:T(8,128)(2,1)} custom-call(bf16[384,2048]{1,0:T(8,128)(2,1)} %bitcast.27.x_hbm, bf16[2048,768]{1,0:T(8,128)(2,1)S(1)} %bitcast.52, bf16[2048,768]{1,0:T(8,128)(2,1)} %bitcast.58, bf16[768,2048]{1,0:T(8,128)(2,1)} %bitcast.60), custom_call_target="tpu_custom_call" | custom-call | tf_op jit(solution)/shard_map/experts/pallas_call | solution.py:200
  115.2 15.5 %all-to-all-done = bf16[16,24,2048]{2,1,0:T(8,128)(2,1)} async-done(((bf16[16,24,2048]{2,1,0:T(8,128)(2,1)}), bf16[16,24,2048]{2,1,0:T(8,128)(2,1)}, u32[]{:S(2)}, u32[]{:S(2)}) %all-to-all-start) | async-done | bytes 1572896 | tf_op jit(solution)/shard_map/all_to_all | solution.py:402
  130.6 4.4 %all-to-all-start.3 = ((bf16[16,24,2048]{2,1,0:T(8,128)(2,1)}), bf16[16,24,2048]{2,1,0:T(8,128)(2,1)}, u32[]{:S(2)}, u32[]{:S(2)}) async-start(bf16[16,24,2048]{2,1,0:T(8,128)(2,1)} %bitcast.65), calls=%async_computation.3 | async-start | bytes 3145728 | tf_op jit(solution)/shard_map/all_to_all | solution.py:402
  135.1 7.3 %experts.2 = bf16[384,2048]{1,0:T(8,128)(2,1)} custom-call(bf16[384,2048]{1,0:T(8,128)(2,1)} %bitcast.18.x_hbm, bf16[2048,768]{1,0:T(8,128)(2,1)S(1)} %bitcast.53, bf16[2048,768]{1,0:T(8,128)(2,1)} %bitcast.59, bf16[768,2048]{1,0:T(8,128)(2,1)} %bitcast.61), custom_call_target="tpu_custom_call" | custom-call | tf_op jit(solution)/shard_map/experts/pallas_call | solution.py:200
  142.4 15.5 %all-to-all-done.3 = bf16[16,24,2048]{2,1,0:T(8,128)(2,1)} async-done(((bf16[16,24,2048]{2,1,0:T(8,128)(2,1)}), bf16[16,24,2048]{2,1,0:T(8,128)(2,1)}, u32[]{:S(2)}, u32[]{:S(2)}) %all-to-all-start.3) | async-done | bytes 1572896 | tf_op jit(solution)/shard_map/all_to_all | solution.py:402
  157.9 3.8 %all-to-all-start.1 = ((bf16[16,24,2048]{2,1,0:T(8,128)(2,1)}), bf16[16,24,2048]{2,1,0:T(8,128)(2,1)S(1)}, u32[]{:S(2)}, u32[]{:S(2)}) async-start(bf16[16,24,2048]{2,1,0:T(8,128)(2,1)} %bitcast.63), calls=%async_computation.1 | async-start | bytes 3145728 | tf_op jit(solution)/shard_map/all_to_all | solution.py:402
  161.8 1.9 fusion.19
  163.7 2.2 %collective-permute-start.11 = (bf16[64,2048]{1,0:T(8,128)(2,1)S(1)}, bf16[64,2048]{1,0:T(8,128)(2,1)S(1)}, u32[]{:S(2)}, u32[]{:S(2)}) collective-permute-start(bf16[64,2048]{1,0:T(8,128)(2,1)S(1)} %fusion.6), channel_id=1, source_target_pairs={{0,24},{1,25},{2,26},{3,27},{4,28},{5,29},{6,30},{7,31},{8,16},{9,... | collective-permute-start | bytes 786440 | tf_op jit(solution)/shard_map/ppermute | solution.py:466
  165.9 18.8 %all-to-all-done.1 = bf16[16,24,2048]{2,1,0:T(8,128)(2,1)S(1)} async-done(((bf16[16,24,2048]{2,1,0:T(8,128)(2,1)}), bf16[16,24,2048]{2,1,0:T(8,128)(2,1)S(1)}, u32[]{:S(2)}, u32[]{:S(2)}) %all-to-all-start.1) | async-done | bytes 1572896 | tf_op jit(solution)/shard_map/all_to_all | solution.py:402
  184.7 0.4 fusion.15
  185.2 2.4 %collective-permute-done.11 = bf16[64,2048]{1,0:T(8,128)(2,1)S(1)} collective-permute-done((bf16[64,2048]{1,0:T(8,128)(2,1)S(1)}, bf16[64,2048]{1,0:T(8,128)(2,1)S(1)}, u32[]{:S(2)}, u32[]{:S(2)}) %collective-permute-start.11) | collective-permute-done | bytes 262176 | tf_op jit(solution)/shard_map/ppermute | solution.py:466
  187.6 0.8 fusion.9
  (71 shorter events, 1.6 us)
Async XLA Ops:
  0.6 20.9 %copy-start.1 = (bf16[256,2048]{1,0:T(8,128)(2,1)S(1)}, bf16[256,2048]{1,0:T(8,128)(2,1)}, u32[]{:S(2)}) copy-start(bf16[256,2048]{1,0:T(8,128)(2,1)} %refs_0_.1) | copy-start | bytes 3145732
  0.6 20.9 %copy-start.6 = (f32[2048]{0:T(1024)S(1)}, f32[2048]{0:T(1024)}, u32[]{:S(2)}) copy-start(f32[2048]{0:T(1024)} %param.15) | copy-start | bytes 24580
  0.6 20.9 %copy-start.7 = (f32[128]{0:T(128)S(1)}, f32[128]{0:T(128)}, u32[]{:S(2)}) copy-start(f32[128]{0:T(128)} %param.19) | copy-start | bytes 1540
  1.4 20.0 %copy-start.3 = (f32[256,128]{1,0:T(8,128)S(1)}, f32[256,128]{1,0:T(8,128)}, u32[]{:S(2)}) copy-start(f32[256,128]{1,0:T(8,128)} %get-tuple-element.33.cos_ref.refs_5_) | copy-start | bytes 393220
  1.4 20.0 %copy-start.4 = (f32[256,128]{1,0:T(8,128)S(1)}, f32[256,128]{1,0:T(8,128)}, u32[]{:S(2)}) copy-start(f32[256,128]{1,0:T(8,128)} %get-tuple-element.34.sin_ref.refs_6_) | copy-start | bytes 393220
  4.8 12.4 %collective-permute-start.4 = (bf16[512,128]{1,0:T(8,128)(2,1)}, bf16[512,128]{1,0:T(8,128)(2,1)S(1)}, u32[]{:S(2)}, u32[]{:S(2)}) collective-permute-start(bf16[512,128]{1,0:T(8,128)(2,1)} %norm_kv.1.rest_0_), channel_id=1, source_target_pairs={{0,8},{1,9},{2,10},{3,11},{4,12},{5,13},{6,14},{7,15},{8,16},{9,17... | collective-permute-start | bytes 393224 | tf_op jit(solution)/shard_map/ppermute | solution.py:297
  9.7 8.7 %collective-permute-start.2 = (bf16[512,128]{1,0:T(8,128)(2,1)}, bf16[512,128]{1,0:T(8,128)(2,1)S(1)}, u32[]{:S(2)}, u32[]{:S(2)}) collective-permute-start(bf16[512,128]{1,0:T(8,128)(2,1)} %norm_kv.1.rest_0_), channel_id=1, source_target_pairs={{0,16},{1,17},{2,18},{3,19},{4,20},{5,21},{6,22},{7,23},{8,24},{9,... | collective-permute-start | bytes 393224 | tf_op jit(solution)/shard_map/ppermute | solution.py:297
  14.3 5.7 %collective-permute-start = (bf16[512,128]{1,0:T(8,128)(2,1)}, bf16[512,128]{1,0:T(8,128)(2,1)S(1)}, u32[]{:S(2)}, u32[]{:S(2)}) collective-permute-start(bf16[512,128]{1,0:T(8,128)(2,1)} %norm_kv.1.rest_0_), channel_id=1, source_target_pairs={{0,24},{1,25},{2,26},{3,27},{4,28},{5,29},{6,30},{7,31}} | collective-permute-start | bytes 393224 | tf_op jit(solution)/shard_map/ppermute | solution.py:297
  15.6 10.0 %collective-permute-start.6 = (bf16[512,128]{1,0:T(8,128)(2,1)}, bf16[512,128]{1,0:T(8,128)(2,1)S(1)}, u32[]{:S(2)}, u32[]{:S(2)}) collective-permute-start(bf16[512,128]{1,0:T(8,128)(2,1)} %norm_kv.1.rest_0_), channel_id=1, source_target_pairs={{0,4},{1,5},{2,6},{3,7},{4,0},{5,1},{6,2},{7,3},{8,12},{9,13},{10,... | collective-permute-start | bytes 393224 | tf_op jit(solution)/shard_map/ppermute | solution.py:302
  17.2 11.2 %collective-permute-start.5 = (bf16[512,128]{1,0:T(8,128)(2,1)S(1)}, bf16[512,128]{1,0:T(8,128)(2,1)S(1)}, u32[]{:S(2)}, u32[]{:S(2)}) collective-permute-start(bf16[512,128]{1,0:T(8,128)(2,1)S(1)} %collective-permute-done.4.rest_1_), channel_id=1, source_target_pairs={{0,4},{1,5},{2,6},{3,7},{4,0},{5,1},{6,2},{7,3},{8,12},{9,13},{10,... | collective-permute-start | bytes 393224 | tf_op jit(solution)/shard_map/ppermute | solution.py:302
  18.4 12.5 %collective-permute-start.3 = (bf16[512,128]{1,0:T(8,128)(2,1)S(1)}, bf16[512,128]{1,0:T(8,128)(2,1)S(1)}, u32[]{:S(2)}, u32[]{:S(2)}) collective-permute-start(bf16[512,128]{1,0:T(8,128)(2,1)S(1)} %collective-permute-done.2.rest_0_), channel_id=1, source_target_pairs={{0,4},{1,5},{2,6},{3,7},{4,0},{5,1},{6,2},{7,3},{8,12},{9,13},{10,... | collective-permute-start | bytes 393224 | tf_op jit(solution)/shard_map/ppermute | solution.py:302
  19.9 13.4 %collective-permute-start.1 = (bf16[512,128]{1,0:T(8,128)(2,1)S(1)}, bf16[512,128]{1,0:T(8,128)(2,1)S(1)}, u32[]{:S(2)}, u32[]{:S(2)}) collective-permute-start(bf16[512,128]{1,0:T(8,128)(2,1)S(1)} %collective-permute-done.rest_0_), channel_id=1, source_target_pairs={{0,4},{1,5},{2,6},{3,7},{4,0},{5,1},{6,2},{7,3},{8,12},{9,13},{10,... | collective-permute-start | bytes 393224 | tf_op jit(solution)/shard_map/ppermute | solution.py:302
  21.5 2.2 %copy-start.2 = (bf16[2048,1024]{1,0:T(8,128)(2,1)S(1)}, bf16[2048,1024]{1,0:T(8,128)(2,1)}, u32[]{:S(2)}) copy-start(bf16[2048,1024]{1,0:T(8,128)(2,1)} %wq_ref.1) | copy-start | bytes 12582916
  23.7 1.9 %copy-start.5 = (bf16[512,128]{1,0:T(8,128)(2,1)S(1)}, bf16[512,128]{1,0:T(8,128)(2,1)}, u32[]{:S(2)}) copy-start(bf16[512,128]{1,0:T(8,128)(2,1)} %norm_kv.1.rest_0_) | copy-start | bytes 393220
  30.9 4.1 %copy-start.8 = (bf16[1024,2048]{1,0:T(8,128)(2,1)S(1)}, bf16[1024,2048]{1,0:T(8,128)(2,1)}, u32[]{:S(2)}) copy-start(bf16[1024,2048]{1,0:T(8,128)(2,1)} %param.21) | copy-start | bytes 12582916
  35.8 1.6 collective-permute-start.8
  36.6 2.4 %copy-start.15 = (f32[64,8]{0,1:T(8,128)S(1)}, f32[64,8]{0,1:T(8,128)}, u32[]{:S(2)}) copy-start(f32[64,8]{0,1:T(8,128)} %param.24) | copy-start | bytes 6148
  36.6 2.5 %copy-start.14 = (s32[64,8]{0,1:T(8,128)S(1)}, s32[64,8]{0,1:T(8,128)}, u32[]{:S(2)}) copy-start(s32[64,8]{0,1:T(8,128)} %param.23) | copy-start | bytes 6148
  36.6 10.3 %copy-start.16 = (f32[2048]{0:T(1024)S(1)}, f32[2048]{0:T(1024)}, u32[]{:S(2)}) copy-start(f32[2048]{0:T(1024)} %param.22) | copy-start | bytes 24580
  36.7 3.2 %collective-permute-start.7 = (bf16[64,2048]{1,0:T(8,128)(2,1)S(1)}, bf16[64,2048]{1,0:T(8,128)(2,1)S(1)}, u32[]{:S(2)}, u32[]{:S(2)}) collective-permute-start(bf16[64,2048]{1,0:T(8,128)(2,1)S(1)} %fusion.13), channel_id=1, source_target_pairs={{0,1},{1,0},{2,3},{3,2},{4,5},{5,4},{6,7},{7,6},{8,9},{9,8},{10,11... | collective-permute-start | bytes 786440 | tf_op jit(solution)/shard_map/ppermute | solution.py:383
  37.4 8.4 %collective-permute-start.9 = (bf16[64,2048]{1,0:T(8,128)(2,1)S(1)}, bf16[64,2048]{1,0:T(8,128)(2,1)S(1)}, u32[]{:S(2)}, u32[]{:S(2)}) collective-permute-start(bf16[64,2048]{1,0:T(8,128)(2,1)S(1)} %fusion.10), channel_id=1, source_target_pairs={{0,2},{1,3},{2,0},{3,1},{4,6},{5,7},{6,4},{7,5},{8,10},{9,11},{10,... | collective-permute-start | bytes 786440 | tf_op jit(solution)/shard_map/ppermute | solution.py:390
  46.1 0.8 copy-start.9
  46.9 22.8 %copy-start = (bf16[1,2048,768]{2,1,0:T(8,128)(2,1)S(1)}, bf16[1,2048,768]{2,1,0:T(8,128)(2,1)}, u32[]{:S(2)}) copy-start(bf16[1,2048,768]{2,1,0:T(8,128)(2,1)} %param.25) | copy-start | bytes 9437188
  47.8 12.7 %collective-permute-start.10 = (bf16[64,2176]{1,0:T(8,128)(2,1)}, bf16[64,2176]{1,0:T(8,128)(2,1)}, u32[]{:S(2)}, u32[]{:S(2)}) collective-permute-start(bf16[64,2176]{1,0:T(8,128)(2,1)} %concatenate.18), channel_id=1, source_target_pairs={{0,24},{1,25},{2,26},{3,27},{4,28},{5,29},{6,30},{7,31},{8,16},{9,... | collective-permute-start | bytes 835592 | tf_op jit(solution)/shard_map/ppermute | solution.py:444
  72.4 31.0 %all-to-all-start.2 = ((bf16[16,24,2048]{2,1,0:T(8,128)(2,1)}), bf16[16,24,2048]{2,1,0:T(8,128)(2,1)}, u32[]{:S(2)}, u32[]{:S(2)}) async-start(bf16[16,24,2048]{2,1,0:T(8,128)(2,1)} %bitcast.62), calls=%async_computation.2 | async-start | bytes 3145728 | tf_op jit(solution)/shard_map/all_to_all | solution.py:402
  103.4 27.2 %all-to-all-start = ((bf16[16,24,2048]{2,1,0:T(8,128)(2,1)}), bf16[16,24,2048]{2,1,0:T(8,128)(2,1)}, u32[]{:S(2)}, u32[]{:S(2)}) async-start(bf16[16,24,2048]{2,1,0:T(8,128)(2,1)} %bitcast.64), calls=%async_computation | async-start | bytes 3145728 | tf_op jit(solution)/shard_map/all_to_all | solution.py:402
  130.6 27.2 %all-to-all-start.3 = ((bf16[16,24,2048]{2,1,0:T(8,128)(2,1)}), bf16[16,24,2048]{2,1,0:T(8,128)(2,1)}, u32[]{:S(2)}, u32[]{:S(2)}) async-start(bf16[16,24,2048]{2,1,0:T(8,128)(2,1)} %bitcast.65), calls=%async_computation.3 | async-start | bytes 3145728 | tf_op jit(solution)/shard_map/all_to_all | solution.py:402
  157.9 3.9 %copy-start.11 = (f32[64,384]{1,0:T(8,128)S(1)}, f32[64,384]{1,0:T(8,128)}, u32[]{:S(2)}) copy-start(f32[64,384]{1,0:T(8,128)} %copy.40) | copy-start | bytes 294916
  157.9 3.9 %copy-start.12 = (bf16[64,384]{1,0:T(8,128)(2,1)S(1)}, bf16[64,384]{1,0:T(8,128)(2,1)}, u32[]{:S(2)}) copy-start(bf16[64,384]{1,0:T(8,128)(2,1)} %get-tuple-element.17) | copy-start | bytes 147460
  157.9 26.9 %all-to-all-start.1 = ((bf16[16,24,2048]{2,1,0:T(8,128)(2,1)}), bf16[16,24,2048]{2,1,0:T(8,128)(2,1)S(1)}, u32[]{:S(2)}, u32[]{:S(2)}) async-start(bf16[16,24,2048]{2,1,0:T(8,128)(2,1)} %bitcast.63), calls=%async_computation.1 | async-start | bytes 3145728 | tf_op jit(solution)/shard_map/all_to_all | solution.py:402
  161.8 23.0 %copy-start.13 = (bf16[64,384]{1,0:T(8,128)(2,1)S(1)}, bf16[64,384]{1,0:T(8,128)(2,1)}, u32[]{:S(2)}) copy-start(bf16[64,384]{1,0:T(8,128)(2,1)} %get-tuple-element.22) | copy-start | bytes 147460
  163.7 23.9 %copy-start.10 = (f32[64,2048]{1,0:T(8,128)S(1)}, f32[64,2048]{1,0:T(8,128)}, u32[]{:S(2)}) copy-start(f32[64,2048]{1,0:T(8,128)} %copy-done.9) | copy-start | bytes 1572868
  163.7 23.9 %collective-permute-start.11 = (bf16[64,2048]{1,0:T(8,128)(2,1)S(1)}, bf16[64,2048]{1,0:T(8,128)(2,1)S(1)}, u32[]{:S(2)}, u32[]{:S(2)}) collective-permute-start(bf16[64,2048]{1,0:T(8,128)(2,1)S(1)} %fusion.6), channel_id=1, source_target_pairs={{0,24},{1,25},{2,26},{3,27},{4,28},{5,29},{6,30},{7,31},{8,16},{9,... | collective-permute-start | bytes 786440 | tf_op jit(solution)/shard_map/ppermute | solution.py:466

commit v5 on v4

--- a/solution.py
+++ b/solution.py
@@ -291,9 +291,7 @@
 
     kv_blocks, kv_bias = [own_kv], [jnp.float32(0.0)]
     for k in range(1, line):
-        up = make_pairs(
-            lambda s, h, k=k: (s + k * side, h) if s + k * side < seq_count else None
-        )
+        up = make_pairs(lambda s, h, k=k: ((s + k * side) % seq_count, h))
         kv_blocks.append(lax.ppermute(own_kv, BOTH, up))
         kv_bias.append(jnp.where(line_index >= k, 0.0, NEGATIVE))
     if side == 2:
@@ -431,24 +429,14 @@
     gates = [pltpu.with_memory_space_constraint(w_gate[e], pltpu.VMEM) for e in range(local_count)]
     weights = (gates, w_up, w_down)
     if halves == 2:
-        spare = -3 * top_count % head_dim
-        sent = jnp.concatenate(
-            [
-                routed,
-                expert_ids.astype(jnp.bfloat16),
-                *split_exact(mixing),
-                jnp.zeros((rows_here, spare), jnp.bfloat16),
-            ],
-            axis=1,
-        )
-        came = lax.ppermute(sent, BOTH, mirror)
+        mirrored = lax.ppermute(routed, BOTH, mirror)
         own_rows_in = dispatch(fill_slots(routed, tables[0][0]))
-        mirrored, beside = came[:, :width], came[:, width:].astype(jnp.float32)
+        sent = jnp.concatenate([expert_ids.astype(jnp.float32), mixing], axis=1)
+        seen = lax.ppermute(sent, BOTH, mirror)
         tables.append(
             slot_tables(
-                beside[:, :top_count].astype(jnp.int32),
-                beside[:, top_count : 2 * top_count]
-                + beside[:, 2 * top_count : 3 * top_count],
+                seen[:, :top_count].astype(jnp.int32),
+                seen[:, top_count:],
                 lax.optimization_barrier(jnp.int32(0)),
             )
         )

time: 189 us -> 175 us (0.926)
  starting transfers between devices: 47.2 us -> 42 us
  waiting for transfers between devices: 78.2 us -> 73.8 us
  local copies, waits for them, and re-layouts: 16.4 us -> 12.8 us
    ppermute x1 -> x2, waiting for transfers between devices: 6.4 us -> 0.01 us  [the longest x1 0.01 us: body(): seen = lax.ppermute(sent, BOTH, mirror)]
    ppermute x3, starting transfers between devices: 10.8 us -> 7.05 us  [body(): kv_blocks.append(lax.ppermute(own_kv, BOTH, up))]
    ppermute x1 -> x2, starting transfers between devices: 6.17 us -> 4.45 us  [the longest x1 3.94 us: body(): mirrored = lax.ppermute(routed, BOTH, mirror)]
  transfers between devices with their start and end apart: 16 -> 17, of which waited for: 9 -> 10; matrix products, arithmetic and copies ran while one was open for 8% -> 11% of each run, Pallas kernels for 13% -> 14%
where the time goes in v5:
time: 175 us
  waiting for transfers between devices  73.8 us (42%)
  starting transfers between devices  42 us (24%)
  Pallas kernels  31.8 us (18%)
  local copies, waits for them, and re-layouts  12.8 us (7%)
  other arithmetic  7.98 us (5%)
  matrix products  5.79 us (3%)
    all_to_all x4, waiting for transfers between devices, exchange(): lax.all_to_all(rows.reshape(members, local_count * capacity, width), BOTH...  61.6 us
    all_to_all x4, starting transfers between devices, exchange(): lax.all_to_all(rows.reshape(members, local_count * capacity, width), BOTH...  20.4 us
    pallas_call x2, Pallas kernels, run_experts(): pl.pallas_call(expert_kernel, out_shape=jax.ShapeDtypeStruct((rows, width...  14.7 us
    pallas_call x4, Pallas kernels, attend(): pl.pallas_call(functools.partial(attend_kernel, head_dim, blocks, not sta...  9.33 us
    ppermute x3, starting transfers between devices, body(): kv_blocks.append(lax.ppermute(own_kv, BOTH, up))  7.05 us
    ppermute x1, waiting for transfers between devices, body(): came = lax.ppermute(given, BOTH, shift).astype(jnp.float32)  6.6 us
    eq x8, local copies, waits for them, and re-layouts, slot_tables(): place[:, :, None]  5.53 us
    ppermute x1, waiting for transfers between devices, body(): far_sum = lax.ppermute(foreign, BOTH, mirror)  4.25 us
  transfers between devices with their start and end apart: 17, of which 10 were waited for; matrix products, arithmetic and copies ran while one was open for 11% of the time, Pallas kernels for 14%

profile of v5, /device:TPU:0, one launch (start us, length us, event | category | flops | bytes accessed | tf_op | source)
XLA Modules:
  0.0 174.6 jit_solution(3297581914598618922)
XLA Ops:
  0.0 0.5 fusion.27
  0.6 0.8 pad_maximum_fusion
  1.5 3.3 %norm_kv.1.rest_0_ = bf16[512,128]{1,0:T(8,128)(2,1)} custom-call(bf16[256,2048]{1,0:T(8,128)(2,1)} %refs_0_.1, bf16[2048,128]{1,0:T(8,128)(2,1)} %refs_1_.1, bf16[2048,128]{1,0:T(8,128)(2,1)} %refs_2_.1, f32[1,2048]{1,0:T(1,128)} %bitcast.55, f32[1,128]{1,0:T(1,128)} %bitcast.73, f32[256,128]{1,0:T(8,128)} %get-tuple-element.30.cos_ref.refs_5_, ...), custom_call_target="tpu_custom_call" | custom-call | tf_op jit(solution)/shard_map/norm_kv/pallas_call | solution.py:282
  4.8 3.1 %collective-permute-start.4 = (bf16[512,128]{1,0:T(8,128)(2,1)}, bf16[512,128]{1,0:T(8,128)(2,1)S(1)}, u32[]{:S(2)}, u32[]{:S(2)}) collective-permute-start(bf16[512,128]{1,0:T(8,128)(2,1)} %norm_kv.1.rest_0_), channel_id=1, source_target_pairs={{0,8},{1,9},{2,10},{3,11},{4,12},{5,13},{6,14},{7,15},{8,16},{9,17... | collective-permute-start | bytes 393224 | tf_op jit(solution)/shard_map/ppermute | solution.py:295
  7.9 1.5 collective-permute-start.6
  9.4 2.6 %collective-permute-start.2 = (bf16[512,128]{1,0:T(8,128)(2,1)}, bf16[512,128]{1,0:T(8,128)(2,1)S(1)}, u32[]{:S(2)}, u32[]{:S(2)}) collective-permute-start(bf16[512,128]{1,0:T(8,128)(2,1)} %norm_kv.1.rest_0_), channel_id=1, source_target_pairs={{0,16},{1,17},{2,18},{3,19},{4,20},{5,21},{6,22},{7,23},{8,24},{9,... | collective-permute-start | bytes 393224 | tf_op jit(solution)/shard_map/ppermute | solution.py:295
  12.0 1.3 collective-permute-start
  13.4 0.5 collective-permute-start.10
  14.2 0.1 eq.92
  14.3 2.2 %copy-done.2 = bf16[2048,1024]{1,0:T(8,128)(2,1)S(1)} copy-done((bf16[2048,1024]{1,0:T(8,128)(2,1)S(1)}, bf16[2048,1024]{1,0:T(8,128)(2,1)}, u32[]{:S(2)}) %copy-start.2) | copy-done | bytes 4194328
  16.5 1.8 %queries.1.q_ref = bf16[256,1024]{1,0:T(8,128)(2,1)S(1)} custom-call(bf16[256,2048]{1,0:T(8,128)(2,1)S(1)} %copy-done.1, f32[1,2048]{1,0:T(1,128)S(1)} %bitcast.56, bf16[2048,1024]{1,0:T(8,128)(2,1)S(1)} %copy-done.2, f32[1,128]{1,0:T(1,128)S(1)} %bitcast.57, f32[256,128]{1,0:T(8,128)S(1)} %copy-done.3, f32[256,128]{1,0:T(8,128)S(1)} %copy-done.4), custom_call_target="tpu_custom_call" | custom-call | tf_op jit(solution)/shard_map/queries/pallas_call | solution.py:335
  18.3 0.6 collective-permute-start.5
  18.9 0.6 collective-permute-done.2.rest_0_
  19.5 1.5 collective-permute-start.3
  21.0 0.6 collective-permute-start.1
  21.6 2.9 %attend.4 = (f32[8,8,256]{2,1,0:T(8,128)S(1)}, f32[8,128,256]{2,1,0:T(8,128)S(1)}) custom-call(f32[3]{0:T(128)S(1)} %pad_maximum_fusion.5.bias_ref, bf16[256,1024]{1,0:T(8,128)(2,1)S(1)} %queries.1.q_ref, bf16[512,128]{1,0:T(8,128)(2,1)S(1)} %copy-done.5, bf16[512,128]{1,0:T(8,128)(2,1)S(1)} %collective-permute-done.4.rest_1_, ...), custom_call_target="tpu_custom_call" | custom-call | tf_op jit(solution)/shard_map/attend/pallas_call | solution.py:146
  24.4 0.3 collective-permute-done.5.rest_1_
  24.7 2.4 %attend.5 = (f32[8,8,256]{2,1,0:T(8,128)S(1)}, f32[8,128,256]{2,1,0:T(8,128)S(1)}) custom-call(f32[2]{0:T(128)S(1)} %pad_maximum_fusion.4.bias_ref, bf16[256,1024]{1,0:T(8,128)(2,1)S(1)} %queries.1.q_ref, bf16[512,128]{1,0:T(8,128)(2,1)S(1)} %collective-permute-done.2.rest_0_, bf16[512,128]{1,0:T(8,128)(2,1)S(1)} %collective-permute-done.5.rest_1_, ...), custom_call_target="tpu_custom_call" | custom-call | tf_op jit(solution)/shard_map/attend/pallas_call | solution.py:146
  27.1 0.4 collective-permute-done.3.rest_1_
  27.5 2.5 %attend.6 = (f32[8,8,256]{2,1,0:T(8,128)S(1)}, f32[8,128,256]{2,1,0:T(8,128)S(1)}) custom-call(f32[2]{0:T(128)S(1)} %pad_maximum_fusion.3.bias_ref, bf16[256,1024]{1,0:T(8,128)(2,1)S(1)} %queries.1.q_ref, bf16[512,128]{1,0:T(8,128)(2,1)S(1)} %collective-permute-done.rest_0_, bf16[512,128]{1,0:T(8,128)(2,1)S(1)} %collective-permute-done.3.rest_1_, ...), custom_call_target="tpu_custom_call" | custom-call | tf_op jit(solution)/shard_map/attend/pallas_call | solution.py:146
  30.0 1.6 attend.7
  31.6 0.7 fusion
  32.4 0.7 fusion.2
  33.2 0.6 collective-permute-start.7
  33.8 0.2 collective-permute-done.8
  34.0 1.6 collective-permute-start.9
  35.7 0.1 fusion.4
  35.8 6.6 %collective-permute-done.9 = bf16[64,2048]{1,0:T(8,128)(2,1)S(1)} collective-permute-done((bf16[64,2048]{1,0:T(8,128)(2,1)S(1)}, bf16[64,2048]{1,0:T(8,128)(2,1)S(1)}, u32[]{:S(2)}, u32[]{:S(2)}) %collective-permute-start.9) | collective-permute-done | bytes 262176 | tf_op jit(solution)/shard_map/ppermute | solution.py:388
  42.4 1.2 multiply_reduce_fusion
  43.6 0.8 copy-done.9
  44.5 0.1 multiply_convert_fusion
  44.6 3.9 %collective-permute-start.11 = (bf16[64,2048]{1,0:T(8,128)(2,1)S(1)}, bf16[64,2048]{1,0:T(8,128)(2,1)}, u32[]{:S(2)}, u32[]{:S(2)}) collective-permute-start(bf16[64,2048]{1,0:T(8,128)(2,1)S(1)} %multiply_convert_fusion), channel_id=1, source_target_pairs={{0,24},{1,25},{2,26},{3,27},{4,28},{5,29},{6,30},{7,31},{8,16},{9,... | collective-permute-start | bytes 786440 | tf_op jit(solution)/shard_map/ppermute | solution.py:432
  48.5 0.1 fusion.26
  48.6 0.7 broadcast_in_dim.86
  49.3 1.0 copy.32
  50.3 0.7 eq.89
  51.0 1.7 copy.31
  52.7 1.5 select_convert_fusion
  54.2 0.6 convert_element_type.124.pick_ref
  54.9 2.7 %fill.1 = bf16[384,2048]{1,0:T(8,128)(2,1)} custom-call(bf16[64,2048]{1,0:T(8,128)(2,1)} %collective-permute-done.11.rows_ref, bf16[64,384]{1,0:T(8,128)(2,1)} %convert_element_type.124.pick_ref, bf16[2048,768]{1,0:T(8,128)(2,1)S(1)} %bitcast.51), custom_call_target="tpu_custom_call" | custom-call | tf_op jit(solution)/shard_map/fill/pallas_call | solution.py:443
  57.5 7.7 %all-to-all-start.2 = ((bf16[16,24,2048]{2,1,0:T(8,128)(2,1)}), bf16[16,24,2048]{2,1,0:T(8,128)(2,1)}, u32[]{:S(2)}, u32[]{:S(2)}) async-start(bf16[16,24,2048]{2,1,0:T(8,128)(2,1)} %bitcast.62), calls=%async_computation.2 | async-start | bytes 3145728 | tf_op jit(solution)/shard_map/all_to_all | solution.py:400
  65.2 0.1 fusion.24
  65.3 0.7 broadcast_in_dim.82
  66.0 1.7 copy.30
  67.8 0.1 fusion.5
  67.9 0.7 eq.80
  68.6 1.7 copy.29
  70.3 0.7 eq.83
  71.0 1.6 select_convert_fusion.1
  72.6 1.8 %convolution_convert_fusion = bf16[384,2048]{1,0:T(8,128)(2,1)} fusion(pred[64,384]{1,0:T(32,128)(4,1)S(1)} %get-tuple-element.20, bf16[64,2048]{1,0:T(8,128)(2,1)S(1)} %multiply_convert_fusion), kind=kOutput, calls=%fused_computation.4 | convolution fusion | flops 101449728 | bytes 1859584 | tf_op jit(solution)/shard_map/dot_general | solution.py:418
  74.4 13.7 %all-to-all-done.2 = bf16[16,24,2048]{2,1,0:T(8,128)(2,1)} async-done(((bf16[16,24,2048]{2,1,0:T(8,128)(2,1)}), bf16[16,24,2048]{2,1,0:T(8,128)(2,1)}, u32[]{:S(2)}, u32[]{:S(2)}) %all-to-all-start.2) | async-done | bytes 1572896 | tf_op jit(solution)/shard_map/all_to_all | solution.py:400
  88.1 4.4 %all-to-all-start = ((bf16[16,24,2048]{2,1,0:T(8,128)(2,1)}), bf16[16,24,2048]{2,1,0:T(8,128)(2,1)}, u32[]{:S(2)}, u32[]{:S(2)}) async-start(bf16[16,24,2048]{2,1,0:T(8,128)(2,1)} %bitcast.64), calls=%async_computation | async-start | bytes 3145728 | tf_op jit(solution)/shard_map/all_to_all | solution.py:400
  92.5 7.3 %experts.3 = bf16[384,2048]{1,0:T(8,128)(2,1)} custom-call(bf16[384,2048]{1,0:T(8,128)(2,1)} %bitcast.27.x_hbm, bf16[2048,768]{1,0:T(8,128)(2,1)S(1)} %bitcast.52, bf16[2048,768]{1,0:T(8,128)(2,1)} %bitcast.58, bf16[768,2048]{1,0:T(8,128)(2,1)} %bitcast.60), custom_call_target="tpu_custom_call" | custom-call | tf_op jit(solution)/shard_map/experts/pallas_call | solution.py:200
  99.8 15.5 %all-to-all-done = bf16[16,24,2048]{2,1,0:T(8,128)(2,1)} async-done(((bf16[16,24,2048]{2,1,0:T(8,128)(2,1)}), bf16[16,24,2048]{2,1,0:T(8,128)(2,1)}, u32[]{:S(2)}, u32[]{:S(2)}) %all-to-all-start) | async-done | bytes 1572896 | tf_op jit(solution)/shard_map/all_to_all | solution.py:400
  115.3 4.4 %all-to-all-start.3 = ((bf16[16,24,2048]{2,1,0:T(8,128)(2,1)}), bf16[16,24,2048]{2,1,0:T(8,128)(2,1)}, u32[]{:S(2)}, u32[]{:S(2)}) async-start(bf16[16,24,2048]{2,1,0:T(8,128)(2,1)} %bitcast.65), calls=%async_computation.3 | async-start | bytes 3145728 | tf_op jit(solution)/shard_map/all_to_all | solution.py:400
  119.7 7.3 %experts.2 = bf16[384,2048]{1,0:T(8,128)(2,1)} custom-call(bf16[384,2048]{1,0:T(8,128)(2,1)} %bitcast.18.x_hbm, bf16[2048,768]{1,0:T(8,128)(2,1)S(1)} %bitcast.53, bf16[2048,768]{1,0:T(8,128)(2,1)} %bitcast.59, bf16[768,2048]{1,0:T(8,128)(2,1)} %bitcast.61), custom_call_target="tpu_custom_call" | custom-call | tf_op jit(solution)/shard_map/experts/pallas_call | solution.py:200
  127.1 15.5 %all-to-all-done.3 = bf16[16,24,2048]{2,1,0:T(8,128)(2,1)} async-done(((bf16[16,24,2048]{2,1,0:T(8,128)(2,1)}), bf16[16,24,2048]{2,1,0:T(8,128)(2,1)}, u32[]{:S(2)}, u32[]{:S(2)}) %all-to-all-start.3) | async-done | bytes 1572896 | tf_op jit(solution)/shard_map/all_to_all | solution.py:400
  142.5 3.8 %all-to-all-start.1 = ((bf16[16,24,2048]{2,1,0:T(8,128)(2,1)}), bf16[16,24,2048]{2,1,0:T(8,128)(2,1)S(1)}, u32[]{:S(2)}, u32[]{:S(2)}) async-start(bf16[16,24,2048]{2,1,0:T(8,128)(2,1)} %bitcast.63), calls=%async_computation.1 | async-start | bytes 3145728 | tf_op jit(solution)/shard_map/all_to_all | solution.py:400
  146.5 1.9 %fusion.19 = f32[128,2048]{1,0:T(8,128)S(1)} fusion(bf16[384,2048]{1,0:T(8,128)(2,1)} %bitcast.29, bf16[64,384]{1,0:T(8,128)(2,1)S(1)} %subtract_convert_fusion, bf16[64,384]{1,0:T(8,128)(2,1)S(1)} %copy-done.12), kind=kOutput, calls=%fused_computation.34 | convolution fusion | flops 201523200 | bytes 2719744 | tf_op jit(solution)/shard_map/dot_general | solution.py:426
  148.4 3.8 %collective-permute-start.12 = (bf16[64,2048]{1,0:T(8,128)(2,1)S(1)}, bf16[64,2048]{1,0:T(8,128)(2,1)S(1)}, u32[]{:S(2)}, u32[]{:S(2)}) collective-permute-start(bf16[64,2048]{1,0:T(8,128)(2,1)S(1)} %fusion.6), channel_id=1, source_target_pairs={{0,24},{1,25},{2,26},{3,27},{4,28},{5,29},{6,30},{7,31},{8,16},{9,... | collective-permute-start | bytes 786440 | tf_op jit(solution)/shard_map/ppermute | solution.py:454
  152.2 17.0 %all-to-all-done.1 = bf16[16,24,2048]{2,1,0:T(8,128)(2,1)S(1)} async-done(((bf16[16,24,2048]{2,1,0:T(8,128)(2,1)}), bf16[16,24,2048]{2,1,0:T(8,128)(2,1)S(1)}, u32[]{:S(2)}, u32[]{:S(2)}) %all-to-all-start.1) | async-done | bytes 1572896 | tf_op jit(solution)/shard_map/all_to_all | solution.py:400
  169.1 0.4 fusion.15
  169.6 4.3 %collective-permute-done.12 = bf16[64,2048]{1,0:T(8,128)(2,1)S(1)} collective-permute-done((bf16[64,2048]{1,0:T(8,128)(2,1)S(1)}, bf16[64,2048]{1,0:T(8,128)(2,1)S(1)}, u32[]{:S(2)}, u32[]{:S(2)}) %collective-permute-start.12) | collective-permute-done | bytes 262176 | tf_op jit(solution)/shard_map/ppermute | solution.py:454
  173.8 0.8 fusion.9
  (65 shorter events, 0.9 us)
Async XLA Ops:
  0.6 12.8 %copy-start.15 = (f32[64,8]{0,1:T(8,128)S(1)}, f32[64,8]{0,1:T(8,128)}, u32[]{:S(2)}) copy-start(f32[64,8]{0,1:T(8,128)} %param.24) | copy-start | bytes 6148
  0.6 12.8 %copy-start.14 = (s32[64,8]{0,1:T(8,128)S(1)}, s32[64,8]{0,1:T(8,128)}, u32[]{:S(2)}) copy-start(s32[64,8]{0,1:T(8,128)} %param.23) | copy-start | bytes 6148
  0.6 13.7 %copy-start.1 = (bf16[256,2048]{1,0:T(8,128)(2,1)S(1)}, bf16[256,2048]{1,0:T(8,128)(2,1)}, u32[]{:S(2)}) copy-start(bf16[256,2048]{1,0:T(8,128)(2,1)} %refs_0_.1) | copy-start | bytes 3145732
  0.6 13.7 %copy-start.6 = (f32[2048]{0:T(1024)S(1)}, f32[2048]{0:T(1024)}, u32[]{:S(2)}) copy-start(f32[2048]{0:T(1024)} %param.15) | copy-start | bytes 24580
  0.6 13.7 %copy-start.7 = (f32[128]{0:T(128)S(1)}, f32[128]{0:T(128)}, u32[]{:S(2)}) copy-start(f32[128]{0:T(128)} %param.19) | copy-start | bytes 1540
  1.5 12.8 %copy-start.3 = (f32[256,128]{1,0:T(8,128)S(1)}, f32[256,128]{1,0:T(8,128)}, u32[]{:S(2)}) copy-start(f32[256,128]{1,0:T(8,128)} %get-tuple-element.30.cos_ref.refs_5_) | copy-start | bytes 393220
  1.5 12.8 %copy-start.4 = (f32[256,128]{1,0:T(8,128)S(1)}, f32[256,128]{1,0:T(8,128)}, u32[]{:S(2)}) copy-start(f32[256,128]{1,0:T(8,128)} %get-tuple-element.31.sin_ref.refs_6_) | copy-start | bytes 393220
  4.8 13.5 %collective-permute-start.4 = (bf16[512,128]{1,0:T(8,128)(2,1)}, bf16[512,128]{1,0:T(8,128)(2,1)S(1)}, u32[]{:S(2)}, u32[]{:S(2)}) collective-permute-start(bf16[512,128]{1,0:T(8,128)(2,1)} %norm_kv.1.rest_0_), channel_id=1, source_target_pairs={{0,8},{1,9},{2,10},{3,11},{4,12},{5,13},{6,14},{7,15},{8,16},{9,17... | collective-permute-start | bytes 393224 | tf_op jit(solution)/shard_map/ppermute | solution.py:295
  7.9 13.6 %collective-permute-start.6 = (bf16[512,128]{1,0:T(8,128)(2,1)}, bf16[512,128]{1,0:T(8,128)(2,1)S(1)}, u32[]{:S(2)}, u32[]{:S(2)}) collective-permute-start(bf16[512,128]{1,0:T(8,128)(2,1)} %norm_kv.1.rest_0_), channel_id=1, source_target_pairs={{0,4},{1,5},{2,6},{3,7},{4,0},{5,1},{6,2},{7,3},{8,12},{9,13},{10,... | collective-permute-start | bytes 393224 | tf_op jit(solution)/shard_map/ppermute | solution.py:300
  9.4 10.1 %collective-permute-start.2 = (bf16[512,128]{1,0:T(8,128)(2,1)}, bf16[512,128]{1,0:T(8,128)(2,1)S(1)}, u32[]{:S(2)}, u32[]{:S(2)}) collective-permute-start(bf16[512,128]{1,0:T(8,128)(2,1)} %norm_kv.1.rest_0_), channel_id=1, source_target_pairs={{0,16},{1,17},{2,18},{3,19},{4,20},{5,21},{6,22},{7,23},{8,24},{9,... | collective-permute-start | bytes 393224 | tf_op jit(solution)/shard_map/ppermute | solution.py:295
  12.0 9.0 %collective-permute-start = (bf16[512,128]{1,0:T(8,128)(2,1)}, bf16[512,128]{1,0:T(8,128)(2,1)S(1)}, u32[]{:S(2)}, u32[]{:S(2)}) collective-permute-start(bf16[512,128]{1,0:T(8,128)(2,1)} %norm_kv.1.rest_0_), channel_id=1, source_target_pairs={{0,24},{1,25},{2,26},{3,27},{4,28},{5,29},{6,30},{7,31},{8,0},{9,1... | collective-permute-start | bytes 393224 | tf_op jit(solution)/shard_map/ppermute | solution.py:295
  13.4 8.1 %collective-permute-start.10 = (f32[64,16]{0,1:T(8,128)S(1)}, f32[64,16]{0,1:T(8,128)S(1)}, u32[]{:S(2)}, u32[]{:S(2)}) collective-permute-start(f32[64,16]{0,1:T(8,128)S(1)} %pad_maximum_fusion.2), channel_id=1, source_target_pairs={{0,24},{1,25},{2,26},{3,27},{4,28},{5,29},{6,30},{7,31},{8,16},{9,... | collective-permute-start | bytes 12296 | tf_op jit(solution)/shard_map/ppermute | solution.py:435
  14.3 2.2 %copy-start.2 = (bf16[2048,1024]{1,0:T(8,128)(2,1)S(1)}, bf16[2048,1024]{1,0:T(8,128)(2,1)}, u32[]{:S(2)}) copy-start(bf16[2048,1024]{1,0:T(8,128)(2,1)} %wq_ref.1) | copy-start | bytes 12582916
  16.5 5.1 %copy-start.5 = (bf16[512,128]{1,0:T(8,128)(2,1)S(1)}, bf16[512,128]{1,0:T(8,128)(2,1)}, u32[]{:S(2)}) copy-start(bf16[512,128]{1,0:T(8,128)(2,1)} %norm_kv.1.rest_0_) | copy-start | bytes 393220
  18.3 6.4 %collective-permute-start.5 = (bf16[512,128]{1,0:T(8,128)(2,1)S(1)}, bf16[512,128]{1,0:T(8,128)(2,1)S(1)}, u32[]{:S(2)}, u32[]{:S(2)}) collective-permute-start(bf16[512,128]{1,0:T(8,128)(2,1)S(1)} %collective-permute-done.4.rest_1_), channel_id=1, source_target_pairs={{0,4},{1,5},{2,6},{3,7},{4,0},{5,1},{6,2},{7,3},{8,12},{9,13},{10,... | collective-permute-start | bytes 393224 | tf_op jit(solution)/shard_map/ppermute | solution.py:300
  19.5 8.0 %collective-permute-start.3 = (bf16[512,128]{1,0:T(8,128)(2,1)S(1)}, bf16[512,128]{1,0:T(8,128)(2,1)S(1)}, u32[]{:S(2)}, u32[]{:S(2)}) collective-permute-start(bf16[512,128]{1,0:T(8,128)(2,1)S(1)} %collective-permute-done.2.rest_0_), channel_id=1, source_target_pairs={{0,4},{1,5},{2,6},{3,7},{4,0},{5,1},{6,2},{7,3},{8,12},{9,13},{10,... | collective-permute-start | bytes 393224 | tf_op jit(solution)/shard_map/ppermute | solution.py:300
  21.0 9.0 %collective-permute-start.1 = (bf16[512,128]{1,0:T(8,128)(2,1)S(1)}, bf16[512,128]{1,0:T(8,128)(2,1)S(1)}, u32[]{:S(2)}, u32[]{:S(2)}) collective-permute-start(bf16[512,128]{1,0:T(8,128)(2,1)S(1)} %collective-permute-done.rest_0_), channel_id=1, source_target_pairs={{0,4},{1,5},{2,6},{3,7},{4,0},{5,1},{6,2},{7,3},{8,12},{9,13},{10,... | collective-permute-start | bytes 393224 | tf_op jit(solution)/shard_map/ppermute | solution.py:300
  27.5 4.1 %copy-start.8 = (bf16[1024,2048]{1,0:T(8,128)(2,1)S(1)}, bf16[1024,2048]{1,0:T(8,128)(2,1)}, u32[]{:S(2)}) copy-start(bf16[1024,2048]{1,0:T(8,128)(2,1)} %param.21) | copy-start | bytes 12582916
  32.4 1.6 collective-permute-start.8
  33.2 11.2 %copy-start.16 = (f32[2048]{0:T(1024)S(1)}, f32[2048]{0:T(1024)}, u32[]{:S(2)}) copy-start(f32[2048]{0:T(1024)} %param.22) | copy-start | bytes 24580
  33.2 2.6 %collective-permute-start.7 = (bf16[64,2048]{1,0:T(8,128)(2,1)S(1)}, bf16[64,2048]{1,0:T(8,128)(2,1)S(1)}, u32[]{:S(2)}, u32[]{:S(2)}) collective-permute-start(bf16[64,2048]{1,0:T(8,128)(2,1)S(1)} %fusion.13), channel_id=1, source_target_pairs={{0,1},{1,0},{2,3},{3,2},{4,5},{5,4},{6,7},{7,6},{8,9},{9,8},{10,11... | collective-permute-start | bytes 786440 | tf_op jit(solution)/shard_map/ppermute | solution.py:381
  34.0 8.4 %collective-permute-start.9 = (bf16[64,2048]{1,0:T(8,128)(2,1)S(1)}, bf16[64,2048]{1,0:T(8,128)(2,1)S(1)}, u32[]{:S(2)}, u32[]{:S(2)}) collective-permute-start(bf16[64,2048]{1,0:T(8,128)(2,1)S(1)} %fusion.10), channel_id=1, source_target_pairs={{0,2},{1,3},{2,0},{3,1},{4,6},{5,7},{6,4},{7,5},{8,10},{9,11},{10,... | collective-permute-start | bytes 786440 | tf_op jit(solution)/shard_map/ppermute | solution.py:388
  35.8 19.0 %copy-start = (bf16[1,2048,768]{2,1,0:T(8,128)(2,1)S(1)}, bf16[1,2048,768]{2,1,0:T(8,128)(2,1)}, u32[]{:S(2)}) copy-start(bf16[1,2048,768]{2,1,0:T(8,128)(2,1)} %param.25) | copy-start | bytes 9437188
  43.6 0.8 copy-start.9
  44.6 10.3 %collective-permute-start.11 = (bf16[64,2048]{1,0:T(8,128)(2,1)S(1)}, bf16[64,2048]{1,0:T(8,128)(2,1)}, u32[]{:S(2)}, u32[]{:S(2)}) collective-permute-start(bf16[64,2048]{1,0:T(8,128)(2,1)S(1)} %multiply_convert_fusion), channel_id=1, source_target_pairs={{0,24},{1,25},{2,26},{3,27},{4,28},{5,29},{6,30},{7,31},{8,16},{9,... | collective-permute-start | bytes 786440 | tf_op jit(solution)/shard_map/ppermute | solution.py:432
  57.5 30.5 %all-to-all-start.2 = ((bf16[16,24,2048]{2,1,0:T(8,128)(2,1)}), bf16[16,24,2048]{2,1,0:T(8,128)(2,1)}, u32[]{:S(2)}, u32[]{:S(2)}) async-start(bf16[16,24,2048]{2,1,0:T(8,128)(2,1)} %bitcast.62), calls=%async_computation.2 | async-start | bytes 3145728 | tf_op jit(solution)/shard_map/all_to_all | solution.py:400
  88.1 27.2 %all-to-all-start = ((bf16[16,24,2048]{2,1,0:T(8,128)(2,1)}), bf16[16,24,2048]{2,1,0:T(8,128)(2,1)}, u32[]{:S(2)}, u32[]{:S(2)}) async-start(bf16[16,24,2048]{2,1,0:T(8,128)(2,1)} %bitcast.64), calls=%async_computation | async-start | bytes 3145728 | tf_op jit(solution)/shard_map/all_to_all | solution.py:400
  115.3 27.2 %all-to-all-start.3 = ((bf16[16,24,2048]{2,1,0:T(8,128)(2,1)}), bf16[16,24,2048]{2,1,0:T(8,128)(2,1)}, u32[]{:S(2)}, u32[]{:S(2)}) async-start(bf16[16,24,2048]{2,1,0:T(8,128)(2,1)} %bitcast.65), calls=%async_computation.3 | async-start | bytes 3145728 | tf_op jit(solution)/shard_map/all_to_all | solution.py:400
  142.5 3.9 %copy-start.11 = (f32[64,384]{1,0:T(8,128)S(1)}, f32[64,384]{1,0:T(8,128)}, u32[]{:S(2)}) copy-start(f32[64,384]{1,0:T(8,128)} %copy.30) | copy-start | bytes 294916
  142.5 3.9 %copy-start.12 = (bf16[64,384]{1,0:T(8,128)(2,1)S(1)}, bf16[64,384]{1,0:T(8,128)(2,1)}, u32[]{:S(2)}) copy-start(bf16[64,384]{1,0:T(8,128)(2,1)} %get-tuple-element.17) | copy-start | bytes 147460
  142.5 26.6 %all-to-all-start.1 = ((bf16[16,24,2048]{2,1,0:T(8,128)(2,1)}), bf16[16,24,2048]{2,1,0:T(8,128)(2,1)S(1)}, u32[]{:S(2)}, u32[]{:S(2)}) async-start(bf16[16,24,2048]{2,1,0:T(8,128)(2,1)} %bitcast.63), calls=%async_computation.1 | async-start | bytes 3145728 | tf_op jit(solution)/shard_map/all_to_all | solution.py:400
  146.5 22.7 %copy-start.13 = (bf16[64,384]{1,0:T(8,128)(2,1)S(1)}, bf16[64,384]{1,0:T(8,128)(2,1)}, u32[]{:S(2)}) copy-start(bf16[64,384]{1,0:T(8,128)(2,1)} %get-tuple-element.19) | copy-start | bytes 147460
  148.4 25.4 %copy-start.10 = (f32[64,2048]{1,0:T(8,128)S(1)}, f32[64,2048]{1,0:T(8,128)}, u32[]{:S(2)}) copy-start(f32[64,2048]{1,0:T(8,128)} %copy-done.9) | copy-start | bytes 1572868
  148.4 25.4 %collective-permute-start.12 = (bf16[64,2048]{1,0:T(8,128)(2,1)S(1)}, bf16[64,2048]{1,0:T(8,128)(2,1)S(1)}, u32[]{:S(2)}, u32[]{:S(2)}) collective-permute-start(bf16[64,2048]{1,0:T(8,128)(2,1)S(1)} %fusion.6), channel_id=1, source_target_pairs={{0,24},{1,25},{2,26},{3,27},{4,28},{5,29},{6,30},{7,31},{8,16},{9,... | collective-permute-start | bytes 786440 | tf_op jit(solution)/shard_map/ppermute | solution.py:454

commit v6 on v5

--- a/solution.py
+++ b/solution.py
@@ -2,6 +2,7 @@
 
 import jax
 import jax.numpy as jnp
+import numpy as np
 from jax import lax
 from jax.experimental import pallas as pl
 from jax.experimental.pallas import tpu as pltpu
@@ -22,9 +23,15 @@
     return vectors * lax.rsqrt(mean_sq + EPSILON) * gain_vector
 
 
-def turn(vectors, cos_ref, sin_ref):
-    half = vectors.shape[-1] // 2
-    return vectors * cos_ref[...] + pltpu.roll(vectors, half, 1) * sin_ref[...]
+def spread(table):
+    half = table.shape[-1] // 2
+    turned = pltpu.roll(table, half, 1)
+    front = lax.broadcasted_iota(jnp.int32, table.shape, 1) < half
+    return jnp.where(front, table, turned), jnp.where(front, -turned, table)
+
+
+def turn(vectors, cosine, sine):
+    return vectors * cosine + pltpu.roll(vectors, vectors.shape[-1] // 2, 1) * sine
 
 
 def room(mib):
@@ -32,27 +39,32 @@
 
 
 def first_kernel(*refs):
-    hbm, (kv_ref,), held, sems = refs[:7], refs[7:8], refs[8:15], refs[15]
-    x_ref, wk_ref, wv_ref, gain_ref, kgain_ref, cos_ref, sin_ref = held
+    hbm, kv_ref, held, sems = refs[:6], refs[6], refs[7:13], refs[13]
+    x_ref, wk_ref, wv_ref, gain_ref, kgain_ref, table_ref = held
     rows, head_dim = x_ref.shape[0], wk_ref.shape[1]
     half = rows // 2
     upper, lower = pl.ds(0, half), pl.ds(half, half)
-    copies = [pltpu.make_async_copy(a, b, sems.at[i]) for i, (a, b) in enumerate(zip(hbm, held))]
-    copies[0] = pltpu.make_async_copy(hbm[0].at[upper], x_ref.at[upper], sems.at[0])
-    copies.append(pltpu.make_async_copy(hbm[0].at[lower], x_ref.at[lower], sems.at[7]))
-    for i in (3, 0, 7, 1, 4, 5, 6, 2):
+    mine = pl.ds(pl.multiple_of(lax.axis_index("seq") * rows, rows), rows)
+    pieces = [
+        (hbm[0].at[upper], x_ref.at[upper]),
+        *zip(hbm[1:5], held[1:5]),
+        (hbm[5].at[mine], table_ref),
+        (hbm[0].at[lower], x_ref.at[lower]),
+    ]
+    copies = [pltpu.make_async_copy(a, b, sems.at[i]) for i, (a, b) in enumerate(pieces)]
+    for i in (3, 0, 6, 1, 4, 5, 2):
         copies[i].start()
     copies[3].wait()
     normed = []
-    for i in (0, 7):
+    for i in (0, 6):
         copies[i].wait()
         part = x_ref[upper if i == 0 else lower, :].astype(jnp.float32)
         normed.append(rms_scale(part, gain_ref[...]).astype(jnp.bfloat16))
     normed = jnp.concatenate(normed, axis=0)
-    for i in (1, 4, 5, 6):
+    for i in (1, 4, 5):
         copies[i].wait()
     keys = jnp.dot(normed, wk_ref[...], preferred_element_type=jnp.float32)
-    keys = turn(rms_scale(keys, kgain_ref[...]), cos_ref, sin_ref)
+    keys = turn(rms_scale(keys, kgain_ref[...]), *spread(table_ref[...]))
     kv_ref[:rows, :] = keys.astype(jnp.bfloat16)
     copies[2].wait()
     values = jnp.dot(normed, wv_ref[...], preferred_element_type=jnp.float32)
@@ -60,7 +72,10 @@
         kv_ref[rows + i : rows + i + head_dim, :] = values[i : i + head_dim, :].T.astype(jnp.bfloat16)
 
 
-def query_kernel(head_dim, step, x_ref, gain_ref, wq_ref, qgain_ref, cos_ref, sin_ref, q_ref):
+def query_kernel(head_dim, step, x_ref, gain_ref, wq_ref, qgain_ref, table_ref, q_ref):
+    rows = x_ref.shape[0]
+    mine = pl.ds(pl.multiple_of(lax.axis_index("seq") * rows, rows), rows)
+    cosine, sine = spread(table_ref[mine, :])
     normed = rms_scale(x_ref[...].astype(jnp.float32), gain_ref[...]).astype(jnp.bfloat16)
     for start in range(0, wq_ref.shape[1], step):
         wide = jnp.dot(
@@ -68,7 +83,7 @@
         )
         for i in range(0, step, head_dim):
             q_ref[:, start + i : start + i + head_dim] = turn(
-                rms_scale(wide[:, i : i + head_dim], qgain_ref[...]), cos_ref, sin_ref
+                rms_scale(wide[:, i : i + head_dim], qgain_ref[...]), cosine, sine
             ).astype(jnp.bfloat16)
 
 
@@ -268,23 +283,21 @@
     make_pairs = functools.partial(pairs, seq_count, head_count)
 
     half_dim = head_dim // 2
-    offset = seq_index * tok_rows
-    positions = (offset + jnp.arange(tok_rows, dtype=jnp.int32)).astype(jnp.float32)
-    frequency = THETA ** (-jnp.arange(half_dim, dtype=jnp.float32) * 2.0 / head_dim)
-    angles = positions[:, None] * frequency[None, :]
-    cosine, sine = jnp.cos(angles), jnp.sin(angles)
-    cos_table = jnp.concatenate([cosine, cosine], axis=1)
-    sin_table = jnp.concatenate([-sine, sine], axis=1)
-
-    first_in = (
-        tokens, w_key, w_value, input_gain[None], key_gain[None], cos_table, sin_table
+    places = np.arange(seq_count * tok_rows, dtype=np.float32)
+    frequency = np.float32(THETA) ** (
+        -np.arange(half_dim, dtype=np.float32) * np.float32(2.0) / np.float32(head_dim)
     )
+    angles = (places[:, None] * frequency[None, :]).astype(np.float64)
+    table = jnp.asarray(np.concatenate([np.cos(angles), np.sin(angles)], axis=1), jnp.float32)
+
+    first_in = (tokens, w_key, w_value, input_gain[None], key_gain[None], table)
     own_kv = pl.pallas_call(
         first_kernel,
         out_shape=jax.ShapeDtypeStruct((2 * tok_rows, head_dim), jnp.bfloat16),
         in_specs=[ANY] * len(first_in),
         out_specs=VMEM,
-        scratch_shapes=[pltpu.VMEM(x.shape, x.dtype) for x in first_in]
+        scratch_shapes=[pltpu.VMEM(x.shape, x.dtype) for x in first_in[:-1]]
+        + [pltpu.VMEM((tok_rows, head_dim), jnp.float32)]
         + [pltpu.SemaphoreType.DMA((len(first_in) + 1,))],
         name="norm_kv",
     )(*first_in)
@@ -335,11 +348,11 @@
     rot_q = pl.pallas_call(
         functools.partial(query_kernel, head_dim, query_step),
         out_shape=jax.ShapeDtypeStruct((tok_rows, w_query.shape[1]), jnp.bfloat16),
-        in_specs=[VMEM] * 6,
+        in_specs=[VMEM] * 5,
         out_specs=VMEM,
-        compiler_params=room(12),
+        compiler_params=room(16),
         name="queries",
-    )(tokens, input_gain[None], w_query, query_gain[None], cos_table, sin_table)
+    )(tokens, input_gain[None], w_query, query_gain[None], table)
 
     near = line // 2
     if side == 2:

time: 175 us -> 174 us (level)
  no operation moved by 1% of the time
where the time goes in v6:
time: 174 us; the launch traced here: 173 us
  waiting for transfers between devices  73.9 us (42%)
  starting transfers between devices  41.9 us (24%)
  Pallas kernels  31.9 us (18%)
  local copies, waits for them, and re-layouts  12.8 us (7%)
  other arithmetic  6.6 us (4%)
  matrix products  5.79 us (3%)
    all_to_all x4, waiting for transfers between devices, exchange(): lax.all_to_all(rows.reshape(members, local_count * capacity, width), BOTH...  61.7 us
    all_to_all x4, starting transfers between devices, exchange(): lax.all_to_all(rows.reshape(members, local_count * capacity, width), BOTH...  20.3 us
    pallas_call x2, Pallas kernels, run_experts(): pl.pallas_call(expert_kernel, out_shape=jax.ShapeDtypeStruct((rows, width...  14.6 us
    pallas_call x4, Pallas kernels, attend(): pl.pallas_call(functools.partial(attend_kernel, head_dim, blocks, not sta...  9.32 us
    ppermute x3, starting transfers between devices, body(): kv_blocks.append(lax.ppermute(own_kv, BOTH, up))  7.06 us
    ppermute x1, waiting for transfers between devices, body(): came = lax.ppermute(given, BOTH, shift).astype(jnp.float32)  6.61 us
    eq x8, local copies, waits for them, and re-layouts, slot_tables(): place[:, :, None]  5.5 us
    ppermute x1, waiting for transfers between devices, body(): far_sum = lax.ppermute(foreign, BOTH, mirror)  4.24 us
  transfers between devices with their start and end apart: 17, of which 10 were waited for; matrix products, arithmetic and copies ran while one was open for 11% of the time, Pallas kernels for 14%

profile of v6, /device:TPU:0, one launch (start us, length us, event | category | flops | bytes accessed | tf_op | source)
XLA Modules:
  0.0 173.3 jit_solution(8864437103219689522)
XLA Ops:
  0.0 3.4 %norm_kv.1.rest_0_ = bf16[512,128]{1,0:T(8,128)(2,1)} custom-call(bf16[256,2048]{1,0:T(8,128)(2,1)} %refs_0_.1, bf16[2048,128]{1,0:T(8,128)(2,1)} %refs_1_.1, bf16[2048,128]{1,0:T(8,128)(2,1)} %refs_2_.1, f32[1,2048]{1,0:T(1,128)} %bitcast.55, f32[1,128]{1,0:T(1,128)} %bitcast.73, f32[2048,128]{1,0:T(8,128)} %constant.105.clone.table_ref.refs_5_), custom_call_target="tpu_custom_call" | custom-call | tf_op jit(solution)/shard_map/norm_kv/pallas_call | solution.py:294
  3.5 3.1 %collective-permute-start.4 = (bf16[512,128]{1,0:T(8,128)(2,1)}, bf16[512,128]{1,0:T(8,128)(2,1)S(1)}, u32[]{:S(2)}, u32[]{:S(2)}) collective-permute-start(bf16[512,128]{1,0:T(8,128)(2,1)} %norm_kv.1.rest_0_), channel_id=1, source_target_pairs={{0,8},{1,9},{2,10},{3,11},{4,12},{5,13},{6,14},{7,15},{8,16},{9,17... | collective-permute-start | bytes 393224 | tf_op jit(solution)/shard_map/ppermute | solution.py:308
  6.6 1.5 collective-permute-start.6
  8.1 2.6 %collective-permute-start.2 = (bf16[512,128]{1,0:T(8,128)(2,1)}, bf16[512,128]{1,0:T(8,128)(2,1)S(1)}, u32[]{:S(2)}, u32[]{:S(2)}) collective-permute-start(bf16[512,128]{1,0:T(8,128)(2,1)} %norm_kv.1.rest_0_), channel_id=1, source_target_pairs={{0,16},{1,17},{2,18},{3,19},{4,20},{5,21},{6,22},{7,23},{8,24},{9,... | collective-permute-start | bytes 393224 | tf_op jit(solution)/shard_map/ppermute | solution.py:308
  10.7 1.3 collective-permute-start
  12.1 0.5 collective-permute-start.10
  12.8 0.1 eq.92
  13.0 2.2 %copy-done.2 = bf16[2048,1024]{1,0:T(8,128)(2,1)S(1)} copy-done((bf16[2048,1024]{1,0:T(8,128)(2,1)S(1)}, bf16[2048,1024]{1,0:T(8,128)(2,1)}, u32[]{:S(2)}) %copy-start.2) | copy-done | bytes 4194328
  15.2 1.8 %queries.1.q_ref = bf16[256,1024]{1,0:T(8,128)(2,1)S(1)} custom-call(bf16[256,2048]{1,0:T(8,128)(2,1)S(1)} %copy-done.1, f32[1,2048]{1,0:T(1,128)S(1)} %bitcast.56, bf16[2048,1024]{1,0:T(8,128)(2,1)S(1)} %copy-done.2, f32[1,128]{1,0:T(1,128)S(1)} %bitcast.57, f32[2048,128]{1,0:T(8,128)S(1)} %copy-done.3), custom_call_target="tpu_custom_call" | custom-call | tf_op jit(solution)/shard_map/queries/pallas_call | solution.py:348
  17.0 0.6 collective-permute-start.5
  17.6 0.6 collective-permute-done.2.rest_0_
  18.2 1.5 collective-permute-start.3
  19.7 0.6 collective-permute-start.1
  20.2 2.9 %attend.4 = (f32[8,8,256]{2,1,0:T(8,128)S(1)}, f32[8,128,256]{2,1,0:T(8,128)S(1)}) custom-call(f32[3]{0:T(128)S(1)} %pad_maximum_fusion.3.bias_ref, bf16[256,1024]{1,0:T(8,128)(2,1)S(1)} %queries.1.q_ref, bf16[512,128]{1,0:T(8,128)(2,1)S(1)} %copy-done.4, bf16[512,128]{1,0:T(8,128)(2,1)S(1)} %collective-permute-done.4.rest_1_, ...), custom_call_target="tpu_custom_call" | custom-call | tf_op jit(solution)/shard_map/attend/pallas_call | solution.py:161
  23.1 0.2 collective-permute-done.5.rest_1_
  23.3 2.4 %attend.5 = (f32[8,8,256]{2,1,0:T(8,128)S(1)}, f32[8,128,256]{2,1,0:T(8,128)S(1)}) custom-call(f32[2]{0:T(128)S(1)} %pad_maximum_fusion.2.bias_ref, bf16[256,1024]{1,0:T(8,128)(2,1)S(1)} %queries.1.q_ref, bf16[512,128]{1,0:T(8,128)(2,1)S(1)} %collective-permute-done.2.rest_0_, bf16[512,128]{1,0:T(8,128)(2,1)S(1)} %collective-permute-done.5.rest_1_, ...), custom_call_target="tpu_custom_call" | custom-call | tf_op jit(solution)/shard_map/attend/pallas_call | solution.py:161
  25.8 0.4 collective-permute-done.3.rest_1_
  26.1 2.5 %attend.6 = (f32[8,8,256]{2,1,0:T(8,128)S(1)}, f32[8,128,256]{2,1,0:T(8,128)S(1)}) custom-call(f32[2]{0:T(128)S(1)} %pad_maximum_fusion.1.bias_ref, bf16[256,1024]{1,0:T(8,128)(2,1)S(1)} %queries.1.q_ref, bf16[512,128]{1,0:T(8,128)(2,1)S(1)} %collective-permute-done.rest_0_, bf16[512,128]{1,0:T(8,128)(2,1)S(1)} %collective-permute-done.3.rest_1_, ...), custom_call_target="tpu_custom_call" | custom-call | tf_op jit(solution)/shard_map/attend/pallas_call | solution.py:161
  28.6 1.6 attend.7
  30.2 0.7 fusion
  31.1 0.7 fusion.2
  31.9 0.6 collective-permute-start.7
  32.4 0.2 collective-permute-done.8
  32.7 1.6 collective-permute-start.9
  34.2 0.1 fusion.25
  34.3 0.1 fusion.4
  34.5 6.6 %collective-permute-done.9 = bf16[64,2048]{1,0:T(8,128)(2,1)S(1)} collective-permute-done((bf16[64,2048]{1,0:T(8,128)(2,1)S(1)}, bf16[64,2048]{1,0:T(8,128)(2,1)S(1)}, u32[]{:S(2)}, u32[]{:S(2)}) %collective-permute-start.9) | collective-permute-done | bytes 262176 | tf_op jit(solution)/shard_map/ppermute | solution.py:401
  41.1 1.2 multiply_reduce_fusion
  42.3 0.8 copy-done.8
  43.1 0.1 multiply_convert_fusion
  43.2 4.0 %collective-permute-start.11 = (bf16[64,2048]{1,0:T(8,128)(2,1)S(1)}, bf16[64,2048]{1,0:T(8,128)(2,1)}, u32[]{:S(2)}, u32[]{:S(2)}) collective-permute-start(bf16[64,2048]{1,0:T(8,128)(2,1)S(1)} %multiply_convert_fusion), channel_id=1, source_target_pairs={{0,24},{1,25},{2,26},{3,27},{4,28},{5,29},{6,30},{7,31},{8,16},{9,... | collective-permute-start | bytes 786440 | tf_op jit(solution)/shard_map/ppermute | solution.py:445
  47.2 0.1 fusion.26
  47.3 0.7 broadcast_in_dim.84
  48.0 1.0 copy.33
  49.0 0.7 eq.89
  49.7 1.7 copy.32
  51.4 1.5 select_convert_fusion
  52.9 0.6 convert_element_type.116.pick_ref
  53.5 2.7 %fill.1 = bf16[384,2048]{1,0:T(8,128)(2,1)} custom-call(bf16[64,2048]{1,0:T(8,128)(2,1)} %collective-permute-done.11.rows_ref, bf16[64,384]{1,0:T(8,128)(2,1)} %convert_element_type.116.pick_ref, bf16[2048,768]{1,0:T(8,128)(2,1)S(1)} %bitcast.51), custom_call_target="tpu_custom_call" | custom-call | tf_op jit(solution)/shard_map/fill/pallas_call | solution.py:456
  56.2 7.7 %all-to-all-start.2 = ((bf16[16,24,2048]{2,1,0:T(8,128)(2,1)}), bf16[16,24,2048]{2,1,0:T(8,128)(2,1)}, u32[]{:S(2)}, u32[]{:S(2)}) async-start(bf16[16,24,2048]{2,1,0:T(8,128)(2,1)} %bitcast.62), calls=%async_computation.2 | async-start | bytes 3145728 | tf_op jit(solution)/shard_map/all_to_all | solution.py:413
  63.9 0.1 fusion.24
  64.0 0.7 broadcast_in_dim.80
  64.7 1.7 copy.31
  66.4 0.1 fusion.23
  66.5 0.1 fusion.5
  66.6 0.7 eq.80
  67.3 1.7 copy.30
  69.0 0.7 eq.83
  69.7 1.6 select_convert_fusion.1
  71.2 1.8 %convolution_convert_fusion = bf16[384,2048]{1,0:T(8,128)(2,1)} fusion(pred[64,384]{1,0:T(32,128)(4,1)S(1)} %get-tuple-element.20, bf16[64,2048]{1,0:T(8,128)(2,1)S(1)} %multiply_convert_fusion), kind=kOutput, calls=%fused_computation.4 | convolution fusion | flops 101449728 | bytes 1859584 | tf_op jit(solution)/shard_map/dot_general | solution.py:431
  73.0 13.7 %all-to-all-done.2 = bf16[16,24,2048]{2,1,0:T(8,128)(2,1)} async-done(((bf16[16,24,2048]{2,1,0:T(8,128)(2,1)}), bf16[16,24,2048]{2,1,0:T(8,128)(2,1)}, u32[]{:S(2)}, u32[]{:S(2)}) %all-to-all-start.2) | async-done | bytes 1572896 | tf_op jit(solution)/shard_map/all_to_all | solution.py:413
  86.8 4.4 %all-to-all-start = ((bf16[16,24,2048]{2,1,0:T(8,128)(2,1)}), bf16[16,24,2048]{2,1,0:T(8,128)(2,1)}, u32[]{:S(2)}, u32[]{:S(2)}) async-start(bf16[16,24,2048]{2,1,0:T(8,128)(2,1)} %bitcast.64), calls=%async_computation | async-start | bytes 3145728 | tf_op jit(solution)/shard_map/all_to_all | solution.py:413
  91.2 7.3 %experts.3 = bf16[384,2048]{1,0:T(8,128)(2,1)} custom-call(bf16[384,2048]{1,0:T(8,128)(2,1)} %bitcast.27.x_hbm, bf16[2048,768]{1,0:T(8,128)(2,1)S(1)} %bitcast.52, bf16[2048,768]{1,0:T(8,128)(2,1)} %bitcast.58, bf16[768,2048]{1,0:T(8,128)(2,1)} %bitcast.60), custom_call_target="tpu_custom_call" | custom-call | tf_op jit(solution)/shard_map/experts/pallas_call | solution.py:215
  98.5 15.5 %all-to-all-done = bf16[16,24,2048]{2,1,0:T(8,128)(2,1)} async-done(((bf16[16,24,2048]{2,1,0:T(8,128)(2,1)}), bf16[16,24,2048]{2,1,0:T(8,128)(2,1)}, u32[]{:S(2)}, u32[]{:S(2)}) %all-to-all-start) | async-done | bytes 1572896 | tf_op jit(solution)/shard_map/all_to_all | solution.py:413
  114.0 4.4 %all-to-all-start.3 = ((bf16[16,24,2048]{2,1,0:T(8,128)(2,1)}), bf16[16,24,2048]{2,1,0:T(8,128)(2,1)}, u32[]{:S(2)}, u32[]{:S(2)}) async-start(bf16[16,24,2048]{2,1,0:T(8,128)(2,1)} %bitcast.65), calls=%async_computation.3 | async-start | bytes 3145728 | tf_op jit(solution)/shard_map/all_to_all | solution.py:413
  118.4 7.3 %experts.2 = bf16[384,2048]{1,0:T(8,128)(2,1)} custom-call(bf16[384,2048]{1,0:T(8,128)(2,1)} %bitcast.18.x_hbm, bf16[2048,768]{1,0:T(8,128)(2,1)S(1)} %bitcast.53, bf16[2048,768]{1,0:T(8,128)(2,1)} %bitcast.59, bf16[768,2048]{1,0:T(8,128)(2,1)} %bitcast.61), custom_call_target="tpu_custom_call" | custom-call | tf_op jit(solution)/shard_map/experts/pallas_call | solution.py:215
  125.7 15.5 %all-to-all-done.3 = bf16[16,24,2048]{2,1,0:T(8,128)(2,1)} async-done(((bf16[16,24,2048]{2,1,0:T(8,128)(2,1)}), bf16[16,24,2048]{2,1,0:T(8,128)(2,1)}, u32[]{:S(2)}, u32[]{:S(2)}) %all-to-all-start.3) | async-done | bytes 1572896 | tf_op jit(solution)/shard_map/all_to_all | solution.py:413
  141.2 3.8 %all-to-all-start.1 = ((bf16[16,24,2048]{2,1,0:T(8,128)(2,1)}), bf16[16,24,2048]{2,1,0:T(8,128)(2,1)S(1)}, u32[]{:S(2)}, u32[]{:S(2)}) async-start(bf16[16,24,2048]{2,1,0:T(8,128)(2,1)} %bitcast.63), calls=%async_computation.1 | async-start | bytes 3145728 | tf_op jit(solution)/shard_map/all_to_all | solution.py:413
  145.1 1.9 %fusion.19 = f32[128,2048]{1,0:T(8,128)S(1)} fusion(bf16[384,2048]{1,0:T(8,128)(2,1)} %bitcast.29, bf16[64,384]{1,0:T(8,128)(2,1)S(1)} %subtract_convert_fusion, bf16[64,384]{1,0:T(8,128)(2,1)S(1)} %copy-done.11), kind=kOutput, calls=%fused_computation.30 | convolution fusion | flops 201523200 | bytes 2719744 | tf_op jit(solution)/shard_map/dot_general | solution.py:439
  147.1 3.7 %collective-permute-start.12 = (bf16[64,2048]{1,0:T(8,128)(2,1)S(1)}, bf16[64,2048]{1,0:T(8,128)(2,1)S(1)}, u32[]{:S(2)}, u32[]{:S(2)}) collective-permute-start(bf16[64,2048]{1,0:T(8,128)(2,1)S(1)} %fusion.6), channel_id=1, source_target_pairs={{0,24},{1,25},{2,26},{3,27},{4,28},{5,29},{6,30},{7,31},{8,16},{9,... | collective-permute-start | bytes 786440 | tf_op jit(solution)/shard_map/ppermute | solution.py:467
  150.8 17.0 %all-to-all-done.1 = bf16[16,24,2048]{2,1,0:T(8,128)(2,1)S(1)} async-done(((bf16[16,24,2048]{2,1,0:T(8,128)(2,1)}), bf16[16,24,2048]{2,1,0:T(8,128)(2,1)S(1)}, u32[]{:S(2)}, u32[]{:S(2)}) %all-to-all-start.1) | async-done | bytes 1572896 | tf_op jit(solution)/shard_map/all_to_all | solution.py:413
  167.8 0.4 fusion.15
  168.2 4.2 %collective-permute-done.12 = bf16[64,2048]{1,0:T(8,128)(2,1)S(1)} collective-permute-done((bf16[64,2048]{1,0:T(8,128)(2,1)S(1)}, bf16[64,2048]{1,0:T(8,128)(2,1)S(1)}, u32[]{:S(2)}, u32[]{:S(2)}) %collective-permute-start.12) | collective-permute-done | bytes 262176 | tf_op jit(solution)/shard_map/ppermute | solution.py:467
  172.5 0.8 fusion.9
  (59 shorter events, 0.7 us)
Async XLA Ops:
  0.0 12.0 %copy-start.14 = (f32[64,8]{0,1:T(8,128)S(1)}, f32[64,8]{0,1:T(8,128)}, u32[]{:S(2)}) copy-start(f32[64,8]{0,1:T(8,128)} %param.25) | copy-start | bytes 6148
  0.0 12.1 %copy-start.13 = (s32[64,8]{0,1:T(8,128)S(1)}, s32[64,8]{0,1:T(8,128)}, u32[]{:S(2)}) copy-start(s32[64,8]{0,1:T(8,128)} %param.24) | copy-start | bytes 6148
  0.0 12.9 %copy-start.1 = (bf16[256,2048]{1,0:T(8,128)(2,1)S(1)}, bf16[256,2048]{1,0:T(8,128)(2,1)}, u32[]{:S(2)}) copy-start(bf16[256,2048]{1,0:T(8,128)(2,1)} %refs_0_.1) | copy-start | bytes 3145732
  0.0 12.9 %copy-start.3 = (f32[2048,128]{1,0:T(8,128)S(1)}, f32[2048,128]{1,0:T(8,128)}, u32[]{:S(2)}) copy-start(f32[2048,128]{1,0:T(8,128)} %constant.105.clone.table_ref.refs_5_) | copy-start | bytes 3145732
  0.0 12.9 %copy-start.5 = (f32[2048]{0:T(1024)S(1)}, f32[2048]{0:T(1024)}, u32[]{:S(2)}) copy-start(f32[2048]{0:T(1024)} %param.16) | copy-start | bytes 24580
  0.0 12.9 %copy-start.6 = (f32[128]{0:T(128)S(1)}, f32[128]{0:T(128)}, u32[]{:S(2)}) copy-start(f32[128]{0:T(128)} %param.20) | copy-start | bytes 1540
  3.5 13.5 %collective-permute-start.4 = (bf16[512,128]{1,0:T(8,128)(2,1)}, bf16[512,128]{1,0:T(8,128)(2,1)S(1)}, u32[]{:S(2)}, u32[]{:S(2)}) collective-permute-start(bf16[512,128]{1,0:T(8,128)(2,1)} %norm_kv.1.rest_0_), channel_id=1, source_target_pairs={{0,8},{1,9},{2,10},{3,11},{4,12},{5,13},{6,14},{7,15},{8,16},{9,17... | collective-permute-start | bytes 393224 | tf_op jit(solution)/shard_map/ppermute | solution.py:308
  6.6 13.6 %collective-permute-start.6 = (bf16[512,128]{1,0:T(8,128)(2,1)}, bf16[512,128]{1,0:T(8,128)(2,1)S(1)}, u32[]{:S(2)}, u32[]{:S(2)}) collective-permute-start(bf16[512,128]{1,0:T(8,128)(2,1)} %norm_kv.1.rest_0_), channel_id=1, source_target_pairs={{0,4},{1,5},{2,6},{3,7},{4,0},{5,1},{6,2},{7,3},{8,12},{9,13},{10,... | collective-permute-start | bytes 393224 | tf_op jit(solution)/shard_map/ppermute | solution.py:313
  8.1 10.1 %collective-permute-start.2 = (bf16[512,128]{1,0:T(8,128)(2,1)}, bf16[512,128]{1,0:T(8,128)(2,1)S(1)}, u32[]{:S(2)}, u32[]{:S(2)}) collective-permute-start(bf16[512,128]{1,0:T(8,128)(2,1)} %norm_kv.1.rest_0_), channel_id=1, source_target_pairs={{0,16},{1,17},{2,18},{3,19},{4,20},{5,21},{6,22},{7,23},{8,24},{9,... | collective-permute-start | bytes 393224 | tf_op jit(solution)/shard_map/ppermute | solution.py:308
  10.7 9.0 %collective-permute-start = (bf16[512,128]{1,0:T(8,128)(2,1)}, bf16[512,128]{1,0:T(8,128)(2,1)S(1)}, u32[]{:S(2)}, u32[]{:S(2)}) collective-permute-start(bf16[512,128]{1,0:T(8,128)(2,1)} %norm_kv.1.rest_0_), channel_id=1, source_target_pairs={{0,24},{1,25},{2,26},{3,27},{4,28},{5,29},{6,30},{7,31},{8,0},{9,1... | collective-permute-start | bytes 393224 | tf_op jit(solution)/shard_map/ppermute | solution.py:308
  12.1 8.1 %collective-permute-start.10 = (f32[64,16]{0,1:T(8,128)S(1)}, f32[64,16]{0,1:T(8,128)S(1)}, u32[]{:S(2)}, u32[]{:S(2)}) collective-permute-start(f32[64,16]{0,1:T(8,128)S(1)} %pad_maximum_fusion), channel_id=1, source_target_pairs={{0,24},{1,25},{2,26},{3,27},{4,28},{5,29},{6,30},{7,31},{8,16},{9,... | collective-permute-start | bytes 12296 | tf_op jit(solution)/shard_map/ppermute | solution.py:448
  13.0 2.2 %copy-start.2 = (bf16[2048,1024]{1,0:T(8,128)(2,1)S(1)}, bf16[2048,1024]{1,0:T(8,128)(2,1)}, u32[]{:S(2)}) copy-start(bf16[2048,1024]{1,0:T(8,128)(2,1)} %wq_ref.1) | copy-start | bytes 12582916
  15.2 5.1 %copy-start.4 = (bf16[512,128]{1,0:T(8,128)(2,1)S(1)}, bf16[512,128]{1,0:T(8,128)(2,1)}, u32[]{:S(2)}) copy-start(bf16[512,128]{1,0:T(8,128)(2,1)} %norm_kv.1.rest_0_) | copy-start | bytes 393220
  17.0 6.3 %collective-permute-start.5 = (bf16[512,128]{1,0:T(8,128)(2,1)S(1)}, bf16[512,128]{1,0:T(8,128)(2,1)S(1)}, u32[]{:S(2)}, u32[]{:S(2)}) collective-permute-start(bf16[512,128]{1,0:T(8,128)(2,1)S(1)} %collective-permute-done.4.rest_1_), channel_id=1, source_target_pairs={{0,4},{1,5},{2,6},{3,7},{4,0},{5,1},{6,2},{7,3},{8,12},{9,13},{10,... | collective-permute-start | bytes 393224 | tf_op jit(solution)/shard_map/ppermute | solution.py:313
  18.2 8.0 %collective-permute-start.3 = (bf16[512,128]{1,0:T(8,128)(2,1)S(1)}, bf16[512,128]{1,0:T(8,128)(2,1)S(1)}, u32[]{:S(2)}, u32[]{:S(2)}) collective-permute-start(bf16[512,128]{1,0:T(8,128)(2,1)S(1)} %collective-permute-done.2.rest_0_), channel_id=1, source_target_pairs={{0,4},{1,5},{2,6},{3,7},{4,0},{5,1},{6,2},{7,3},{8,12},{9,13},{10,... | collective-permute-start | bytes 393224 | tf_op jit(solution)/shard_map/ppermute | solution.py:313
  19.7 8.9 %collective-permute-start.1 = (bf16[512,128]{1,0:T(8,128)(2,1)S(1)}, bf16[512,128]{1,0:T(8,128)(2,1)S(1)}, u32[]{:S(2)}, u32[]{:S(2)}) collective-permute-start(bf16[512,128]{1,0:T(8,128)(2,1)S(1)} %collective-permute-done.rest_0_), channel_id=1, source_target_pairs={{0,4},{1,5},{2,6},{3,7},{4,0},{5,1},{6,2},{7,3},{8,12},{9,13},{10,... | collective-permute-start | bytes 393224 | tf_op jit(solution)/shard_map/ppermute | solution.py:313
  26.1 4.1 %copy-start.7 = (bf16[1024,2048]{1,0:T(8,128)(2,1)S(1)}, bf16[1024,2048]{1,0:T(8,128)(2,1)}, u32[]{:S(2)}) copy-start(bf16[1024,2048]{1,0:T(8,128)(2,1)} %param.22) | copy-start | bytes 12582916
  31.0 1.6 collective-permute-start.8
  31.9 11.2 %copy-start.15 = (f32[2048]{0:T(1024)S(1)}, f32[2048]{0:T(1024)}, u32[]{:S(2)}) copy-start(f32[2048]{0:T(1024)} %param.23) | copy-start | bytes 24580
  31.9 2.6 %collective-permute-start.7 = (bf16[64,2048]{1,0:T(8,128)(2,1)S(1)}, bf16[64,2048]{1,0:T(8,128)(2,1)S(1)}, u32[]{:S(2)}, u32[]{:S(2)}) collective-permute-start(bf16[64,2048]{1,0:T(8,128)(2,1)S(1)} %fusion.13), channel_id=1, source_target_pairs={{0,1},{1,0},{2,3},{3,2},{4,5},{5,4},{6,7},{7,6},{8,9},{9,8},{10,11... | collective-permute-start | bytes 786440 | tf_op jit(solution)/shard_map/ppermute | solution.py:394
  32.7 8.4 %collective-permute-start.9 = (bf16[64,2048]{1,0:T(8,128)(2,1)S(1)}, bf16[64,2048]{1,0:T(8,128)(2,1)S(1)}, u32[]{:S(2)}, u32[]{:S(2)}) collective-permute-start(bf16[64,2048]{1,0:T(8,128)(2,1)S(1)} %fusion.10), channel_id=1, source_target_pairs={{0,2},{1,3},{2,0},{3,1},{4,6},{5,7},{6,4},{7,5},{8,10},{9,11},{10,... | collective-permute-start | bytes 786440 | tf_op jit(solution)/shard_map/ppermute | solution.py:401
  34.5 19.1 %copy-start = (bf16[1,2048,768]{2,1,0:T(8,128)(2,1)S(1)}, bf16[1,2048,768]{2,1,0:T(8,128)(2,1)}, u32[]{:S(2)}) copy-start(bf16[1,2048,768]{2,1,0:T(8,128)(2,1)} %param.26) | copy-start | bytes 9437188
  42.3 0.8 copy-start.8
  43.2 10.3 %collective-permute-start.11 = (bf16[64,2048]{1,0:T(8,128)(2,1)S(1)}, bf16[64,2048]{1,0:T(8,128)(2,1)}, u32[]{:S(2)}, u32[]{:S(2)}) collective-permute-start(bf16[64,2048]{1,0:T(8,128)(2,1)S(1)} %multiply_convert_fusion), channel_id=1, source_target_pairs={{0,24},{1,25},{2,26},{3,27},{4,28},{5,29},{6,30},{7,31},{8,16},{9,... | collective-permute-start | bytes 786440 | tf_op jit(solution)/shard_map/ppermute | solution.py:445
  56.2 30.5 %all-to-all-start.2 = ((bf16[16,24,2048]{2,1,0:T(8,128)(2,1)}), bf16[16,24,2048]{2,1,0:T(8,128)(2,1)}, u32[]{:S(2)}, u32[]{:S(2)}) async-start(bf16[16,24,2048]{2,1,0:T(8,128)(2,1)} %bitcast.62), calls=%async_computation.2 | async-start | bytes 3145728 | tf_op jit(solution)/shard_map/all_to_all | solution.py:413
  86.8 27.2 %all-to-all-start = ((bf16[16,24,2048]{2,1,0:T(8,128)(2,1)}), bf16[16,24,2048]{2,1,0:T(8,128)(2,1)}, u32[]{:S(2)}, u32[]{:S(2)}) async-start(bf16[16,24,2048]{2,1,0:T(8,128)(2,1)} %bitcast.64), calls=%async_computation | async-start | bytes 3145728 | tf_op jit(solution)/shard_map/all_to_all | solution.py:413
  114.0 27.2 %all-to-all-start.3 = ((bf16[16,24,2048]{2,1,0:T(8,128)(2,1)}), bf16[16,24,2048]{2,1,0:T(8,128)(2,1)}, u32[]{:S(2)}, u32[]{:S(2)}) async-start(bf16[16,24,2048]{2,1,0:T(8,128)(2,1)} %bitcast.65), calls=%async_computation.3 | async-start | bytes 3145728 | tf_op jit(solution)/shard_map/all_to_all | solution.py:413
  141.2 3.9 %copy-start.10 = (f32[64,384]{1,0:T(8,128)S(1)}, f32[64,384]{1,0:T(8,128)}, u32[]{:S(2)}) copy-start(f32[64,384]{1,0:T(8,128)} %copy.31) | copy-start | bytes 294916
  141.2 3.9 %copy-start.11 = (bf16[64,384]{1,0:T(8,128)(2,1)S(1)}, bf16[64,384]{1,0:T(8,128)(2,1)}, u32[]{:S(2)}) copy-start(bf16[64,384]{1,0:T(8,128)(2,1)} %get-tuple-element.17) | copy-start | bytes 147460
  141.2 26.6 %all-to-all-start.1 = ((bf16[16,24,2048]{2,1,0:T(8,128)(2,1)}), bf16[16,24,2048]{2,1,0:T(8,128)(2,1)S(1)}, u32[]{:S(2)}, u32[]{:S(2)}) async-start(bf16[16,24,2048]{2,1,0:T(8,128)(2,1)} %bitcast.63), calls=%async_computation.1 | async-start | bytes 3145728 | tf_op jit(solution)/shard_map/all_to_all | solution.py:413
  145.1 22.7 %copy-start.12 = (bf16[64,384]{1,0:T(8,128)(2,1)S(1)}, bf16[64,384]{1,0:T(8,128)(2,1)}, u32[]{:S(2)}) copy-start(bf16[64,384]{1,0:T(8,128)(2,1)} %get-tuple-element.19) | copy-start | bytes 147460
  147.0 25.4 %copy-start.9 = (f32[64,2048]{1,0:T(8,128)S(1)}, f32[64,2048]{1,0:T(8,128)}, u32[]{:S(2)}) copy-start(f32[64,2048]{1,0:T(8,128)} %copy-done.8) | copy-start | bytes 1572868
  147.1 25.4 %collective-permute-start.12 = (bf16[64,2048]{1,0:T(8,128)(2,1)S(1)}, bf16[64,2048]{1,0:T(8,128)(2,1)S(1)}, u32[]{:S(2)}, u32[]{:S(2)}) collective-permute-start(bf16[64,2048]{1,0:T(8,128)(2,1)S(1)} %fusion.6), channel_id=1, source_target_pairs={{0,24},{1,25},{2,26},{3,27},{4,28},{5,29},{6,30},{7,31},{8,16},{9,... | collective-permute-start | bytes 786440 | tf_op jit(solution)/shard_map/ppermute | solution.py:467

commit v7 on v6

--- a/solution.py
+++ b/solution.py
@@ -228,6 +228,13 @@
     return made[0][None] if experts == 1 else jnp.stack(made)
 
 
+def finish_kernel(mix_ref, came_ref, far_ref, residual_ref, out_ref):
+    rows = residual_ref.shape[0]
+    both = jnp.dot(mix_ref[...], came_ref[...], preferred_element_type=jnp.float32)
+    expert_sum = both[:rows] + both[rows:] + far_ref[...].astype(jnp.float32)
+    out_ref[...] = (residual_ref[...] + expert_sum).astype(jnp.bfloat16)
+
+
 def fill_kernel(rows_ref, pick_ref, gate_ref, out_ref):
     del gate_ref
     out_ref[...] = lax.dot_general(
@@ -465,8 +472,17 @@
         far_result = run_experts(far_rows_in, *weights)
         foreign = give_back(far_result, tables[1][1]).astype(jnp.bfloat16)
         far_sum = lax.ppermute(foreign, BOTH, mirror)
-        expert_sum = give_back(own_result, tables[0][1])
-        expert_sum = expert_sum + far_sum.astype(jnp.float32)
+        came_back = exchange(
+            own_result.reshape(local_count, members, capacity, width).transpose(1, 0, 2, 3)
+        ).reshape(slots, width)
+        return pl.pallas_call(
+            finish_kernel,
+            out_shape=jax.ShapeDtypeStruct((rows_here, width), jnp.bfloat16),
+            in_specs=[VMEM] * 4,
+            out_specs=VMEM,
+            compiler_params=room(16),
+            name="finish",
+        )(tables[0][1], came_back, far_sum, residual)
     else:
         result = run_experts(dispatch(fill_slots(routed, tables[0][0])), *weights)
         expert_sum = give_back(result, tables[0][1])

time: 174 us -> 174 us (level)
  no operation moved by 1% of the time
where the time goes in v7:
time: 174 us
  waiting for transfers between devices  74.4 us (43%)
  starting transfers between devices  41.7 us (24%)
  Pallas kernels  33.1 us (19%)
  local copies, waits for them, and re-layouts  12.8 us (7%)
  other arithmetic  5.81 us (3%)
  matrix products  5.38 us (3%)
    all_to_all x4, waiting for transfers between devices, exchange(): lax.all_to_all(rows.reshape(members, local_count * capacity, width), BOTH...  61.6 us
    all_to_all x4, starting transfers between devices, exchange(): lax.all_to_all(rows.reshape(members, local_count * capacity, width), BOTH...  20.3 us
    pallas_call x2, Pallas kernels, run_experts(): pl.pallas_call(expert_kernel, out_shape=jax.ShapeDtypeStruct((rows, width...  14.7 us
    pallas_call x4, Pallas kernels, attend(): pl.pallas_call(functools.partial(attend_kernel, head_dim, blocks, not sta...  9.28 us
    ppermute x3, starting transfers between devices, body(): kv_blocks.append(lax.ppermute(own_kv, BOTH, up))  7.06 us
    ppermute x1, waiting for transfers between devices, body(): came = lax.ppermute(given, BOTH, shift).astype(jnp.float32)  6.61 us
    eq x8, local copies, waits for them, and re-layouts, slot_tables(): place[:, :, None]  5.5 us
    ppermute x1, waiting for transfers between devices, body(): far_sum = lax.ppermute(foreign, BOTH, mirror)  4.67 us
  transfers between devices with their start and end apart: 17, of which 10 were waited for; matrix products, arithmetic and copies ran while one was open for 11% of the time, Pallas kernels for 14%

profile of v7, /device:TPU:0, one launch (start us, length us, event | category | flops | bytes accessed | tf_op | source)
XLA Modules:
  0.0 173.6 jit_solution(866873152524723981)
XLA Ops:
  0.0 3.4 %norm_kv.1.rest_0_ = bf16[512,128]{1,0:T(8,128)(2,1)} custom-call(bf16[256,2048]{1,0:T(8,128)(2,1)} %refs_0_.1, bf16[2048,128]{1,0:T(8,128)(2,1)} %refs_1_.1, bf16[2048,128]{1,0:T(8,128)(2,1)} %refs_2_.1, f32[1,2048]{1,0:T(1,128)} %bitcast.55, f32[1,128]{1,0:T(1,128)} %bitcast.72, f32[2048,128]{1,0:T(8,128)} %constant.105.clone.table_ref.refs_5_), custom_call_target="tpu_custom_call" | custom-call | tf_op jit(solution)/shard_map/norm_kv/pallas_call | solution.py:301
  3.5 3.1 %collective-permute-start.4 = (bf16[512,128]{1,0:T(8,128)(2,1)}, bf16[512,128]{1,0:T(8,128)(2,1)S(1)}, u32[]{:S(2)}, u32[]{:S(2)}) collective-permute-start(bf16[512,128]{1,0:T(8,128)(2,1)} %norm_kv.1.rest_0_), channel_id=1, source_target_pairs={{0,8},{1,9},{2,10},{3,11},{4,12},{5,13},{6,14},{7,15},{8,16},{9,17... | collective-permute-start | bytes 393224 | tf_op jit(solution)/shard_map/ppermute | solution.py:315
  6.6 1.5 collective-permute-start.6
  8.1 2.6 %collective-permute-start.2 = (bf16[512,128]{1,0:T(8,128)(2,1)}, bf16[512,128]{1,0:T(8,128)(2,1)S(1)}, u32[]{:S(2)}, u32[]{:S(2)}) collective-permute-start(bf16[512,128]{1,0:T(8,128)(2,1)} %norm_kv.1.rest_0_), channel_id=1, source_target_pairs={{0,16},{1,17},{2,18},{3,19},{4,20},{5,21},{6,22},{7,23},{8,24},{9,... | collective-permute-start | bytes 393224 | tf_op jit(solution)/shard_map/ppermute | solution.py:315
  10.7 1.3 collective-permute-start
  12.1 0.5 collective-permute-start.10
  12.7 0.1 pad_maximum_fusion.4.bias_ref
  12.8 0.1 eq.92
  13.0 2.2 %copy-done.4 = bf16[2048,1024]{1,0:T(8,128)(2,1)S(1)} copy-done((bf16[2048,1024]{1,0:T(8,128)(2,1)S(1)}, bf16[2048,1024]{1,0:T(8,128)(2,1)}, u32[]{:S(2)}) %copy-start.4) | copy-done | bytes 4194328
  15.2 1.8 %queries.1.q_ref = bf16[256,1024]{1,0:T(8,128)(2,1)S(1)} custom-call(bf16[256,2048]{1,0:T(8,128)(2,1)S(1)} %copy-done.1, f32[1,2048]{1,0:T(1,128)S(1)} %bitcast.56, bf16[2048,1024]{1,0:T(8,128)(2,1)S(1)} %copy-done.4, f32[1,128]{1,0:T(1,128)S(1)} %bitcast.57, f32[2048,128]{1,0:T(8,128)S(1)} %copy-done.5), custom_call_target="tpu_custom_call" | custom-call | tf_op jit(solution)/shard_map/queries/pallas_call | solution.py:355
  17.0 0.6 collective-permute-start.5
  17.6 0.5 collective-permute-done.2.rest_0_
  18.2 1.5 collective-permute-start.3
  19.6 0.6 collective-permute-start.1
  20.2 2.8 %attend.4 = (f32[8,8,256]{2,1,0:T(8,128)S(1)}, f32[8,128,256]{2,1,0:T(8,128)S(1)}) custom-call(f32[3]{0:T(128)S(1)} %pad_maximum_fusion.4.bias_ref, bf16[256,1024]{1,0:T(8,128)(2,1)S(1)} %queries.1.q_ref, bf16[512,128]{1,0:T(8,128)(2,1)S(1)} %copy-done.6, bf16[512,128]{1,0:T(8,128)(2,1)S(1)} %collective-permute-done.4.rest_1_, ...), custom_call_target="tpu_custom_call" | custom-call | tf_op jit(solution)/shard_map/attend/pallas_call | solution.py:161
  23.1 0.4 collective-permute-done.5.rest_1_
  23.4 2.4 %attend.5 = (f32[8,8,256]{2,1,0:T(8,128)S(1)}, f32[8,128,256]{2,1,0:T(8,128)S(1)}) custom-call(f32[2]{0:T(128)S(1)} %pad_maximum_fusion.3.bias_ref, bf16[256,1024]{1,0:T(8,128)(2,1)S(1)} %queries.1.q_ref, bf16[512,128]{1,0:T(8,128)(2,1)S(1)} %collective-permute-done.2.rest_0_, bf16[512,128]{1,0:T(8,128)(2,1)S(1)} %collective-permute-done.5.rest_1_, ...), custom_call_target="tpu_custom_call" | custom-call | tf_op jit(solution)/shard_map/attend/pallas_call | solution.py:161
  25.9 0.4 collective-permute-done.3.rest_1_
  26.2 2.4 %attend.6 = (f32[8,8,256]{2,1,0:T(8,128)S(1)}, f32[8,128,256]{2,1,0:T(8,128)S(1)}) custom-call(f32[2]{0:T(128)S(1)} %pad_maximum_fusion.2.bias_ref, bf16[256,1024]{1,0:T(8,128)(2,1)S(1)} %queries.1.q_ref, bf16[512,128]{1,0:T(8,128)(2,1)S(1)} %collective-permute-done.rest_0_, bf16[512,128]{1,0:T(8,128)(2,1)S(1)} %collective-permute-done.3.rest_1_, ...), custom_call_target="tpu_custom_call" | custom-call | tf_op jit(solution)/shard_map/attend/pallas_call | solution.py:161
  28.7 1.6 attend.7
  30.3 0.7 fusion
  31.2 0.7 fusion.2
  32.0 0.6 collective-permute-start.7
  32.5 0.2 collective-permute-done.8
  32.8 1.6 collective-permute-start.9
  34.3 0.1 fusion.18
  34.4 0.1 fusion.4
  34.6 6.6 %collective-permute-done.9 = bf16[64,2048]{1,0:T(8,128)(2,1)S(1)} collective-permute-done((bf16[64,2048]{1,0:T(8,128)(2,1)S(1)}, bf16[64,2048]{1,0:T(8,128)(2,1)S(1)}, u32[]{:S(2)}, u32[]{:S(2)}) %collective-permute-start.9) | collective-permute-done | bytes 262176 | tf_op jit(solution)/shard_map/ppermute | solution.py:408
  41.2 1.2 multiply_reduce_fusion
  42.4 0.1 multiply_convert_fusion
  42.5 0.8 copy-done.2
  43.3 3.8 %collective-permute-start.11 = (bf16[64,2048]{1,0:T(8,128)(2,1)S(1)}, bf16[64,2048]{1,0:T(8,128)(2,1)}, u32[]{:S(2)}, u32[]{:S(2)}) collective-permute-start(bf16[64,2048]{1,0:T(8,128)(2,1)S(1)} %multiply_convert_fusion), channel_id=1, source_target_pairs={{0,24},{1,25},{2,26},{3,27},{4,28},{5,29},{6,30},{7,31},{8,16},{9,... | collective-permute-start | bytes 786440 | tf_op jit(solution)/shard_map/ppermute | solution.py:452
  47.1 0.1 fusion.19
  47.2 0.7 broadcast_in_dim.84
  47.9 1.0 copy.33
  48.9 0.7 eq.89
  49.6 1.7 copy.32
  51.3 1.5 select_convert_fusion
  52.8 0.6 convert_element_type.110.pick_ref
  53.5 2.7 %fill.1 = bf16[384,2048]{1,0:T(8,128)(2,1)} custom-call(bf16[64,2048]{1,0:T(8,128)(2,1)} %collective-permute-done.11.rows_ref, bf16[64,384]{1,0:T(8,128)(2,1)} %convert_element_type.110.pick_ref, bf16[2048,768]{1,0:T(8,128)(2,1)S(1)} %bitcast.50), custom_call_target="tpu_custom_call" | custom-call | tf_op jit(solution)/shard_map/fill/pallas_call | solution.py:463
  56.2 7.7 %all-to-all-start.2 = ((bf16[16,24,2048]{2,1,0:T(8,128)(2,1)}), bf16[16,24,2048]{2,1,0:T(8,128)(2,1)}, u32[]{:S(2)}, u32[]{:S(2)}) async-start(bf16[16,24,2048]{2,1,0:T(8,128)(2,1)} %bitcast.62), calls=%async_computation.2 | async-start | bytes 3145728 | tf_op jit(solution)/shard_map/all_to_all | solution.py:420
  63.9 0.1 fusion.17
  64.0 0.7 broadcast_in_dim.77
  64.7 1.7 copy.31
  66.3 0.1 fusion.16
  66.4 0.1 fusion.5
  66.5 0.7 eq.79
  67.3 1.7 copy.30
  68.9 0.7 eq.82
  69.6 1.6 select_convert_fusion.1
  71.2 1.8 %convolution_convert_fusion = bf16[384,2048]{1,0:T(8,128)(2,1)} fusion(pred[64,384]{1,0:T(32,128)(4,1)S(1)} %get-tuple-element.22, bf16[64,2048]{1,0:T(8,128)(2,1)S(1)} %multiply_convert_fusion), kind=kOutput, calls=%fused_computation.4 | convolution fusion | flops 101449728 | bytes 1859584 | tf_op jit(solution)/shard_map/dot_general | solution.py:438
  73.0 13.7 %all-to-all-done.2 = bf16[16,24,2048]{2,1,0:T(8,128)(2,1)} async-done(((bf16[16,24,2048]{2,1,0:T(8,128)(2,1)}), bf16[16,24,2048]{2,1,0:T(8,128)(2,1)}, u32[]{:S(2)}, u32[]{:S(2)}) %all-to-all-start.2) | async-done | bytes 1572896 | tf_op jit(solution)/shard_map/all_to_all | solution.py:420
  86.7 4.4 %all-to-all-start = ((bf16[16,24,2048]{2,1,0:T(8,128)(2,1)}), bf16[16,24,2048]{2,1,0:T(8,128)(2,1)}, u32[]{:S(2)}, u32[]{:S(2)}) async-start(bf16[16,24,2048]{2,1,0:T(8,128)(2,1)} %bitcast.64), calls=%async_computation | async-start | bytes 3145728 | tf_op jit(solution)/shard_map/all_to_all | solution.py:420
  91.1 7.3 %experts.3 = bf16[384,2048]{1,0:T(8,128)(2,1)} custom-call(bf16[384,2048]{1,0:T(8,128)(2,1)} %bitcast.27.x_hbm, bf16[2048,768]{1,0:T(8,128)(2,1)S(1)} %bitcast.51, bf16[2048,768]{1,0:T(8,128)(2,1)} %bitcast.58, bf16[768,2048]{1,0:T(8,128)(2,1)} %bitcast.60), custom_call_target="tpu_custom_call" | custom-call | tf_op jit(solution)/shard_map/experts/pallas_call | solution.py:215
  98.4 15.5 %all-to-all-done = bf16[16,24,2048]{2,1,0:T(8,128)(2,1)} async-done(((bf16[16,24,2048]{2,1,0:T(8,128)(2,1)}), bf16[16,24,2048]{2,1,0:T(8,128)(2,1)}, u32[]{:S(2)}, u32[]{:S(2)}) %all-to-all-start) | async-done | bytes 1572896 | tf_op jit(solution)/shard_map/all_to_all | solution.py:420
  113.9 4.4 %all-to-all-start.3 = ((bf16[16,24,2048]{2,1,0:T(8,128)(2,1)}), bf16[16,24,2048]{2,1,0:T(8,128)(2,1)}, u32[]{:S(2)}, u32[]{:S(2)}) async-start(bf16[16,24,2048]{2,1,0:T(8,128)(2,1)} %bitcast.65), calls=%async_computation.3 | async-start | bytes 3145728 | tf_op jit(solution)/shard_map/all_to_all | solution.py:420
  118.3 7.4 %experts.2 = bf16[384,2048]{1,0:T(8,128)(2,1)} custom-call(bf16[384,2048]{1,0:T(8,128)(2,1)} %bitcast.18.x_hbm, bf16[2048,768]{1,0:T(8,128)(2,1)S(1)} %bitcast.52, bf16[2048,768]{1,0:T(8,128)(2,1)} %bitcast.59, bf16[768,2048]{1,0:T(8,128)(2,1)} %bitcast.61), custom_call_target="tpu_custom_call" | custom-call | tf_op jit(solution)/shard_map/experts/pallas_call | solution.py:215
  125.7 15.4 %all-to-all-done.3 = bf16[16,24,2048]{2,1,0:T(8,128)(2,1)} async-done(((bf16[16,24,2048]{2,1,0:T(8,128)(2,1)}), bf16[16,24,2048]{2,1,0:T(8,128)(2,1)}, u32[]{:S(2)}, u32[]{:S(2)}) %all-to-all-start.3) | async-done | bytes 1572896 | tf_op jit(solution)/shard_map/all_to_all | solution.py:420
  141.1 3.8 %all-to-all-start.1 = ((bf16[16,24,2048]{2,1,0:T(8,128)(2,1)}), bf16[16,24,2048]{2,1,0:T(8,128)(2,1)S(1)}, u32[]{:S(2)}, u32[]{:S(2)}) async-start(bf16[16,24,2048]{2,1,0:T(8,128)(2,1)} %bitcast.63), calls=%async_computation.1 | async-start | bytes 3145728 | tf_op jit(solution)/shard_map/all_to_all | solution.py:420
  145.0 1.8 %fusion.12 = f32[128,2048]{1,0:T(8,128)S(1)} fusion(bf16[384,2048]{1,0:T(8,128)(2,1)} %bitcast.29, bf16[64,384]{1,0:T(8,128)(2,1)S(1)} %subtract_convert_fusion, bf16[64,384]{1,0:T(8,128)(2,1)S(1)} %copy-done.12), kind=kOutput, calls=%fused_computation.23 | convolution fusion | flops 201523200 | bytes 2719744 | tf_op jit(solution)/shard_map/dot_general | solution.py:446
  146.9 3.7 %collective-permute-start.12 = (bf16[64,2048]{1,0:T(8,128)(2,1)S(1)}, bf16[64,2048]{1,0:T(8,128)(2,1)S(1)}, u32[]{:S(2)}, u32[]{:S(2)}) collective-permute-start(bf16[64,2048]{1,0:T(8,128)(2,1)S(1)} %fusion.6), channel_id=1, source_target_pairs={{0,24},{1,25},{2,26},{3,27},{4,28},{5,29},{6,30},{7,31},{8,16},{9,... | collective-permute-start | bytes 786440 | tf_op jit(solution)/shard_map/ppermute | solution.py:474
  150.7 17.0 %all-to-all-done.1 = bf16[16,24,2048]{2,1,0:T(8,128)(2,1)S(1)} async-done(((bf16[16,24,2048]{2,1,0:T(8,128)(2,1)}), bf16[16,24,2048]{2,1,0:T(8,128)(2,1)S(1)}, u32[]{:S(2)}, u32[]{:S(2)}) %all-to-all-start.1) | async-done | bytes 1572896 | tf_op jit(solution)/shard_map/all_to_all | solution.py:420
  167.7 4.7 %collective-permute-done.12.far_ref = bf16[64,2048]{1,0:T(8,128)(2,1)S(1)} collective-permute-done((bf16[64,2048]{1,0:T(8,128)(2,1)S(1)}, bf16[64,2048]{1,0:T(8,128)(2,1)S(1)}, u32[]{:S(2)}, u32[]{:S(2)}) %collective-permute-start.12) | collective-permute-done | bytes 262176 | tf_op jit(solution)/shard_map/ppermute | solution.py:474
  172.4 1.2 finish.1
  (59 shorter events, 0.6 us)
Async XLA Ops:
  0.0 12.9 %copy-start.5 = (f32[2048,128]{1,0:T(8,128)S(1)}, f32[2048,128]{1,0:T(8,128)}, u32[]{:S(2)}) copy-start(f32[2048,128]{1,0:T(8,128)} %constant.105.clone.table_ref.refs_5_) | copy-start | bytes 3145732
  0.0 12.9 %copy-start.7 = (f32[2048]{0:T(1024)S(1)}, f32[2048]{0:T(1024)}, u32[]{:S(2)}) copy-start(f32[2048]{0:T(1024)} %param.16) | copy-start | bytes 24580
  0.0 12.9 %copy-start.1 = (bf16[256,2048]{1,0:T(8,128)(2,1)S(1)}, bf16[256,2048]{1,0:T(8,128)(2,1)}, u32[]{:S(2)}) copy-start(bf16[256,2048]{1,0:T(8,128)(2,1)} %refs_0_.1) | copy-start | bytes 3145732
  0.0 12.0 %copy-start.14 = (f32[64,8]{0,1:T(8,128)S(1)}, f32[64,8]{0,1:T(8,128)}, u32[]{:S(2)}) copy-start(f32[64,8]{0,1:T(8,128)} %param.25) | copy-start | bytes 6148
  0.0 12.0 %copy-start.13 = (s32[64,8]{0,1:T(8,128)S(1)}, s32[64,8]{0,1:T(8,128)}, u32[]{:S(2)}) copy-start(s32[64,8]{0,1:T(8,128)} %param.24) | copy-start | bytes 6148
  0.0 12.9 %copy-start.8 = (f32[128]{0:T(128)S(1)}, f32[128]{0:T(128)}, u32[]{:S(2)}) copy-start(f32[128]{0:T(128)} %param.20) | copy-start | bytes 1540
  3.5 13.5 %collective-permute-start.4 = (bf16[512,128]{1,0:T(8,128)(2,1)}, bf16[512,128]{1,0:T(8,128)(2,1)S(1)}, u32[]{:S(2)}, u32[]{:S(2)}) collective-permute-start(bf16[512,128]{1,0:T(8,128)(2,1)} %norm_kv.1.rest_0_), channel_id=1, source_target_pairs={{0,8},{1,9},{2,10},{3,11},{4,12},{5,13},{6,14},{7,15},{8,16},{9,17... | collective-permute-start | bytes 393224 | tf_op jit(solution)/shard_map/ppermute | solution.py:315
  6.6 13.6 %collective-permute-start.6 = (bf16[512,128]{1,0:T(8,128)(2,1)}, bf16[512,128]{1,0:T(8,128)(2,1)S(1)}, u32[]{:S(2)}, u32[]{:S(2)}) collective-permute-start(bf16[512,128]{1,0:T(8,128)(2,1)} %norm_kv.1.rest_0_), channel_id=1, source_target_pairs={{0,4},{1,5},{2,6},{3,7},{4,0},{5,1},{6,2},{7,3},{8,12},{9,13},{10,... | collective-permute-start | bytes 393224 | tf_op jit(solution)/shard_map/ppermute | solution.py:320
  8.1 10.1 %collective-permute-start.2 = (bf16[512,128]{1,0:T(8,128)(2,1)}, bf16[512,128]{1,0:T(8,128)(2,1)S(1)}, u32[]{:S(2)}, u32[]{:S(2)}) collective-permute-start(bf16[512,128]{1,0:T(8,128)(2,1)} %norm_kv.1.rest_0_), channel_id=1, source_target_pairs={{0,16},{1,17},{2,18},{3,19},{4,20},{5,21},{6,22},{7,23},{8,24},{9,... | collective-permute-start | bytes 393224 | tf_op jit(solution)/shard_map/ppermute | solution.py:315
  10.7 9.0 %collective-permute-start = (bf16[512,128]{1,0:T(8,128)(2,1)}, bf16[512,128]{1,0:T(8,128)(2,1)S(1)}, u32[]{:S(2)}, u32[]{:S(2)}) collective-permute-start(bf16[512,128]{1,0:T(8,128)(2,1)} %norm_kv.1.rest_0_), channel_id=1, source_target_pairs={{0,24},{1,25},{2,26},{3,27},{4,28},{5,29},{6,30},{7,31},{8,0},{9,1... | collective-permute-start | bytes 393224 | tf_op jit(solution)/shard_map/ppermute | solution.py:315
  12.1 8.1 %collective-permute-start.10 = (f32[64,16]{0,1:T(8,128)S(1)}, f32[64,16]{0,1:T(8,128)S(1)}, u32[]{:S(2)}, u32[]{:S(2)}) collective-permute-start(f32[64,16]{0,1:T(8,128)S(1)} %pad_maximum_fusion.1), channel_id=1, source_target_pairs={{0,24},{1,25},{2,26},{3,27},{4,28},{5,29},{6,30},{7,31},{8,16},{9,... | collective-permute-start | bytes 12296 | tf_op jit(solution)/shard_map/ppermute | solution.py:455
  13.0 2.2 %copy-start.4 = (bf16[2048,1024]{1,0:T(8,128)(2,1)S(1)}, bf16[2048,1024]{1,0:T(8,128)(2,1)}, u32[]{:S(2)}) copy-start(bf16[2048,1024]{1,0:T(8,128)(2,1)} %wq_ref.1) | copy-start | bytes 12582916
  15.2 5.1 %copy-start.6 = (bf16[512,128]{1,0:T(8,128)(2,1)S(1)}, bf16[512,128]{1,0:T(8,128)(2,1)}, u32[]{:S(2)}) copy-start(bf16[512,128]{1,0:T(8,128)(2,1)} %norm_kv.1.rest_0_) | copy-start | bytes 393220
  17.0 6.4 %collective-permute-start.5 = (bf16[512,128]{1,0:T(8,128)(2,1)S(1)}, bf16[512,128]{1,0:T(8,128)(2,1)S(1)}, u32[]{:S(2)}, u32[]{:S(2)}) collective-permute-start(bf16[512,128]{1,0:T(8,128)(2,1)S(1)} %collective-permute-done.4.rest_1_), channel_id=1, source_target_pairs={{0,4},{1,5},{2,6},{3,7},{4,0},{5,1},{6,2},{7,3},{8,12},{9,13},{10,... | collective-permute-start | bytes 393224 | tf_op jit(solution)/shard_map/ppermute | solution.py:320
  18.2 8.1 %collective-permute-start.3 = (bf16[512,128]{1,0:T(8,128)(2,1)S(1)}, bf16[512,128]{1,0:T(8,128)(2,1)S(1)}, u32[]{:S(2)}, u32[]{:S(2)}) collective-permute-start(bf16[512,128]{1,0:T(8,128)(2,1)S(1)} %collective-permute-done.2.rest_0_), channel_id=1, source_target_pairs={{0,4},{1,5},{2,6},{3,7},{4,0},{5,1},{6,2},{7,3},{8,12},{9,13},{10,... | collective-permute-start | bytes 393224 | tf_op jit(solution)/shard_map/ppermute | solution.py:320
  19.6 9.1 %collective-permute-start.1 = (bf16[512,128]{1,0:T(8,128)(2,1)S(1)}, bf16[512,128]{1,0:T(8,128)(2,1)S(1)}, u32[]{:S(2)}, u32[]{:S(2)}) collective-permute-start(bf16[512,128]{1,0:T(8,128)(2,1)S(1)} %collective-permute-done.rest_0_), channel_id=1, source_target_pairs={{0,4},{1,5},{2,6},{3,7},{4,0},{5,1},{6,2},{7,3},{8,12},{9,13},{10,... | collective-permute-start | bytes 393224 | tf_op jit(solution)/shard_map/ppermute | solution.py:320
  23.4 6.9 %copy-start.9 = (bf16[1024,2048]{1,0:T(8,128)(2,1)S(1)}, bf16[1024,2048]{1,0:T(8,128)(2,1)}, u32[]{:S(2)}) copy-start(bf16[1024,2048]{1,0:T(8,128)(2,1)} %param.22) | copy-start | bytes 12582916
  31.1 1.6 collective-permute-start.8
  31.9 10.5 %copy-start.15 = (f32[2048]{0:T(1024)S(1)}, f32[2048]{0:T(1024)}, u32[]{:S(2)}) copy-start(f32[2048]{0:T(1024)} %param.23) | copy-start | bytes 24580
  31.9 21.5 %copy-start = (bf16[1,2048,768]{2,1,0:T(8,128)(2,1)S(1)}, bf16[1,2048,768]{2,1,0:T(8,128)(2,1)}, u32[]{:S(2)}) copy-start(bf16[1,2048,768]{2,1,0:T(8,128)(2,1)} %param.26) | copy-start | bytes 9437188
  32.0 2.6 %collective-permute-start.7 = (bf16[64,2048]{1,0:T(8,128)(2,1)S(1)}, bf16[64,2048]{1,0:T(8,128)(2,1)S(1)}, u32[]{:S(2)}, u32[]{:S(2)}) collective-permute-start(bf16[64,2048]{1,0:T(8,128)(2,1)S(1)} %fusion.10), channel_id=1, source_target_pairs={{0,1},{1,0},{2,3},{3,2},{4,5},{5,4},{6,7},{7,6},{8,9},{9,8},{10,11... | collective-permute-start | bytes 786440 | tf_op jit(solution)/shard_map/ppermute | solution.py:401
  32.8 8.4 %collective-permute-start.9 = (bf16[64,2048]{1,0:T(8,128)(2,1)S(1)}, bf16[64,2048]{1,0:T(8,128)(2,1)S(1)}, u32[]{:S(2)}, u32[]{:S(2)}) collective-permute-start(bf16[64,2048]{1,0:T(8,128)(2,1)S(1)} %fusion.7), channel_id=1, source_target_pairs={{0,2},{1,3},{2,0},{3,1},{4,6},{5,7},{6,4},{7,5},{8,10},{9,11},{10,... | collective-permute-start | bytes 786440 | tf_op jit(solution)/shard_map/ppermute | solution.py:408
  42.5 0.8 copy-start.2
  43.3 10.1 %collective-permute-start.11 = (bf16[64,2048]{1,0:T(8,128)(2,1)S(1)}, bf16[64,2048]{1,0:T(8,128)(2,1)}, u32[]{:S(2)}, u32[]{:S(2)}) collective-permute-start(bf16[64,2048]{1,0:T(8,128)(2,1)S(1)} %multiply_convert_fusion), channel_id=1, source_target_pairs={{0,24},{1,25},{2,26},{3,27},{4,28},{5,29},{6,30},{7,31},{8,16},{9,... | collective-permute-start | bytes 786440 | tf_op jit(solution)/shard_map/ppermute | solution.py:452
  56.2 30.5 %all-to-all-start.2 = ((bf16[16,24,2048]{2,1,0:T(8,128)(2,1)}), bf16[16,24,2048]{2,1,0:T(8,128)(2,1)}, u32[]{:S(2)}, u32[]{:S(2)}) async-start(bf16[16,24,2048]{2,1,0:T(8,128)(2,1)} %bitcast.62), calls=%async_computation.2 | async-start | bytes 3145728 | tf_op jit(solution)/shard_map/all_to_all | solution.py:420
  86.7 27.2 %all-to-all-start = ((bf16[16,24,2048]{2,1,0:T(8,128)(2,1)}), bf16[16,24,2048]{2,1,0:T(8,128)(2,1)}, u32[]{:S(2)}, u32[]{:S(2)}) async-start(bf16[16,24,2048]{2,1,0:T(8,128)(2,1)} %bitcast.64), calls=%async_computation | async-start | bytes 3145728 | tf_op jit(solution)/shard_map/all_to_all | solution.py:420
  113.9 27.2 %all-to-all-start.3 = ((bf16[16,24,2048]{2,1,0:T(8,128)(2,1)}), bf16[16,24,2048]{2,1,0:T(8,128)(2,1)}, u32[]{:S(2)}, u32[]{:S(2)}) async-start(bf16[16,24,2048]{2,1,0:T(8,128)(2,1)} %bitcast.65), calls=%async_computation.3 | async-start | bytes 3145728 | tf_op jit(solution)/shard_map/all_to_all | solution.py:420
  125.7 19.3 %copy-start.12 = (bf16[64,384]{1,0:T(8,128)(2,1)S(1)}, bf16[64,384]{1,0:T(8,128)(2,1)}, u32[]{:S(2)}) copy-start(bf16[64,384]{1,0:T(8,128)(2,1)} %get-tuple-element.17) | copy-start | bytes 147460
  141.1 9.5 %copy-start.10 = (f32[64,384]{1,0:T(8,128)S(1)}, f32[64,384]{1,0:T(8,128)}, u32[]{:S(2)}) copy-start(f32[64,384]{1,0:T(8,128)} %copy.31) | copy-start | bytes 294916
  141.1 9.5 %copy-start.11 = (bf16[64,384]{1,0:T(8,128)(2,1)S(1)}, bf16[64,384]{1,0:T(8,128)(2,1)}, u32[]{:S(2)}) copy-start(bf16[64,384]{1,0:T(8,128)(2,1)} %get-tuple-element.21) | copy-start | bytes 147460
  141.1 31.3 %copy-start.3 = (f32[64,2048]{1,0:T(8,128)S(1)}, f32[64,2048]{1,0:T(8,128)}, u32[]{:S(2)}) copy-start(f32[64,2048]{1,0:T(8,128)} %copy-done.2) | copy-start | bytes 1572868
  141.1 26.6 %all-to-all-start.1 = ((bf16[16,24,2048]{2,1,0:T(8,128)(2,1)}), bf16[16,24,2048]{2,1,0:T(8,128)(2,1)S(1)}, u32[]{:S(2)}, u32[]{:S(2)}) async-start(bf16[16,24,2048]{2,1,0:T(8,128)(2,1)} %bitcast.63), calls=%async_computation.1 | async-start | bytes 3145728 | tf_op jit(solution)/shard_map/all_to_all | solution.py:420
  146.9 25.5 %collective-permute-start.12 = (bf16[64,2048]{1,0:T(8,128)(2,1)S(1)}, bf16[64,2048]{1,0:T(8,128)(2,1)S(1)}, u32[]{:S(2)}, u32[]{:S(2)}) collective-permute-start(bf16[64,2048]{1,0:T(8,128)(2,1)S(1)} %fusion.6), channel_id=1, source_target_pairs={{0,24},{1,25},{2,26},{3,27},{4,28},{5,29},{6,30},{7,31},{8,16},{9,... | collective-permute-start | bytes 786440 | tf_op jit(solution)/shard_map/ppermute | solution.py:474
